TPU v7x, 32 devices: a whole 2x2x4 slice. The times are simulated.
32 devices in a mesh: gx: 4 (over y, x), gy: 8 (over z, core).
Axes of the slice: x: 2, y: 2, z: 4, core: 2. Of those that a mesh axis runs over, the one named last changes fastest.
Arguments:
- grid_latent: bfloat16 [16384, 512], P(('gx', 'gy')), may hold values from -6 to 6
- mesh_latent: bfloat16 [4096, 512], P(('gx', 'gy')), may hold values from -6 to 6
- encode_senders: int32 [32, 4096], P(None, ('gx', 'gy')), may hold values from -1 to 16383, as said below
- mesh_senders: int32 [32, 4096], P(None, ('gx', 'gy')), may hold values from -1 to 4095, as said below
- decode_senders: int32 [3, 16384], P(None, ('gx', 'gy')), may hold values from 0 to 4095, as said below
- encoder_edges: bfloat16 [3, 512, 512], replicated, may hold values from -0.25 to 0.25
- encoder_edgebias: float32 [2, 512], replicated, may hold values from -3 to 3
- encoder_nodes: bfloat16 [3, 512, 512], replicated, may hold values from -0.25 to 0.25
- encoder_nodebias: float32 [2, 512], replicated, may hold values from -3 to 3
- process_edges: bfloat16 [3, 512, 512], replicated, may hold values from -0.25 to 0.25
- process_edgebias: float32 [2, 512], replicated, may hold values from -3 to 3
- process_nodes: bfloat16 [3, 512, 512], replicated, may hold values from -0.25 to 0.25
- process_nodebias: float32 [2, 512], replicated, may hold values from -3 to 3
- decoder_edges: bfloat16 [3, 512, 512], replicated, may hold values from -0.25 to 0.25
- decoder_edgebias: float32 [2, 512], replicated, may hold values from -3 to 3
- decoder_nodes: bfloat16 [3, 512, 512], replicated, may hold values from -0.25 to 0.25
- decoder_nodebias: float32 [2, 512], replicated, may hold values from -3 to 3
Outputs:
- decoded_grid: bfloat16 [16384, 512], P(('gx', 'gy'))
- processed_mesh: bfloat16 [4096, 512], P(('gx', 'gy'))
Inputs may be any that keep to these rules, and one draw needn't show every extreme that they name: `encode_senders`: devices form a torus of regions, device number = gx index * gy size + gy index, and device d owns grid points d * 512 to (d + 1) * 512 - 1. In each column the live senders come first, then -1; a column has 8 to 32 live senders and some column has 32. A live sender is a grid point of the column's own device, or one of the first 128 grid points of one of the eight devices around it on the torus (wrapping on both axes). `mesh_senders`: device d owns mesh nodes d * 128 to (d + 1) * 128 - 1. In each column the live senders come first, then -1; a column has 8 to 32 live senders and some column has 32. A live sender is a mesh node of the column's own device, or one of the first 32 mesh nodes of one of the eight devices around it on the torus, or one of the first 4 mesh nodes of any device. `decode_senders`: every entry is live: a mesh node of the grid point's own device, or one of the first 32 mesh nodes of one of the eight devices around it on the torus.
All inputs are finite; a program needn't handle non-finite values.
Results may differ from a plain program's by a relative error of at most 0.013.
Values may be sent and summed in bfloat16 or wider, within the bound.
No kernel may reach another device: no remote copies, remote signals or barrier semaphores. Data moves between devices by JAX's collectives and lax.ppermute only.
A program may use at most 64 MiB of HBM per device.

v0:
```python
import jax
import jax.numpy as jnp
from jax import lax
from jax.sharding import PartitionSpec as P

CM = 4


def with_halo(shard, sides, width):
    for axis, dim in sides:
        peers, length = (lax.axis_size(axis), shard.shape[dim])
        up = [(i, (i + 1) % peers) for i in range(peers)]
        down = [(j, i) for i, j in up]
        last = lax.slice_in_dim(shard, length - width, length, axis=dim)
        initial = lax.slice_in_dim(shard, 0, width, axis=dim)
        before = lax.ppermute(last, axis, up)
        after = lax.ppermute(initial, axis, down)
        shard = jnp.concatenate([before, shard, after], axis=dim)
    return shard


def project(latent, weight):
    return jnp.dot(latent, weight, preferred_element_type=jnp.float32)


def finish(preact, weights, vectors):
    hidden = jax.nn.silu(preact).astype(jnp.bfloat16)
    output = jnp.dot(hidden, weights[2], preferred_element_type=jnp.float32)
    centre = jnp.mean(output, axis=-1, keepdims=True)
    centred = output - centre
    spread = jnp.mean(centred * centred, axis=-1, keepdims=True)
    return centred * lax.rsqrt(spread + 1e-05) * (1.0 + vectors[1])


def block_size(count, degree):
    target = max(1, 4096 // degree)
    chosen = min(count, target)
    while count % chosen:
        chosen -= 1
    return chosen


def aggregate(sources, receiving, positions, active, weights, vectors):
    degree, count = positions.shape
    chosen = block_size(count, degree)
    blocks = count // chosen
    source_rows, width = sources.shape
    shifted = (receiving + vectors[0]).reshape(blocks, chosen, width)
    places = positions.reshape(degree, blocks, chosen).transpose(1, 0, 2)
    masks = active.reshape(degree, blocks, chosen).transpose(1, 0, 2)
    columns = lax.broadcasted_iota(jnp.int32, (1, source_rows), 1)

    def one_block(item):
        base, place, present = item
        selector = (place.reshape(degree * chosen, 1) == columns).astype(jnp.bfloat16)
        picked = jnp.dot(selector, sources, preferred_element_type=jnp.float32).astype(jnp.bfloat16)
        preact = project(picked, weights[0]).reshape(degree, chosen, width) + base[None]
        message = finish(preact.reshape(degree * chosen, width), weights, vectors)
        message = message.reshape(degree, chosen, width)
        return jnp.sum(jnp.where(present[..., None], message, 0.0), axis=0)

    return lax.map(one_block, (shifted, places, masks)).reshape(count, width)


def update(latent, summed, weights, vectors):
    preact = (
        project(latent, weights[0]) + project(summed.astype(jnp.bfloat16), weights[1]) + vectors[0]
    )
    return (latent.astype(jnp.float32) + finish(preact, weights, vectors)).astype(jnp.bfloat16)


def locate(sender_ids, rows, border, coarse, place_x, place_y, size_x, size_y):
    cleaned = jnp.maximum(sender_ids, 0)
    owner = cleaned // rows
    offset = cleaned % rows
    owner_x = owner // size_y
    owner_y = owner % size_y
    step_x = (owner_x - place_x) % size_x
    step_y = (owner_y - place_y) % size_y
    slot_x = jnp.where(step_x == 1, 2, jnp.where(step_x == size_x - 1, 0, 1))
    slot_y = jnp.where(step_y == 1, 2, jnp.where(step_y == size_y - 1, 0, 1))
    nearby = (
        ((step_x <= 1) | (step_x == size_x - 1))
        & ((step_y <= 1) | (step_y == size_y - 1))
        & (offset < border)
    )
    itself = (step_x == 0) & (step_y == 0)
    rim_place = rows + (slot_x * 3 + slot_y) * border + offset
    far_place = rows + 9 * border + owner * coarse + offset
    return jnp.where(itself, offset, jnp.where(nearby, rim_place, far_place))


def per_device(
    grid_latent,
    mesh_latent,
    encode_senders,
    mesh_senders,
    decode_senders,
    encoder_edges,
    encoder_edgebias,
    encoder_nodes,
    encoder_nodebias,
    process_edges,
    process_edgebias,
    process_nodes,
    process_nodebias,
    decoder_edges,
    decoder_edgebias,
    decoder_nodes,
    decoder_nodebias,
):
    grid_rows, width = grid_latent.shape
    mesh_rows = mesh_latent.shape[0]
    grid_border = grid_rows // 4
    mesh_border = mesh_rows // 4
    size_x = lax.axis_size("gx")
    size_y = lax.axis_size("gy")
    place_x = lax.axis_index("gx")
    place_y = lax.axis_index("gy")
    border_rows = grid_latent[:grid_border].reshape(1, 1, grid_border, width)
    rim_rows = with_halo(border_rows, (("gx", 0), ("gy", 1)), 1)
    grid_sources = jnp.concatenate([grid_latent, rim_rows.reshape(9 * grid_border, width)], axis=0)
    positions = locate(encode_senders, grid_rows, grid_border, 0, place_x, place_y, size_x, size_y)
    summed = aggregate(
        grid_sources,
        project(mesh_latent, encoder_edges[1]),
        positions,
        encode_senders >= 0,
        encoder_edges,
        encoder_edgebias,
    )
    encoded = update(mesh_latent, summed, encoder_nodes, encoder_nodebias)
    mesh_rim = with_halo(
        encoded[:mesh_border].reshape(1, 1, mesh_border, width), (("gx", 0), ("gy", 1)), 1
    )
    coarse_rows = lax.all_gather(encoded[:CM], ("gx", "gy"), axis=0, tiled=True)
    mesh_sources = jnp.concatenate(
        [encoded, mesh_rim.reshape(9 * mesh_border, width), coarse_rows], axis=0
    )
    positions = locate(mesh_senders, mesh_rows, mesh_border, CM, place_x, place_y, size_x, size_y)
    summed = aggregate(
        mesh_sources,
        project(encoded, process_edges[1]),
        positions,
        mesh_senders >= 0,
        process_edges,
        process_edgebias,
    )
    processed = update(encoded, summed, process_nodes, process_nodebias)
    final_rim = with_halo(
        processed[:mesh_border].reshape(1, 1, mesh_border, width), (("gx", 0), ("gy", 1)), 1
    )
    decode_sources = jnp.concatenate([processed, final_rim.reshape(9 * mesh_border, width)], axis=0)
    positions = locate(decode_senders, mesh_rows, mesh_border, 0, place_x, place_y, size_x, size_y)
    summed = aggregate(
        decode_sources,
        project(grid_latent, decoder_edges[1]),
        positions,
        decode_senders >= 0,
        decoder_edges,
        decoder_edgebias,
    )
    decoded = update(grid_latent, summed, decoder_nodes, decoder_nodebias)
    return (decoded, processed)


def solution(mesh):
    return jax.shard_map(
        per_device,
        mesh=mesh,
        in_specs=(
            P(("gx", "gy"), None),
            P(("gx", "gy"), None),
            P(None, ("gx", "gy")),
            P(None, ("gx", "gy")),
            P(None, ("gx", "gy")),
            P(),
            P(),
            P(),
            P(),
            P(),
            P(),
            P(),
            P(),
            P(),
            P(),
            P(),
            P(),
        ),
        out_specs=(P(("gx", "gy"), None), P(("gx", "gy"), None)),
        check_vma=False,
    )
```

profile of v0, /device:TPU:0, one launch (start us, length us, event | category | flops | bytes accessed | tf_op | source)
XLA Modules:
  0.0 136.2 jit_solution(2139973905397093933)
XLA Ops:
  1.6 3.0 %collective-permute-start = (bf16[1,1,128,512]{3,2,1,0:T(8,128)(2,1)S(1)}, bf16[1,1,128,512]{3,2,1,0:T(8,128)(2,1)S(1)}, u32[]{:S(2)}, u32[]{:S(2)}) collective-permute-start(bf16[1,1,128,512]{3,2,1,0:T(8,128)(2,1)S(1)} %slice_bitcast_fusion), channel_id=1, source_target_pairs={{0,8},{8,16},{16,24},{24,0},{1,9},{9,17},{17,25},{25,1},{2,10},{10... | collective-permute-start | bytes 393224 | tf_op jit(solution)/shard_map/ppermute | solution.py:16
  11.8 2.6 %fusion.46 = f32[512,512]{1,0:T(8,128)} fusion(bf16[512,512]{1,0:T(8,128)(2,1)} %param.17, bf16[3,512,512]{2,1,0:T(8,128)(2,1)} %param.32), kind=kOutput, calls=%fused_computation.70 | convolution fusion | flops 268435456 | bytes 2097152 | tf_op jit(solution)/shard_map/dot_general | solution.py:23
  14.4 1.3 fusion.44
  15.8 1.3 convolution_add_fusion.5
  17.2 3.5 %collective-permute-start.3 = (bf16[3,1,128,512]{3,2,1,0:T(8,128)(2,1)S(1)}, bf16[3,1,128,512]{3,2,1,0:T(8,128)(2,1)S(1)}, u32[]{:S(2)}, u32[]{:S(2)}) collective-permute-start(bf16[3,1,128,512]{3,2,1,0:T(8,128)(2,1)S(1)} %pad_maximum_fusion.1), channel_id=1, source_target_pairs={{1,0},{2,1},{3,2},{4,3},{5,4},{6,5},{7,6},{0,7},{9,8},{10,9},{11,1... | collective-permute-start | bytes 1179656 | tf_op jit(solution)/shard_map/ppermute | solution.py:17
  20.8 1.5 %convolution_add_fusion.1 = f32[512,512]{1,0:T(8,128)S(1)} fusion(bf16[512,512]{1,0:T(8,128)(2,1)S(1)} %copy-done, f32[512]{0:T(512)S(1)} %bitcast.152, bf16[3,512,512]{2,1,0:T(8,128)(2,1)} %param.30), kind=kOutput, calls=%fused_computation.29 | convolution fusion | flops 268697600 | bytes 2099200 | tf_op jit(solution)/shard_map/dot_general | solution.py:23
  22.2 5.6 %collective-permute-done.2 = bf16[3,1,128,512]{3,2,1,0:T(8,128)(2,1)S(1)} collective-permute-done((bf16[3,1,128,512]{3,2,1,0:T(8,128)(2,1)S(1)}, bf16[3,1,128,512]{3,2,1,0:T(8,128)(2,1)S(1)}, u32[]{:S(2)}, u32[]{:S(2)}) %collective-permute-start.2) | collective-permute-done | bytes 393248 | tf_op jit(solution)/shard_map/ppermute | solution.py:16
  28.3 8.2 %fusion.4 = bf16[4096,512]{1,0:T(8,128)(2,1)S(1)} fusion(s32[4096]{0:T(1024)S(1)} %select_bitcast_fusion.1, bf16[1152,512]{1,0:T(8,128)(2,1)S(1)} %bitcast.141, bf16[512,512]{1,0:T(8,128)(2,1)S(1)} %copy-done), kind=kOutput, calls=%fused_computation.14 | convolution fusion | flops 6991642624 | bytes 5914624 | tf_op jit(solution)/shard_map/while/body/eval_jaxpr/dot_general | solution.py:56
  36.6 3.9 %multiply_convert_fusion.1 = bf16[32,128,512]{2,1,0:T(8,128)(2,1)S(1)} fusion(f32[128,512]{1,0:T(8,128)S(1)} %convolution_add_fusion.5, bf16[32,128,512]{2,1,0:T(8,128)(2,1)S(1)} %bitcast.157, bf16[3,512,512]{2,1,0:T(8,128)(2,1)S(1)} %copy-done.3), kind=kOutput, calls=%fused_computation.12 | convolution fusion | flops 2160066560 | bytes 9175040 | tf_op jit(solution)/shard_map/while/body/eval_jaxpr/dot_general | solution.py:23
  40.4 2.4 %fusion.115 = (f32[4096]{0:T(1024)S(1)}, f32[4096,512]{1,0:T(8,128)S(1)}) fusion(bf16[4096,512]{1,0:T(8,128)(2,1)S(1)} %bitcast.138, bf16[3,512,512]{2,1,0:T(8,128)(2,1)S(1)} %copy-done.3), kind=kOutput, calls=%fused_computation.211 | convolution fusion | flops 2149576704 | bytes 13123584 | tf_op jit(solution)/shard_map/while/body/eval_jaxpr/dot_general | solution.py:28
  42.9 1.4 %multiply_reduce_fusion.1 = f32[4096]{0:T(1024)S(1)} fusion(f32[4096,512]{1,0:T(8,128)S(1)} %get-tuple-element.93, f32[4096]{0:T(1024)S(1)} %broadcast_multiply_fusion.1), kind=kLoop, calls=%fused_computation.11 | loop fusion | flops 6287360 | bytes 8421376 | tf_op jit(solution)/shard_map/while/body/eval_jaxpr/reduce_sum | solution.py:31
  44.3 1.5 %multiply_multiply_fusion.1 = f32[4096,512]{1,0:T(8,128)S(1)} fusion(f32[4096,512]{1,0:T(8,128)S(1)} %get-tuple-element.93, f32[512]{0:T(512)S(1)} %bitcast.149, f32[4096]{0:T(1024)S(1)} %add_rsqrt_fusion.1, f32[4096]{0:T(1024)S(1)} %broadcast_multiply_fusion.1), kind=kLoop, calls=%fused_computation.10 | loop fusion | flops 6291456 | bytes 16812032 | tf_op jit(solution)/shard_map/while/body/eval_jaxpr/mul | solution.py:32
  46.7 1.7 %fusion.116 = (f32[128]{0:T(128)S(1)}, f32[128,512]{1,0:T(8,128)S(1)}) fusion(bf16[3,512,512]{2,1,0:T(8,128)(2,1)} %param.24, f32[128,512]{1,0:T(8,128)S(1)} %fusion.44, f32[512]{0:T(512)S(1)} %bitcast.154, bf16[128,512]{1,0:T(8,128)(2,1)S(1)} %select_reduce_fusion.1), kind=kOutput, calls=%fused_computation.212 | convolution fusion | flops 134741888 | bytes 1706496 | tf_op jit(solution)/shard_map/dot_general | solution.py:28
  48.8 1.2 collective-permute-start.4
  50.0 1.8 %collective-permute-start.5 = (bf16[1,1,32,512]{3,2,1,0:T(8,128)(2,1)S(1)}, bf16[1,1,32,512]{3,2,1,0:T(8,128)(2,1)S(1)}, u32[]{:S(2)}, u32[]{:S(2)}) collective-permute-start(bf16[1,1,32,512]{3,2,1,0:T(8,128)(2,1)S(1)} %slice_bitcast_fusion.2), channel_id=1, source_target_pairs={{8,0},{16,8},{24,16},{0,24},{9,1},{17,9},{25,17},{1,25},{10,2},{18... | collective-permute-start | bytes 98312 | tf_op jit(solution)/shard_map/ppermute | solution.py:17
  51.7 1.3 convolution_add_fusion.3
  53.0 1.3 fusion.35
  54.6 1.5 %collective-permute-start.6 = (bf16[3,1,32,512]{3,2,1,0:T(8,128)(2,1)S(1)}, bf16[3,1,32,512]{3,2,1,0:T(8,128)(2,1)S(1)}, u32[]{:S(2)}, u32[]{:S(2)}) collective-permute-start(bf16[3,1,32,512]{3,2,1,0:T(8,128)(2,1)S(1)} %pad_maximum_fusion.4), channel_id=1, source_target_pairs={{0,1},{1,2},{2,3},{3,4},{4,5},{5,6},{6,7},{7,0},{8,9},{9,10},{10,1... | collective-permute-start | bytes 294920 | tf_op jit(solution)/shard_map/ppermute | solution.py:16
  56.1 2.3 %collective-permute-start.7 = (bf16[3,1,32,512]{3,2,1,0:T(8,128)(2,1)S(1)}, bf16[3,1,32,512]{3,2,1,0:T(8,128)(2,1)S(1)}, u32[]{:S(2)}, u32[]{:S(2)}) collective-permute-start(bf16[3,1,32,512]{3,2,1,0:T(8,128)(2,1)S(1)} %pad_maximum_fusion.4), channel_id=1, source_target_pairs={{1,0},{2,1},{3,2},{4,3},{5,4},{6,5},{7,6},{0,7},{9,8},{10,9},{11,1... | collective-permute-start | bytes 294920 | tf_op jit(solution)/shard_map/ppermute | solution.py:17
  58.4 40.8 %all-gather = bf16[32,4,512]{2,1,0:T(4,128)(2,1)S(1)} all-gather(bf16[1,4,512]{2,1,0:T(4,128)(2,1)S(1)} %slice_bitcast_fusion.3), channel_id=1, replica_groups=mesh['gx'=4,'gy'=8] {'gx','gy'}, dimensions={0}, use_global_device_ids=true | all-gather | bytes 135168 | tf_op jit(solution)/shard_map/all_gather | solution.py:136
  99.4 3.7 %fusion.3 = bf16[4096,512]{1,0:T(8,128)(2,1)S(1)} fusion(s32[4096]{0:T(1024)S(1)} %select_bitcast_fusion, bf16[128,512]{1,0:T(8,128)(2,1)S(1)} %reshape.182, bf16[288,512]{1,0:T(8,128)(2,1)S(1)} %bitcast.142, bf16[128,512]{1,0:T(8,128)(2,1)S(1)} %add_convert_fusion.2), kind=kOutput, calls=%fused_computation.13 | convolution fusion | flops 2287697920 | bytes 4767744 | tf_op jit(solution)/shard_map/while/body/eval_jaxpr/dot_general | solution.py:56
  103.1 3.8 %multiply_convert_fusion = bf16[32,128,512]{2,1,0:T(8,128)(2,1)S(1)} fusion(f32[128,512]{1,0:T(8,128)S(1)} %convolution_add_fusion.3, bf16[32,128,512]{2,1,0:T(8,128)(2,1)S(1)} %bitcast.156, bf16[3,512,512]{2,1,0:T(8,128)(2,1)S(1)} %copy-done.4), kind=kOutput, calls=%fused_computation.8 | convolution fusion | flops 2160066560 | bytes 9175040 | tf_op jit(solution)/shard_map/while/body/eval_jaxpr/dot_general | solution.py:23
  106.9 2.4 %fusion.119 = (f32[4096]{0:T(1024)S(1)}, f32[4096,512]{1,0:T(8,128)S(1)}) fusion(bf16[4096,512]{1,0:T(8,128)(2,1)S(1)} %bitcast.139, bf16[3,512,512]{2,1,0:T(8,128)(2,1)S(1)} %copy-done.4), kind=kOutput, calls=%fused_computation.213 | convolution fusion | flops 2149576704 | bytes 13123584 | tf_op jit(solution)/shard_map/while/body/eval_jaxpr/dot_general | solution.py:28
  109.3 1.4 %multiply_reduce_fusion = f32[4096]{0:T(1024)S(1)} fusion(f32[4096,512]{1,0:T(8,128)S(1)} %get-tuple-element.97, f32[4096]{0:T(1024)S(1)} %broadcast_multiply_fusion), kind=kLoop, calls=%fused_computation.7 | loop fusion | flops 6287360 | bytes 8421376 | tf_op jit(solution)/shard_map/while/body/eval_jaxpr/reduce_sum | solution.py:31
  110.8 1.5 %multiply_multiply_fusion = f32[4096,512]{1,0:T(8,128)S(1)} fusion(f32[4096,512]{1,0:T(8,128)S(1)} %get-tuple-element.97, f32[512]{0:T(512)S(1)} %bitcast.146, f32[4096]{0:T(1024)S(1)} %add_rsqrt_fusion, f32[4096]{0:T(1024)S(1)} %broadcast_multiply_fusion), kind=kLoop, calls=%fused_computation.6 | loop fusion | flops 6291456 | bytes 16812032 | tf_op jit(solution)/shard_map/while/body/eval_jaxpr/mul | solution.py:32
  113.2 1.7 %fusion.120 = (f32[128]{0:T(128)S(1)}, f32[128,512]{1,0:T(8,128)S(1)}) fusion(bf16[3,512,512]{2,1,0:T(8,128)(2,1)} %param.28, f32[128,512]{1,0:T(8,128)S(1)} %fusion.35, f32[512]{0:T(512)S(1)} %bitcast.153, bf16[128,512]{1,0:T(8,128)(2,1)S(1)} %select_reduce_fusion), kind=kOutput, calls=%fused_computation.214 | convolution fusion | flops 134741888 | bytes 1706496 | tf_op jit(solution)/shard_map/dot_general | solution.py:28
  115.4 2.9 %collective-permute-start.9 = (bf16[1,1,32,512]{3,2,1,0:T(8,128)(2,1)S(1)}, bf16[1,1,32,512]{3,2,1,0:T(8,128)(2,1)S(1)}, u32[]{:S(2)}, u32[]{:S(2)}) collective-permute-start(bf16[1,1,32,512]{3,2,1,0:T(8,128)(2,1)S(1)} %slice_bitcast_fusion.1), channel_id=1, source_target_pairs={{8,0},{16,8},{24,16},{0,24},{9,1},{17,9},{25,17},{1,25},{10,2},{18... | collective-permute-start | bytes 98312 | tf_op jit(solution)/shard_map/ppermute | solution.py:17
  118.3 1.9 %collective-permute-done.8 = bf16[1,1,32,512]{3,2,1,0:T(8,128)(2,1)S(1)} collective-permute-done((bf16[1,1,32,512]{3,2,1,0:T(8,128)(2,1)S(1)}, bf16[1,1,32,512]{3,2,1,0:T(8,128)(2,1)S(1)}, u32[]{:S(2)}, u32[]{:S(2)}) %collective-permute-start.8) | collective-permute-done | bytes 32800 | tf_op jit(solution)/shard_map/ppermute | solution.py:16
  120.8 3.5 %collective-permute-start.11 = (bf16[3,1,32,512]{3,2,1,0:T(8,128)(2,1)S(1)}, bf16[3,1,32,512]{3,2,1,0:T(8,128)(2,1)S(1)}, u32[]{:S(2)}, u32[]{:S(2)}) collective-permute-start(bf16[3,1,32,512]{3,2,1,0:T(8,128)(2,1)S(1)} %pad_maximum_fusion.5), channel_id=1, source_target_pairs={{1,0},{2,1},{3,2},{4,3},{5,4},{6,5},{7,6},{0,7},{9,8},{10,9},{11,1... | collective-permute-start | bytes 294920 | tf_op jit(solution)/shard_map/ppermute | solution.py:17
  124.5 2.0 %collective-permute-done.10 = bf16[3,1,32,512]{3,2,1,0:T(8,128)(2,1)S(1)} collective-permute-done((bf16[3,1,32,512]{3,2,1,0:T(8,128)(2,1)S(1)}, bf16[3,1,32,512]{3,2,1,0:T(8,128)(2,1)S(1)}, u32[]{:S(2)}, u32[]{:S(2)}) %collective-permute-start.10) | collective-permute-done | bytes 98336 | tf_op jit(solution)/shard_map/ppermute | solution.py:16
  127.7 1.4 %multiply_convert_fusion.2 = bf16[3,512,512]{2,1,0:T(8,128)(2,1)S(1)} fusion(bf16[3,512,512]{2,1,0:T(8,128)(2,1)S(1)} %bitcast.158, f32[512,512]{1,0:T(8,128)S(1)} %convolution_add_fusion.1, bf16[3,512,512]{2,1,0:T(8,128)(2,1)S(1)} %copy-done.5), kind=kOutput, calls=%fused_computation.19 | convolution fusion | flops 810024960 | bytes 4718592 | tf_op jit(solution)/shard_map/while/body/eval_jaxpr/dot_general | solution.py:23
  132.5 2.2 %fusion.124 = (f32[512]{0:T(512)S(1)}, f32[512,512]{0,1:T(8,128)S(1)}) fusion(bf16[3,512,512]{2,1,0:T(8,128)(2,1)} %param.32, f32[512,512]{1,0:T(8,128)S(1)} %copy-done.2, f32[512]{0:T(512)S(1)} %bitcast.155, bf16[512,512]{1,0:T(8,128)(2,1)S(1)} %select_reduce_fusion.2), kind=kOutput, calls=%fused_computation.216 | convolution fusion | flops 538967552 | bytes 3674112 | tf_op jit(solution)/shard_map/dot_general | solution.py:28
  (86 shorter events, 18.2 us)
Async XLA Ops:
  0.6 20.1 %copy-start = (bf16[512,512]{1,0:T(8,128)(2,1)S(1)}, bf16[512,512]{1,0:T(8,128)(2,1)}, u32[]{:S(2)}) copy-start(bf16[512,512]{1,0:T(8,128)(2,1)} %param.17) | copy-start | bytes 1572868
  0.6 15.1 %copy-start.1 = (bf16[128,512]{1,0:T(8,128)(2,1)S(1)}, bf16[128,512]{1,0:T(8,128)(2,1)}, u32[]{:S(2)}) copy-start(bf16[128,512]{1,0:T(8,128)(2,1)} %param.18) | copy-start | bytes 393220
  0.7 16.4 %copy-start.8 = (f32[2,512]{1,0:T(2,128)S(1)}, f32[2,512]{1,0:T(2,128)}, u32[]{:S(2)}) copy-start(f32[2,512]{1,0:T(2,128)} %param.29) | copy-start | bytes 12292
  0.7 20.1 %copy-start.9 = (f32[2,512]{1,0:T(2,128)S(1)}, f32[2,512]{1,0:T(2,128)}, u32[]{:S(2)}) copy-start(f32[2,512]{1,0:T(2,128)} %param.31) | copy-start | bytes 12292
  1.6 15.4 %collective-permute-start = (bf16[1,1,128,512]{3,2,1,0:T(8,128)(2,1)S(1)}, bf16[1,1,128,512]{3,2,1,0:T(8,128)(2,1)S(1)}, u32[]{:S(2)}, u32[]{:S(2)}) collective-permute-start(bf16[1,1,128,512]{3,2,1,0:T(8,128)(2,1)S(1)} %slice_bitcast_fusion), channel_id=1, source_target_pairs={{0,8},{8,16},{16,24},{24,0},{1,9},{9,17},{17,25},{25,1},{2,10},{10... | collective-permute-start | bytes 393224 | tf_op jit(solution)/shard_map/ppermute | solution.py:16
  4.7 12.4 %collective-permute-start.1 = (bf16[1,1,128,512]{3,2,1,0:T(8,128)(2,1)S(1)}, bf16[1,1,128,512]{3,2,1,0:T(8,128)(2,1)S(1)}, u32[]{:S(2)}, u32[]{:S(2)}) collective-permute-start(bf16[1,1,128,512]{3,2,1,0:T(8,128)(2,1)S(1)} %slice_bitcast_fusion), channel_id=1, source_target_pairs={{8,0},{16,8},{24,16},{0,24},{9,1},{17,9},{25,17},{1,25},{10,2},{18... | collective-permute-start | bytes 393224 | tf_op jit(solution)/shard_map/ppermute | solution.py:17
  17.1 10.8 %collective-permute-start.2 = (bf16[3,1,128,512]{3,2,1,0:T(8,128)(2,1)S(1)}, bf16[3,1,128,512]{3,2,1,0:T(8,128)(2,1)S(1)}, u32[]{:S(2)}, u32[]{:S(2)}) collective-permute-start(bf16[3,1,128,512]{3,2,1,0:T(8,128)(2,1)S(1)} %pad_maximum_fusion.1), channel_id=1, source_target_pairs={{0,1},{1,2},{2,3},{3,4},{4,5},{5,6},{6,7},{7,0},{8,9},{9,10},{10,1... | collective-permute-start | bytes 1179656 | tf_op jit(solution)/shard_map/ppermute | solution.py:16
  17.2 11.0 %collective-permute-start.3 = (bf16[3,1,128,512]{3,2,1,0:T(8,128)(2,1)S(1)}, bf16[3,1,128,512]{3,2,1,0:T(8,128)(2,1)S(1)}, u32[]{:S(2)}, u32[]{:S(2)}) collective-permute-start(bf16[3,1,128,512]{3,2,1,0:T(8,128)(2,1)S(1)} %pad_maximum_fusion.1), channel_id=1, source_target_pairs={{1,0},{2,1},{3,2},{4,3},{5,4},{6,5},{7,6},{0,7},{9,8},{10,9},{11,1... | collective-permute-start | bytes 1179656 | tf_op jit(solution)/shard_map/ppermute | solution.py:17
  28.3 8.3 %copy-start.3 = (bf16[3,512,512]{2,1,0:T(8,128)(2,1)S(1)}, bf16[3,512,512]{2,1,0:T(8,128)(2,1)}, u32[]{:S(2)}) copy-start(bf16[3,512,512]{2,1,0:T(8,128)(2,1)} %param.22) | copy-start | bytes 4718596
  48.8 5.5 %collective-permute-start.4 = (bf16[1,1,32,512]{3,2,1,0:T(8,128)(2,1)S(1)}, bf16[1,1,32,512]{3,2,1,0:T(8,128)(2,1)S(1)}, u32[]{:S(2)}, u32[]{:S(2)}) collective-permute-start(bf16[1,1,32,512]{3,2,1,0:T(8,128)(2,1)S(1)} %slice_bitcast_fusion.2), channel_id=1, source_target_pairs={{0,8},{8,16},{16,24},{24,0},{1,9},{9,17},{17,25},{25,1},{2,10},{10... | collective-permute-start | bytes 98312 | tf_op jit(solution)/shard_map/ppermute | solution.py:16
  50.0 4.6 %collective-permute-start.5 = (bf16[1,1,32,512]{3,2,1,0:T(8,128)(2,1)S(1)}, bf16[1,1,32,512]{3,2,1,0:T(8,128)(2,1)S(1)}, u32[]{:S(2)}, u32[]{:S(2)}) collective-permute-start(bf16[1,1,32,512]{3,2,1,0:T(8,128)(2,1)S(1)} %slice_bitcast_fusion.2), channel_id=1, source_target_pairs={{8,0},{16,8},{24,16},{0,24},{9,1},{17,9},{25,17},{1,25},{10,2},{18... | collective-permute-start | bytes 98312 | tf_op jit(solution)/shard_map/ppermute | solution.py:17
  54.6 44.7 %collective-permute-start.6 = (bf16[3,1,32,512]{3,2,1,0:T(8,128)(2,1)S(1)}, bf16[3,1,32,512]{3,2,1,0:T(8,128)(2,1)S(1)}, u32[]{:S(2)}, u32[]{:S(2)}) collective-permute-start(bf16[3,1,32,512]{3,2,1,0:T(8,128)(2,1)S(1)} %pad_maximum_fusion.4), channel_id=1, source_target_pairs={{0,1},{1,2},{2,3},{3,4},{4,5},{5,6},{6,7},{7,0},{8,9},{9,10},{10,1... | collective-permute-start | bytes 294920 | tf_op jit(solution)/shard_map/ppermute | solution.py:16
  56.1 43.2 %collective-permute-start.7 = (bf16[3,1,32,512]{3,2,1,0:T(8,128)(2,1)S(1)}, bf16[3,1,32,512]{3,2,1,0:T(8,128)(2,1)S(1)}, u32[]{:S(2)}, u32[]{:S(2)}) collective-permute-start(bf16[3,1,32,512]{3,2,1,0:T(8,128)(2,1)S(1)} %pad_maximum_fusion.4), channel_id=1, source_target_pairs={{1,0},{2,1},{3,2},{4,3},{5,4},{6,5},{7,6},{0,7},{9,8},{10,9},{11,1... | collective-permute-start | bytes 294920 | tf_op jit(solution)/shard_map/ppermute | solution.py:17
  99.3 3.8 %copy-start.4 = (bf16[3,512,512]{2,1,0:T(8,128)(2,1)S(1)}, bf16[3,512,512]{2,1,0:T(8,128)(2,1)}, u32[]{:S(2)}) copy-start(bf16[3,512,512]{2,1,0:T(8,128)(2,1)} %param.26) | copy-start | bytes 4718596
  113.1 5.1 %copy-start.7 = (s32[3,512]{1,0:T(4,128)S(1)}, s32[3,512]{1,0:T(4,128)}, u32[]{:S(2)}) copy-start(s32[3,512]{1,0:T(4,128)} %param.21) | copy-start | bytes 18436
  113.2 11.1 %copy-start.10 = (f32[2,512]{1,0:T(2,128)S(1)}, f32[2,512]{1,0:T(2,128)}, u32[]{:S(2)}) copy-start(f32[2,512]{1,0:T(2,128)} %param.33) | copy-start | bytes 12292
  115.3 12.4 %copy-start.6 = (bf16[128,512]{1,0:T(8,128)(2,1)}, bf16[128,512]{1,0:T(8,128)(2,1)S(1)}, u32[]{:S(2)}) copy-start(bf16[128,512]{1,0:T(8,128)(2,1)S(1)} %add_convert_fusion.1) | copy-start | bytes 393220
  115.3 4.9 %collective-permute-start.8 = (bf16[1,1,32,512]{3,2,1,0:T(8,128)(2,1)S(1)}, bf16[1,1,32,512]{3,2,1,0:T(8,128)(2,1)S(1)}, u32[]{:S(2)}, u32[]{:S(2)}) collective-permute-start(bf16[1,1,32,512]{3,2,1,0:T(8,128)(2,1)S(1)} %slice_bitcast_fusion.1), channel_id=1, source_target_pairs={{0,8},{8,16},{16,24},{24,0},{1,9},{9,17},{17,25},{25,1},{2,10},{10... | collective-permute-start | bytes 98312 | tf_op jit(solution)/shard_map/ppermute | solution.py:16
  115.4 5.3 %collective-permute-start.9 = (bf16[1,1,32,512]{3,2,1,0:T(8,128)(2,1)S(1)}, bf16[1,1,32,512]{3,2,1,0:T(8,128)(2,1)S(1)}, u32[]{:S(2)}, u32[]{:S(2)}) collective-permute-start(bf16[1,1,32,512]{3,2,1,0:T(8,128)(2,1)S(1)} %slice_bitcast_fusion.1), channel_id=1, source_target_pairs={{8,0},{16,8},{24,16},{0,24},{9,1},{17,9},{25,17},{1,25},{10,2},{18... | collective-permute-start | bytes 98312 | tf_op jit(solution)/shard_map/ppermute | solution.py:17
  120.7 5.9 %collective-permute-start.10 = (bf16[3,1,32,512]{3,2,1,0:T(8,128)(2,1)S(1)}, bf16[3,1,32,512]{3,2,1,0:T(8,128)(2,1)S(1)}, u32[]{:S(2)}, u32[]{:S(2)}) collective-permute-start(bf16[3,1,32,512]{3,2,1,0:T(8,128)(2,1)S(1)} %pad_maximum_fusion.5), channel_id=1, source_target_pairs={{0,1},{1,2},{2,3},{3,4},{4,5},{5,6},{6,7},{7,0},{8,9},{9,10},{10,1... | collective-permute-start | bytes 294920 | tf_op jit(solution)/shard_map/ppermute | solution.py:16
  120.8 5.8 %collective-permute-start.11 = (bf16[3,1,32,512]{3,2,1,0:T(8,128)(2,1)S(1)}, bf16[3,1,32,512]{3,2,1,0:T(8,128)(2,1)S(1)}, u32[]{:S(2)}, u32[]{:S(2)}) collective-permute-start(bf16[3,1,32,512]{3,2,1,0:T(8,128)(2,1)S(1)} %pad_maximum_fusion.5), channel_id=1, source_target_pairs={{1,0},{2,1},{3,2},{4,3},{5,4},{6,5},{7,6},{0,7},{9,8},{10,9},{11,1... | collective-permute-start | bytes 294920 | tf_op jit(solution)/shard_map/ppermute | solution.py:17
  124.5 3.1 %copy-start.5 = (bf16[3,512,512]{2,1,0:T(8,128)(2,1)S(1)}, bf16[3,512,512]{2,1,0:T(8,128)(2,1)}, u32[]{:S(2)}) copy-start(bf16[3,512,512]{2,1,0:T(8,128)(2,1)} %param.30) | copy-start | bytes 4718596
  131.3 1.2 copy-start.2
where the time goes:
time: 137 us; the launch traced here: 136 us
  matrix products  42.9 us (31%)
  blocking collectives  40.8 us (30%)
  starting transfers between devices  20.9 us (15%)
  other arithmetic  16.4 us (12%)
  waiting for transfers between devices  10.7 us (8%)
  local copies, waits for them, and re-layouts  3.23 us (2%)
    all_gather x1, blocking collectives, per_device(): coarse_rows = lax.all_gather(encoded[:CM], ('gx', 'gy'), axis=0, tiled=True)  40.8 us
    dot_general x9, matrix products, project(): return jnp.dot(latent, weight, preferred_element_type=jnp.float32)  18.3 us
    ppermute x6, starting transfers between devices, with_halo(): after = lax.ppermute(initial, axis, down)  15.1 us
    dot_general x3, matrix products, one_block(): jnp.dot(selector, sources, preferred_element_type=jnp.float32)  13 us
    dot_general x6, matrix products, finish(): output = jnp.dot(hidden, weights[2], preferred_element_type=jnp.float32)  11.6 us
    ppermute x6, waiting for transfers between devices, with_halo(): before = lax.ppermute(last, axis, up)  9.65 us
    ppermute x6, starting transfers between devices, with_halo(): before = lax.ppermute(last, axis, up)  5.85 us
    reduce_sum x6, other arithmetic, finish(): spread = jnp.mean(centred * centred, axis=-1, keepdims=True)  4 us
  transfers between devices with their start and end apart: 12, of which 6 were waited for; matrix products, arithmetic and copies ran while one was open for 11% of the time, Pallas kernels for 0%

commit v1 on v0

v1 whole, which is shorter than its diff:
```python
import functools

import jax
import jax.numpy as jnp
from jax import lax
from jax.experimental import pallas as pl
from jax.experimental.pallas import tpu as pltpu
from jax.sharding import PartitionSpec as P

AXES = ("gx", "gy")
CM = 4
EPS = 1e-05
BF = jnp.bfloat16
F32 = jnp.float32
I32 = jnp.int32
SDS = jax.ShapeDtypeStruct


def mm(a, b):
    return jnp.dot(a, b, preferred_element_type=F32)


def half_silu(half):
    return (half + half * jnp.tanh(half)).astype(BF)


def inverse_norm(centred):
    spread = jnp.mean(centred * centred, axis=-1, keepdims=True)
    return lax.rsqrt(spread + EPS)


def centre(w):
    w = w.astype(F32)
    return (w - jnp.mean(w, axis=-1, keepdims=True)).astype(BF)


class Mover:
    def __init__(self, sems):
        self.sems = sems
        self.used = 0

    def start(self, source, target):
        copy = pltpu.make_async_copy(source, target, self.sems.at[self.used])
        self.used += 1
        copy.start()
        return copy


def launch(body, name, ins, outs, scratch, copies, flops, nbytes):
    hbm = pl.BlockSpec(memory_space=pltpu.HBM)
    return pl.pallas_call(
        body,
        out_shape=outs,
        in_specs=[hbm] * len(ins),
        out_specs=[hbm] * len(outs),
        scratch_shapes=[pltpu.VMEM(s, d) for s, d in scratch] + [pltpu.SemaphoreType.DMA((copies,))],
        compiler_params=pltpu.CompilerParams(vmem_limit_bytes=56 << 20),
        cost_estimate=pl.CostEstimate(flops=flops, bytes_accessed=nbytes, transcendentals=0),
        name=name,
    )(*ins)


def border_kernel(x, w, out, x_v, w_v, out_v, sems):
    mover = Mover(sems)
    loads = [mover.start(x.at[pl.ds(0, x_v.shape[0])], x_v), mover.start(w.at[0], w_v)]
    for load in loads:
        load.wait()
    out_v[...] = (mm(x_v[...], w_v[...]) * 0.5).astype(BF)
    mover.start(out_v, out).wait()


def split(value, by):
    if by & (by - 1) == 0:
        return value >> (by.bit_length() - 1), value & (by - 1)
    return value // by, value % by


def locate(ids, rows, border, coarse, sizes, places):
    size_x, size_y = sizes
    place_x, place_y = places
    owner, offset = split(jnp.maximum(ids, 0), rows)
    owner_x, owner_y = split(owner, size_y)
    step_x = owner_x - place_x
    step_x = jnp.where(step_x < 0, step_x + size_x, step_x)
    step_y = owner_y - place_y
    step_y = jnp.where(step_y < 0, step_y + size_y, step_y)
    ahead_x, ahead_y = (place_x & 1) == 0, (place_y & 1) == 0
    pair_x = jnp.where(ahead_x, 1, size_x - 1)
    pair_y = jnp.where(ahead_y, 1, size_y - 1)
    kind_x = jnp.where(step_x == 0, 0, jnp.where(step_x == pair_x, 1, 2))
    kind_y = jnp.where(step_y == 0, 0, jnp.where(step_y == pair_y, 1, 2))
    near_x = (step_x <= 1) | (step_x == size_x - 1)
    near_y = (step_y <= 1) | (step_y == size_y - 1)
    group = 3 * border + coarse * size_y
    first = jnp.where(kind_x == 0, rows - border, rows + 2 * border + (kind_x - 1) * group)
    found = first + kind_y * border + offset
    if coarse:
        flip = owner_y ^ place_y
        column = jnp.where(kind_x == 0, 0, 3 * border)
        far = first + column
        tail = rows + 2 * border + 2 * group
        far = jnp.where(kind_x == 0, tail, far)
        far = jnp.where(near_x, far, tail + (step_x - 1) * coarse * size_y)
        far = far + (flip ^ (flip >> 1)) * coarse + offset
        nearby = near_x & near_y & (offset < border)
        found = jnp.where(nearby, found, far)
    found = jnp.where((step_x == 0) & (step_y == 0), offset, found)
    return jnp.where(ids >= 0, found, -1)


def turned(found):
    degree, count = found.shape
    pad = -degree % 8
    if pad:
        found = jnp.concatenate([found, jnp.full((pad, count), -1, I32)], axis=0)
    return found.astype(F32).T.astype(I32)


def prepare_kernel(
    sizes, shapes,
    grid, mesh, eids, mids, dids, ee, en, pe, pn, de, dn, eb, db,
    own_o, ebase_o, dbase_o, eat_o, mat_o, dat_o, ee2_o, en2_o, pe2_o, pn2_o, de2_o, dn2_o,
    grid_v, mesh_v, eids_v, mids_v, dids_v, w0_v, w1_v, wd_v, eb_v, db_v, w2_v,
    own_v, ebase_v, dbase_v, eat_v, mat_v, dat_v, c2_v, sems,
):
    mover = Mover(sems)
    grid_rows, mesh_rows, grid_border, mesh_border = shapes
    heads = [
        mover.start(a, b)
        for a, b in (
            (eids, eids_v), (mids, mids_v), (dids, dids_v), (grid, grid_v), (mesh, mesh_v),
            (ee.at[0], w0_v), (ee.at[1], w1_v), (de.at[1], wd_v), (eb, eb_v), (db, db_v),
        )
    ]
    seconds = [mover.start(w.at[2], w2_v.at[i]) for i, w in enumerate((ee, en, pe, pn, de, dn))]
    for head in heads:
        head.wait()
    places = (lax.axis_index("gx"), lax.axis_index("gy"))
    tails = []
    own_v[...] = (mm(grid_v[...], w0_v[...]) * 0.5).astype(BF)
    tails.append(mover.start(own_v, own_o))
    eat_v[...] = turned(locate(eids_v[...], grid_rows, grid_border, 0, sizes, places))
    tails.append(mover.start(eat_v, eat_o))
    ebase_v[...] = (mm(mesh_v[...], w1_v[...]) + eb_v[0:1, :]) * 0.5
    tails.append(mover.start(ebase_v, ebase_o))
    for i, (second, out) in enumerate(zip(seconds, (ee2_o, en2_o, pe2_o, pn2_o, de2_o, dn2_o))):
        second.wait()
        c2_v[i] = centre(w2_v[i])
        tails.append(mover.start(c2_v.at[i], out))
    mat_v[...] = turned(locate(mids_v[...], mesh_rows, mesh_border, CM, sizes, places))
    tails.append(mover.start(mat_v, mat_o))
    dat_v[...] = turned(locate(dids_v[...], mesh_rows, mesh_border, 0, sizes, places))
    tails.append(mover.start(dat_v, dat_o))
    dbase_v[...] = (mm(grid_v[...], wd_v[...]) + db_v[0:1, :]) * 0.5
    tails.append(mover.start(dbase_v, dbase_o))
    for tail in tails:
        tail.wait()


def edge_sum(places, degree, table, base, w2, vectors, slots_per_step):
    rows, width = base.shape
    lanes = lax.broadcasted_iota(I32, (rows, table.shape[0]), 1)
    total = jnp.zeros((rows, width), F32)
    for first in range(0, degree, slots_per_step):
        ks = range(first, min(first + slots_per_step, degree))
        count = len(ks)
        selector = jnp.concatenate(
            [(places[:, k : k + 1] == lanes).astype(F32).astype(BF) for k in ks], axis=0
        )
        half = mm(selector, table[...]).reshape(count, rows, width) + base[None]
        hidden = half_silu(half.reshape(count * rows, width))
        y = mm(hidden, w2)
        scale = inverse_norm(y).reshape(count, rows, 1)
        y = y.reshape(count, rows, width)
        for i, k in enumerate(ks):
            live = (places[:, k : k + 1] >= 0).astype(F32)
            total = total + y[i] * (scale[i] * live)
    return total * (1.0 + vectors[1:2, :])


def node_update(x, summed, w0, w1, w2, vectors):
    half = (mm(x, w0) + mm(summed.astype(BF), w1) + vectors[0:1, :]) * 0.5
    y = mm(half_silu(half), w2)
    return (x.astype(F32) + y * inverse_norm(y) * (1.0 + vectors[1:2, :])).astype(BF)


def mesh_stage(x, x_at, places, at, count, pieces, base, base_at, ew2, ev, nw, nw2, nv, following, fv, joined, steps, name):
    width = x.shape[1]
    degree = places.shape[1]
    table_rows = sum(p.shape[0] for p in pieces)
    again = fv is not None
    ins = [x, places, base, ew2, ev, nw, nw2, nv, following] + ([fv] if again else []) + ([joined] if joined is not None else []) + pieces
    rows_out = count + (joined.shape[0] if joined is not None else 0)
    outs = [SDS((rows_out, width), BF), SDS((count, width), BF)] + ([SDS((count, width), F32)] if again else [])
    scratch = [
        ((count, width), BF), ((count, degree), I32), ((count, width), F32), ((width, width), BF), ((2, width), F32),
        ((2, width, width), BF), ((width, width), BF), ((2, width), F32), ((2, width, width), BF), ((2, width), F32),
        ((table_rows, width), BF), ((rows_out, width), BF), ((count, width), BF), ((count, width), F32),
    ]

    def body(*refs):
        refs = list(refs)
        x_h, places_h, base_h, ew2_h, ev_h, nw_h, nw2_h, nv_h, follow_h = refs[:9]
        refs = refs[9:]
        fv_h = refs.pop(0) if again else None
        joined_h = refs.pop(0) if joined is not None else None
        pieces_h, refs = refs[: len(pieces)], refs[len(pieces) :]
        outs_h, refs = refs[: len(outs)], refs[len(outs) :]
        (x_v, places_v, base_v, ew2_v, ev_v, nw_v, nw2_v, nv_v, follow_v, fv_v, table_v, new_v, proj_v, nbase_v, sems) = refs
        mover = Mover(sems)
        early = []
        start = 0
        for piece in pieces_h:
            early.append(mover.start(piece, table_v.at[pl.ds(start, piece.shape[0])]))
            start += piece.shape[0]
        early.append(mover.start(places_h.at[pl.ds(at, count)], places_v))
        early.append(mover.start(base_h.at[pl.ds(base_at, count)], base_v))
        early.append(mover.start(ew2_h, ew2_v))
        early.append(mover.start(ev_h, ev_v))
        late = [
            mover.start(x_h.at[pl.ds(x_at, count)], x_v),
            mover.start(nw_h.at[pl.ds(0, 2)], nw_v),
            mover.start(nw2_h, nw2_v),
            mover.start(nv_h, nv_v),
            mover.start(follow_h.at[pl.ds(0, 2)], follow_v),
        ]
        if again:
            late.append(mover.start(fv_h, fv_v))
        if joined is not None:
            late.append(mover.start(joined_h, new_v.at[pl.ds(0, joined.shape[0])]))
        for load in early:
            load.wait()
        summed = edge_sum(places_v[...], degree, table_v, base_v[...], ew2_v[...], ev_v, steps)
        for load in late:
            load.wait()
        new = node_update(x_v[...], summed, nw_v[0], nw_v[1], nw2_v[...], nv_v)
        new_v[pl.ds(rows_out - count, count), :] = new
        proj_v[...] = (mm(new, follow_v[0]) * 0.5).astype(BF)
        tails = [mover.start(proj_v, outs_h[1]), mover.start(new_v, outs_h[0])]
        if again:
            nbase_v[...] = (mm(new, follow_v[1]) + fv_v[0:1, :]) * 0.5
            tails.append(mover.start(nbase_v, outs_h[2]))
        for tail in tails:
            tail.wait()

    flops = count * degree * (2 * width * table_rows + 2 * width * width)
    return launch(body, name, ins, outs, scratch, len(pieces) + 16, flops, 6 << 20)


def decode_stage(x, places, degree, pieces, base, ew2, ev, nw, nw2, nv, block):
    rows, width = x.shape
    table_rows = sum(p.shape[0] for p in pieces)
    ins = [x, places, base, ew2, ev, nw, nw2, nv] + pieces
    outs = [SDS((rows, width), BF)]
    scratch = [
        ((rows, width), BF), (places.shape, I32), ((rows, width), F32), ((width, width), BF), ((2, width), F32),
        ((2, width, width), BF), ((width, width), BF), ((2, width), F32), ((table_rows, width), BF), ((rows, width), BF),
    ]

    def body(*refs):
        refs = list(refs)
        x_h, places_h, base_h, ew2_h, ev_h, nw_h, nw2_h, nv_h = refs[:8]
        pieces_h = refs[8 : 8 + len(pieces)]
        out_h, x_v, places_v, base_v, ew2_v, ev_v, nw_v, nw2_v, nv_v, table_v, new_v, sems = refs[8 + len(pieces) :]
        mover = Mover(sems)
        loads = []
        start = 0
        for piece in pieces_h:
            loads.append(mover.start(piece, table_v.at[pl.ds(start, piece.shape[0])]))
            start += piece.shape[0]
        loads += [
            mover.start(a, b)
            for a, b in (
                (places_h, places_v), (base_h, base_v), (ew2_h, ew2_v), (ev_h, ev_v), (x_h, x_v),
                (nw_h.at[pl.ds(0, 2)], nw_v), (nw2_h, nw2_v), (nv_h, nv_v),
            )
        ]
        for load in loads:
            load.wait()
        tails = []
        for at in range(0, rows, block):
            part = pl.ds(at, block)
            summed = edge_sum(places_v[part, :], degree, table_v, base_v[part, :], ew2_v[...], ev_v, degree)
            new_v[part, :] = node_update(x_v[part, :], summed, nw_v[0], nw_v[1], nw2_v[...], nv_v)
            tails.append(mover.start(new_v.at[part], out_h.at[part]))
        for tail in tails:
            tail.wait()

    flops = rows * degree * (2 * width * table_rows + 2 * width * width)
    return launch(body, "decode", ins, outs, scratch, len(pieces) + 8 + rows // block, flops, 6 << 20)[0]


def sender(size_x, size_y):
    def send(rows, move):
        pairs = []
        for i in range(size_x):
            for j in range(size_y):
                a, b = move(i, j)
                pairs.append((i * size_y + j, (a % size_x) * size_y + b % size_y))
        return lax.ppermute(rows, AXES, pairs)

    return send


def next_pair(i):
    return i + 1 if i % 2 else i - 1


def per_device(
    grid_latent, mesh_latent, encode_senders, mesh_senders, decode_senders,
    encoder_edges, encoder_edgebias, encoder_nodes, encoder_nodebias,
    process_edges, process_edgebias, process_nodes, process_nodebias,
    decoder_edges, decoder_edgebias, decoder_nodes, decoder_nodebias,
):
    grid_rows, width = grid_latent.shape
    mesh_rows = mesh_latent.shape[0]
    grid_border = grid_rows // 4
    mesh_border = mesh_rows // 4
    size_x = lax.axis_size("gx")
    size_y = lax.axis_size("gy")
    square = 2 * width * width
    send = sender(size_x, size_y)
    pair_x = lambda i, j: (i ^ 1, j)
    next_x = lambda i, j: (next_pair(i), j)
    pair_y = lambda i, j: (i, j ^ 1)
    next_y = lambda i, j: (i, next_pair(j))

    border = launch(
        border_kernel, "project_border", [grid_latent, encoder_edges], [SDS((grid_border, width), BF)],
        [((grid_border, width), BF), ((width, width), BF), ((grid_border, width), BF)], 3, grid_border * square, 1 << 20,
    )[0]
    e = send(border, pair_x)
    o = send(border, next_x)
    z = send(border, next_y)
    c = send(border, pair_y)

    degrees = [ids.shape[0] + -ids.shape[0] % 8 for ids in (encode_senders, mesh_senders, decode_senders)]
    square_shape = ((width, width), BF)
    outs = [
        ((grid_rows, width), BF), ((mesh_rows, width), F32), ((grid_rows, width), F32),
        ((mesh_rows, degrees[0]), I32), ((mesh_rows, degrees[1]), I32), ((grid_rows, degrees[2]), I32),
    ]
    own, base, grid_base, encode_at, mesh_at, decode_at, ee2, en2, pe2, pn2, de2, dn2 = launch(
        functools.partial(prepare_kernel, (size_x, size_y), (grid_rows, mesh_rows, grid_border, mesh_border)), "prepare",
        [
            grid_latent, mesh_latent, encode_senders, mesh_senders, decode_senders, encoder_edges, encoder_nodes,
            process_edges, process_nodes, decoder_edges, decoder_nodes, encoder_edgebias, decoder_edgebias,
        ],
        [SDS(s, d) for s, d in outs + [square_shape] * 6],
        [
            ((grid_rows, width), BF), ((mesh_rows, width), BF), (encode_senders.shape, I32), (mesh_senders.shape, I32),
            (decode_senders.shape, I32), square_shape, square_shape, square_shape, ((2, width), F32), ((2, width), F32),
            ((6, width, width), BF), *outs, ((6, width, width), BF),
        ],
        28, 2 * grid_rows * square, 12 << 20,
    )
    ec = send(e, pair_y)
    oc = send(o, pair_y)
    ez = send(z, pair_x)
    oz = send(z, next_x)
    pieces = [own, c, z, e, ec, ez, o, oc, oz]

    cuts = [0, mesh_border, mesh_border * 5 // 2, mesh_rows]
    encoded = []
    for at, end in zip(cuts, cuts[1:]):
        encoded.append(
            mesh_stage(
                mesh_latent, at, encode_at, at, end - at, pieces, base, at, ee2, encoder_edgebias, encoder_nodes, en2,
                encoder_nodebias, process_edges, process_edgebias, None, 512 // (end - at), "encode",
            )
        )

    border = encoded[0][1]
    c = send(border, pair_y)
    z = send(border, next_y)
    column = jnp.concatenate([border[:CM], c[:CM]], axis=0)
    step = 2
    while step < size_y:
        flip = 2 * step - 1
        column = jnp.concatenate([column, send(column, lambda i, j, flip=flip: (i, j ^ flip))], axis=0)
        step *= 2
    stack = jnp.concatenate([border, c, z, column], axis=0)
    e = send(stack, pair_x)
    o = send(stack, next_x)
    far = [send(column, lambda i, j, d=d: (i - d, j)) for d in range(2, size_x - 1)]
    pieces = [part[1] for part in encoded] + [c, z, e, o, column] + far

    x = jnp.concatenate([part[0] for part in encoded[1:]], axis=0)
    base = jnp.concatenate([part[2] for part in encoded[1:]], axis=0)
    first = mesh_stage(
        encoded[0][0], 0, mesh_at, 0, mesh_border, pieces, encoded[0][2], 0, pe2, process_edgebias, process_nodes, pn2,
        process_nodebias, decoder_edges, None, None, 512 // mesh_border, "process",
    )
    border = first[1]
    c = send(border, pair_y)
    z = send(border, next_y)
    rest = mesh_rows - mesh_border
    processed, projected = mesh_stage(
        x, 0, mesh_at, mesh_border, rest, pieces, base, 0, pe2, process_edgebias, process_nodes, pn2,
        process_nodebias, decoder_edges, None, first[0], 4, "process",
    )
    stack = jnp.concatenate([border, c, z], axis=0)
    e = send(stack, pair_x)
    o = send(stack, next_x)
    decoded = decode_stage(
        grid_latent, decode_at, decode_senders.shape[0], [border, projected, c, z, e, o], grid_base, de2, decoder_edgebias,
        decoder_nodes, dn2, decoder_nodebias, 128,
    )
    return (decoded, processed)


def solution(mesh):
    rows = P(AXES, None)
    senders = P(None, AXES)
    return jax.shard_map(
        per_device,
        mesh=mesh,
        in_specs=(rows, rows, senders, senders, senders) + (P(),) * 12,
        out_specs=(rows, rows),
        check_vma=False,
    )
```

time: 137 us -> 90.2 us (0.66)
  Pallas kernels: 0 us -> 47.8 us
  matrix products: 42.9 us -> 0 us
  blocking collectives: 40.8 us -> 0 us
  other arithmetic: 16.4 us -> 3.05 us
  waiting for transfers between devices: 10.7 us -> 14.2 us
    pallas_call x0 -> x8, Pallas kernels: none -> 47.8 us  [launch(): pl.pallas_call(body, out_shape=outs, in_specs=[hbm] * len(ins), out_specs...]
    dot_general x18 -> x0, matrix products: 42.9 us -> none  [the longest x9 18.3 us: project(): return jnp.dot(latent, weight, preferred_element_type=jnp.float32)]
    all_gather x1 -> x0, blocking collectives: 40.8 us -> none  [per_device(): coarse_rows = lax.all_gather(encoded[:CM], ('gx', 'gy'), axis=0, tiled=True)]
    reduce_sum x9 -> x0, other arithmetic: 6.04 us -> none  [the longest x6 4 us: finish(): spread = jnp.mean(centred * centred, axis=-1, keepdims=True)]
    ppermute x12 -> x19, waiting for transfers between devices: 10.7 us -> 14.2 us  [send(): return lax.ppermute(rows, AXES, pairs)]
    mul x3 -> x0, other arithmetic: 3.39 us -> none  [finish(): return centred * lax.rsqrt(spread + 1e-05) * (1.0 + vectors[1])]
    concatenate x6 -> x5, other arithmetic: 0.28 us -> 3.05 us  [the longest x1 1.58 us: per_device(): base = jnp.concatenate([part[2] for part in encoded[1:]], axis=0)]
    add x6 -> x0, other arithmetic: 2.32 us -> none  [finish(): return centred * lax.rsqrt(spread + 1e-05) * (1.0 + vectors[1])]
  transfers between devices with their start and end apart: 12 -> 19, of which waited for: 6 -> 7; matrix products, arithmetic and copies ran while one was open for 11% -> 4% of each run, Pallas kernels for 0% -> 30%
where the time goes in v1:
time: 90.2 us; the launch traced here: 89.9 us
  Pallas kernels  47.8 us (53%)
  starting transfers between devices  20.8 us (23%)
  waiting for transfers between devices  14.2 us (16%)
  other arithmetic  3.05 us (3%)
  local copies, waits for them, and re-layouts  2.81 us (3%)
  between operations  1.14 us (1%)
    pallas_call x8, Pallas kernels, launch(): pl.pallas_call(body, out_shape=outs, in_specs=[hbm] * len(ins), out_specs...  47.8 us
    ppermute x19, starting transfers between devices, send(): return lax.ppermute(rows, AXES, pairs)  20.8 us
    ppermute x19, waiting for transfers between devices, send(): return lax.ppermute(rows, AXES, pairs)  14.2 us
    unnamed x44, local copies, waits for them, and re-layouts  2.76 us
  transfers between devices with their start and end apart: 19, of which 7 were waited for; matrix products, arithmetic and copies ran while one was open for 4% of the time, Pallas kernels for 30%

profile of v1, /device:TPU:0, one launch (start us, length us, event | category | flops | bytes accessed | tf_op | source)
XLA Modules:
  0.0 89.9 jit_solution(9468098303804210111)
XLA Ops:
  0.6 2.0 %project_border.1 = bf16[128,512]{1,0:T(8,128)(2,1)} custom-call(bf16[512,512]{1,0:T(8,128)(2,1)} %refs_0_.7, bf16[3,512,512]{2,1,0:T(8,128)(2,1)} %w.1), custom_call_target="tpu_custom_call" | custom-call | flops 67108864 | bytes 1048576 | tf_op jit(solution)/shard_map/project_border/pallas_call | solution.py:51
  2.7 3.0 %collective-permute-start.2 = (bf16[128,512]{1,0:T(8,128)(2,1)}, bf16[128,512]{1,0:T(8,128)(2,1)S(1)}, u32[]{:S(2)}, u32[]{:S(2)}) collective-permute-start(bf16[128,512]{1,0:T(8,128)(2,1)} %project_border.1), channel_id=1, source_target_pairs={{0,8},{1,9},{2,10},{3,11},{4,12},{5,13},{6,14},{7,15},{8,0},{9,1},... | collective-permute-start | bytes 393224 | tf_op jit(solution)/shard_map/ppermute | solution.py:300
  5.7 2.8 %collective-permute-start.1 = (bf16[128,512]{1,0:T(8,128)(2,1)}, bf16[128,512]{1,0:T(8,128)(2,1)S(1)}, u32[]{:S(2)}, u32[]{:S(2)}) collective-permute-start(bf16[128,512]{1,0:T(8,128)(2,1)} %project_border.1), channel_id=1, source_target_pairs={{0,7},{1,2},{2,1},{3,4},{4,3},{5,6},{6,5},{7,0},{8,15},{9,10},{10,... | collective-permute-start | bytes 393224 | tf_op jit(solution)/shard_map/ppermute | solution.py:300
  8.5 1.5 %collective-permute-start.5 = (bf16[128,512]{1,0:T(8,128)(2,1)}, bf16[128,512]{1,0:T(8,128)(2,1)S(1)}, u32[]{:S(2)}, u32[]{:S(2)}) collective-permute-start(bf16[128,512]{1,0:T(8,128)(2,1)} %project_border.1), channel_id=1, source_target_pairs={{0,24},{1,25},{2,26},{3,27},{4,28},{5,29},{6,30},{7,31},{8,16},{9,... | collective-permute-start | bytes 393224 | tf_op jit(solution)/shard_map/ppermute | solution.py:300
  10.5 2.6 %collective-permute-done.1.refs_12_ = bf16[128,512]{1,0:T(8,128)(2,1)S(1)} collective-permute-done((bf16[128,512]{1,0:T(8,128)(2,1)}, bf16[128,512]{1,0:T(8,128)(2,1)S(1)}, u32[]{:S(2)}, u32[]{:S(2)}) %collective-permute-start.1) | collective-permute-done | bytes 131104 | tf_op jit(solution)/shard_map/ppermute | solution.py:300
  13.1 2.0 %collective-permute-done.5.refs_16_ = bf16[128,512]{1,0:T(8,128)(2,1)S(1)} collective-permute-done((bf16[128,512]{1,0:T(8,128)(2,1)}, bf16[128,512]{1,0:T(8,128)(2,1)S(1)}, u32[]{:S(2)}, u32[]{:S(2)}) %collective-permute-start.5) | collective-permute-done | bytes 131104 | tf_op jit(solution)/shard_map/ppermute | solution.py:300
  15.1 1.3 %collective-permute-start.7 = (bf16[128,512]{1,0:T(8,128)(2,1)S(1)}, bf16[128,512]{1,0:T(8,128)(2,1)S(1)}, u32[]{:S(2)}, u32[]{:S(2)}) collective-permute-start(bf16[128,512]{1,0:T(8,128)(2,1)S(1)} %collective-permute-done.1.refs_12_), channel_id=1, source_target_pairs={{0,24},{1,25},{2,26},{3,27},{4,28},{5,29},{6,30},{7,31},{8,16},{9,... | collective-permute-start | bytes 393224 | tf_op jit(solution)/shard_map/ppermute | solution.py:300
  16.4 4.7 %prepare.1 = (bf16[512,512]{1,0:T(8,128)(2,1)}, f32[128,512]{1,0:T(8,128)}, f32[512,512]{1,0:T(8,128)}, s32[128,32]{1,0:T(8,128)}, s32[128,32]{1,0:T(8,128)}, /*...) custom-call(bf16[512,512]{1,0:T(8,128)(2,1)} %refs_0_.7, ...), custom_call_target="tpu_custom_call" | custom-call | flops 536870912 | bytes 12582912 | tf_op jit(solution)/shard_map/prepare/pallas_call | solution.py:51
  21.2 0.7 collective-permute-done.7.refs_18_
  22.0 0.6 copy-done.20
  22.6 6.1 %encode.3 = (bf16[32,512]{1,0:T(8,128)(2,1)}, bf16[32,512]{1,0:T(8,128)(2,1)}, f32[32,512]{1,0:T(8,128)}) custom-call(bf16[128,512]{1,0:T(8,128)(2,1)} %refs_0_.6, s32[128,32]{1,0:T(8,128)} %get-tuple-element.31.refs_1_, f32[128,512]{1,0:T(8,128)} %get-tuple-element.32.refs_2_, bf16[512,512]{1,0:T(8,128)(2,1)} %get-tuple-element.33.refs_3_, ...), custom_call_target="tpu_custom_call" | custom-call | flops 2147483648 | bytes 6291456 | tf_op jit(solution)/shard_map/encode/pallas_call | solution.py:51
  28.8 2.4 %collective-permute-start.9 = (bf16[32,512]{1,0:T(8,128)(2,1)}, bf16[32,512]{1,0:T(8,128)(2,1)S(1)}, u32[]{:S(2)}, u32[]{:S(2)}) collective-permute-start(bf16[32,512]{1,0:T(8,128)(2,1)} %get-tuple-element.41.refs_9_.refs_10_), channel_id=1, source_target_pairs={{0,7},{1,2},{2,1},{3,4},{4,3},{5,6},{6,5},{7,0},{8,15},{9,10},{10,... | collective-permute-start | bytes 98312 | tf_op jit(solution)/shard_map/ppermute | solution.py:300
  31.2 7.1 %encode.4 = (bf16[48,512]{1,0:T(8,128)(2,1)}, bf16[48,512]{1,0:T(8,128)(2,1)}, f32[48,512]{1,0:T(8,128)}) custom-call(bf16[128,512]{1,0:T(8,128)(2,1)} %refs_0_.6, s32[128,32]{1,0:T(8,128)} %get-tuple-element.31.refs_1_, f32[128,512]{1,0:T(8,128)} %get-tuple-element.32.refs_2_, bf16[512,512]{1,0:T(8,128)(2,1)} %get-tuple-element.33.refs_3_, ...), custom_call_target="tpu_custom_call" | custom-call | flops 3221225472 | bytes 6291456 | tf_op jit(solution)/shard_map/encode/pallas_call | solution.py:51
  38.5 7.3 %encode.5 = (bf16[48,512]{1,0:T(8,128)(2,1)}, bf16[48,512]{1,0:T(8,128)(2,1)}, f32[48,512]{1,0:T(8,128)}) custom-call(bf16[128,512]{1,0:T(8,128)(2,1)} %refs_0_.6, s32[128,32]{1,0:T(8,128)} %get-tuple-element.31.refs_1_, f32[128,512]{1,0:T(8,128)} %get-tuple-element.32.refs_2_, bf16[512,512]{1,0:T(8,128)(2,1)} %get-tuple-element.33.refs_3_, ...), custom_call_target="tpu_custom_call" | custom-call | flops 3221225472 | bytes 6291456 | tf_op jit(solution)/shard_map/encode/pallas_call | solution.py:51
  45.8 1.2 %collective-permute-start.11 = (bf16[16,512]{1,0:T(8,128)(2,1)S(1)}, bf16[16,512]{1,0:T(8,128)(2,1)S(1)}, u32[]{:S(2)}, u32[]{:S(2)}) collective-permute-start(bf16[16,512]{1,0:T(8,128)(2,1)S(1)} %pad_maximum_fusion.3), channel_id=1, source_target_pairs={{0,7},{1,6},{2,5},{3,4},{4,3},{5,2},{6,1},{7,0},{8,15},{9,14},{10,... | collective-permute-start | bytes 49160 | tf_op jit(solution)/shard_map/ppermute | solution.py:300
  47.0 1.6 %pad_maximum_fusion.refs_2_ = f32[96,512]{1,0:T(8,128)} fusion(f32[48,512]{1,0:T(8,128)} %get-tuple-element.48, f32[48,512]{1,0:T(8,128)S(1)} %copy-done.8), kind=kLoop, calls=%fused_computation | loop fusion | flops 49152 | bytes 393216 | tf_op jit(solution)/shard_map/concatenate | solution.py:389
  48.6 2.4 %collective-permute-done.11 = bf16[16,512]{1,0:T(8,128)(2,1)S(1)} collective-permute-done((bf16[16,512]{1,0:T(8,128)(2,1)S(1)}, bf16[16,512]{1,0:T(8,128)(2,1)S(1)}, u32[]{:S(2)}, u32[]{:S(2)}) %collective-permute-start.11) | collective-permute-done | bytes 16416 | tf_op jit(solution)/shard_map/ppermute | solution.py:300
  51.1 1.2 %collective-permute-start.12 = (bf16[128,512]{1,0:T(8,128)(2,1)S(1)}, bf16[128,512]{1,0:T(8,128)(2,1)S(1)}, u32[]{:S(2)}, u32[]{:S(2)}) collective-permute-start(bf16[128,512]{1,0:T(8,128)(2,1)S(1)} %concatenate.26), channel_id=1, source_target_pairs={{0,8},{1,9},{2,10},{3,11},{4,12},{5,13},{6,14},{7,15},{8,0},{9,1},... | collective-permute-start | bytes 393224 | tf_op jit(solution)/shard_map/ppermute | solution.py:300
  52.3 0.7 collective-permute-start.13
  53.1 1.7 %collective-permute-start.14 = (bf16[32,512]{1,0:T(8,128)(2,1)S(1)}, bf16[32,512]{1,0:T(8,128)(2,1)S(1)}, u32[]{:S(2)}, u32[]{:S(2)}) collective-permute-start(bf16[32,512]{1,0:T(8,128)(2,1)S(1)} %pad_maximum_fusion.2.refs_16_.refs_17_), channel_id=1, source_target_pairs={{0,16},{1,17},{2,18},{3,19},{4,20},{5,21},{6,22},{7,23},{8,24},{9,... | collective-permute-start | bytes 98312 | tf_op jit(solution)/shard_map/ppermute | solution.py:300
  54.7 1.4 %pad_maximum_fusion.1.refs_0_ = bf16[96,512]{1,0:T(8,128)(2,1)} fusion(bf16[48,512]{1,0:T(8,128)(2,1)} %get-tuple-element.46, bf16[48,512]{1,0:T(8,128)(2,1)S(1)} %copy-done.11), kind=kLoop, calls=%fused_computation.1 | loop fusion | flops 196608 | bytes 196608 | tf_op jit(solution)/shard_map/concatenate | solution.py:388
  56.2 1.4 %collective-permute-done.14.refs_17_.refs_18_ = bf16[32,512]{1,0:T(8,128)(2,1)S(1)} collective-permute-done((bf16[32,512]{1,0:T(8,128)(2,1)S(1)}, bf16[32,512]{1,0:T(8,128)(2,1)S(1)}, u32[]{:S(2)}, u32[]{:S(2)}) %collective-permute-start.14) | collective-permute-done | bytes 32800 | tf_op jit(solution)/shard_map/ppermute | solution.py:300
  57.6 2.1 %collective-permute-done.13.refs_15_.refs_16_ = bf16[128,512]{1,0:T(8,128)(2,1)S(1)} collective-permute-done((bf16[128,512]{1,0:T(8,128)(2,1)S(1)}, bf16[128,512]{1,0:T(8,128)(2,1)S(1)}, u32[]{:S(2)}, u32[]{:S(2)}) %collective-permute-start.13) | collective-permute-done | bytes 131104 | tf_op jit(solution)/shard_map/ppermute | solution.py:300
  59.8 0.6 copy-done.7
  60.4 4.8 %process.2 = (bf16[32,512]{1,0:T(8,128)(2,1)}, bf16[32,512]{1,0:T(8,128)(2,1)}) custom-call(bf16[32,512]{1,0:T(8,128)(2,1)} %get-tuple-element.36.refs_0_, s32[128,32]{1,0:T(8,128)} %get-tuple-element.37.refs_1_, f32[32,512]{1,0:T(8,128)} %get-tuple-element.38.refs_2_, bf16[512,512]{1,0:T(8,128)(2,1)} %get-tuple-element.39.refs_3_, f32[2,512]{1,0:T(2,128)} %refs_4_.10, ...), custom_call_target="tpu_custom_call" | custom-call | flops 1073741824 | bytes 6291456 | tf_op jit(solution)/shard_map/process/pallas_call | solution.py:51
  65.5 1.7 %collective-permute-start.16 = (bf16[32,512]{1,0:T(8,128)(2,1)}, bf16[32,512]{1,0:T(8,128)(2,1)S(1)}, u32[]{:S(2)}, u32[]{:S(2)}) collective-permute-start(bf16[32,512]{1,0:T(8,128)(2,1)} %get-tuple-element.44.refs_8_), channel_id=1, source_target_pairs={{0,7},{1,2},{2,1},{3,4},{4,3},{5,6},{6,5},{7,0},{8,15},{9,10},{10,... | collective-permute-start | bytes 98312 | tf_op jit(solution)/shard_map/ppermute | solution.py:300
  67.2 0.8 constant_dynamic-update-slice_fusion.2
  68.0 2.9 %collective-permute-done.16.refs_11_ = bf16[32,512]{1,0:T(8,128)(2,1)S(1)} collective-permute-done((bf16[32,512]{1,0:T(8,128)(2,1)}, bf16[32,512]{1,0:T(8,128)(2,1)S(1)}, u32[]{:S(2)}, u32[]{:S(2)}) %collective-permute-start.16) | collective-permute-done | bytes 32800 | tf_op jit(solution)/shard_map/ppermute | solution.py:300
  70.9 1.0 %collective-permute-start.17 = (bf16[96,512]{1,0:T(8,128)(2,1)S(1)}, bf16[96,512]{1,0:T(8,128)(2,1)S(1)}, u32[]{:S(2)}, u32[]{:S(2)}) collective-permute-start(bf16[96,512]{1,0:T(8,128)(2,1)S(1)} %constant_dynamic-update-slice_fusion), channel_id=1, source_target_pairs={{0,8},{1,9},{2,10},{3,11},{4,12},{5,13},{6,14},{7,15},{8,0},{9,1},... | collective-permute-start | bytes 294920 | tf_op jit(solution)/shard_map/ppermute | solution.py:300
  71.8 1.3 %collective-permute-start.18 = (bf16[96,512]{1,0:T(8,128)(2,1)S(1)}, bf16[96,512]{1,0:T(8,128)(2,1)S(1)}, u32[]{:S(2)}, u32[]{:S(2)}) collective-permute-start(bf16[96,512]{1,0:T(8,128)(2,1)S(1)} %constant_dynamic-update-slice_fusion), channel_id=1, source_target_pairs={{0,24},{1,25},{2,26},{3,27},{4,28},{5,29},{6,30},{7,31},{8,16},{9,... | collective-permute-start | bytes 294920 | tf_op jit(solution)/shard_map/ppermute | solution.py:300
  73.2 7.6 %process.3 = (bf16[128,512]{1,0:T(8,128)(2,1)}, bf16[96,512]{1,0:T(8,128)(2,1)}) custom-call(bf16[96,512]{1,0:T(8,128)(2,1)} %pad_maximum_fusion.1.refs_0_, s32[128,32]{1,0:T(8,128)} %get-tuple-element.37.refs_1_, f32[96,512]{1,0:T(8,128)} %pad_maximum_fusion.refs_2_, bf16[512,512]{1,0:T(8,128)(2,1)} %get-tuple-element.39.refs_3_, f32[2,512]{1,0:T(2,128)} %refs_4_.10, ...), custom_call_target="tpu_custom_call" | custom-call | flops 3221225472 | bytes 6291456 | tf_op jit(solution)/shard_map/process/pallas_call | solution.py:51
  81.5 8.2 %decode.1 = bf16[512,512]{1,0:T(8,128)(2,1)} custom-call(bf16[512,512]{1,0:T(8,128)(2,1)} %refs_0_.7, s32[512,8]{1,0:T(8,128)} %get-tuple-element.27.refs_1_, f32[512,512]{1,0:T(8,128)} %get-tuple-element.28.refs_2_, bf16[512,512]{1,0:T(8,128)(2,1)} %get-tuple-element.29.refs_3_, f32[2,512]{1,0:T(2,128)} %refs_4_.11, bf16[3,512,512]{2,1,0:T(8,128)(2,1)} %refs_5_.11, ...), custom_call_target="tpu_custom_call" | custom-call | flops 1409286144 | bytes 6291456 | tf_op jit(solution)/shard_map/decode/pallas_call | solution.py:51
  (67 shorter events, 1.8 us)
Async XLA Ops:
  2.7 7.3 %collective-permute-start.2 = (bf16[128,512]{1,0:T(8,128)(2,1)}, bf16[128,512]{1,0:T(8,128)(2,1)S(1)}, u32[]{:S(2)}, u32[]{:S(2)}) collective-permute-start(bf16[128,512]{1,0:T(8,128)(2,1)} %project_border.1), channel_id=1, source_target_pairs={{0,8},{1,9},{2,10},{3,11},{4,12},{5,13},{6,14},{7,15},{8,0},{9,1},... | collective-permute-start | bytes 393224 | tf_op jit(solution)/shard_map/ppermute | solution.py:300
  5.7 7.4 %collective-permute-start.1 = (bf16[128,512]{1,0:T(8,128)(2,1)}, bf16[128,512]{1,0:T(8,128)(2,1)S(1)}, u32[]{:S(2)}, u32[]{:S(2)}) collective-permute-start(bf16[128,512]{1,0:T(8,128)(2,1)} %project_border.1), channel_id=1, source_target_pairs={{0,7},{1,2},{2,1},{3,4},{4,3},{5,6},{6,5},{7,0},{8,15},{9,10},{10,... | collective-permute-start | bytes 393224 | tf_op jit(solution)/shard_map/ppermute | solution.py:300
  8.5 6.7 %collective-permute-start.5 = (bf16[128,512]{1,0:T(8,128)(2,1)}, bf16[128,512]{1,0:T(8,128)(2,1)S(1)}, u32[]{:S(2)}, u32[]{:S(2)}) collective-permute-start(bf16[128,512]{1,0:T(8,128)(2,1)} %project_border.1), channel_id=1, source_target_pairs={{0,24},{1,25},{2,26},{3,27},{4,28},{5,29},{6,30},{7,31},{8,16},{9,... | collective-permute-start | bytes 393224 | tf_op jit(solution)/shard_map/ppermute | solution.py:300
  10.0 11.2 %collective-permute-start = (bf16[128,512]{1,0:T(8,128)(2,1)}, bf16[128,512]{1,0:T(8,128)(2,1)S(1)}, u32[]{:S(2)}, u32[]{:S(2)}) collective-permute-start(bf16[128,512]{1,0:T(8,128)(2,1)} %project_border.1), channel_id=1, source_target_pairs={{0,1},{1,0},{2,3},{3,2},{4,5},{5,4},{6,7},{7,6},{8,9},{9,8},{10,11... | collective-permute-start | bytes 393224 | tf_op jit(solution)/shard_map/ppermute | solution.py:300
  10.0 11.2 %copy-start.13 = (bf16[128,512]{1,0:T(8,128)(2,1)}, bf16[128,512]{1,0:T(8,128)(2,1)S(1)}, u32[]{:S(2)}) copy-start(bf16[128,512]{1,0:T(8,128)(2,1)S(1)} %collective-permute-done.2.refs_13_) | copy-start | bytes 393220
  10.0 11.2 %collective-permute-start.3 = (bf16[128,512]{1,0:T(8,128)(2,1)S(1)}, bf16[128,512]{1,0:T(8,128)(2,1)S(1)}, u32[]{:S(2)}, u32[]{:S(2)}) collective-permute-start(bf16[128,512]{1,0:T(8,128)(2,1)S(1)} %collective-permute-done.2.refs_13_), channel_id=1, source_target_pairs={{0,1},{1,0},{2,3},{3,2},{4,5},{5,4},{6,7},{7,6},{8,9},{9,8},{10,11... | collective-permute-start | bytes 393224 | tf_op jit(solution)/shard_map/ppermute | solution.py:300
  13.1 8.0 %copy-start.14 = (bf16[128,512]{1,0:T(8,128)(2,1)}, bf16[128,512]{1,0:T(8,128)(2,1)S(1)}, u32[]{:S(2)}) copy-start(bf16[128,512]{1,0:T(8,128)(2,1)S(1)} %collective-permute-done.1.refs_12_) | copy-start | bytes 393220
  13.1 8.1 %collective-permute-start.4 = (bf16[128,512]{1,0:T(8,128)(2,1)S(1)}, bf16[128,512]{1,0:T(8,128)(2,1)S(1)}, u32[]{:S(2)}, u32[]{:S(2)}) collective-permute-start(bf16[128,512]{1,0:T(8,128)(2,1)S(1)} %collective-permute-done.1.refs_12_), channel_id=1, source_target_pairs={{0,8},{1,9},{2,10},{3,11},{4,12},{5,13},{6,14},{7,15},{8,0},{9,1},... | collective-permute-start | bytes 393224 | tf_op jit(solution)/shard_map/ppermute | solution.py:300
  15.1 6.0 %copy-start.15 = (bf16[128,512]{1,0:T(8,128)(2,1)}, bf16[128,512]{1,0:T(8,128)(2,1)S(1)}, u32[]{:S(2)}) copy-start(bf16[128,512]{1,0:T(8,128)(2,1)S(1)} %collective-permute-done.5.refs_16_) | copy-start | bytes 393220
  15.1 6.1 %collective-permute-start.6 = (bf16[128,512]{1,0:T(8,128)(2,1)S(1)}, bf16[128,512]{1,0:T(8,128)(2,1)S(1)}, u32[]{:S(2)}, u32[]{:S(2)}) collective-permute-start(bf16[128,512]{1,0:T(8,128)(2,1)S(1)} %collective-permute-done.5.refs_16_), channel_id=1, source_target_pairs={{0,1},{1,0},{2,3},{3,2},{4,5},{5,4},{6,7},{7,6},{8,9},{9,8},{10,11... | collective-permute-start | bytes 393224 | tf_op jit(solution)/shard_map/ppermute | solution.py:300
  15.1 6.8 %collective-permute-start.7 = (bf16[128,512]{1,0:T(8,128)(2,1)S(1)}, bf16[128,512]{1,0:T(8,128)(2,1)S(1)}, u32[]{:S(2)}, u32[]{:S(2)}) collective-permute-start(bf16[128,512]{1,0:T(8,128)(2,1)S(1)} %collective-permute-done.1.refs_12_), channel_id=1, source_target_pairs={{0,24},{1,25},{2,26},{3,27},{4,28},{5,29},{6,30},{7,31},{8,16},{9,... | collective-permute-start | bytes 393224 | tf_op jit(solution)/shard_map/ppermute | solution.py:300
  28.7 9.7 %copy-start = (bf16[32,512]{1,0:T(8,128)(2,1)S(1)}, bf16[32,512]{1,0:T(8,128)(2,1)}, u32[]{:S(2)}) copy-start(bf16[32,512]{1,0:T(8,128)(2,1)} %get-tuple-element.41.refs_9_.refs_10_) | copy-start | bytes 98308
  28.7 9.7 %collective-permute-start.8 = (bf16[32,512]{1,0:T(8,128)(2,1)}, bf16[32,512]{1,0:T(8,128)(2,1)S(1)}, u32[]{:S(2)}, u32[]{:S(2)}) collective-permute-start(bf16[32,512]{1,0:T(8,128)(2,1)} %get-tuple-element.41.refs_9_.refs_10_), channel_id=1, source_target_pairs={{0,1},{1,0},{2,3},{3,2},{4,5},{5,4},{6,7},{7,6},{8,9},{9,8},{10,11... | collective-permute-start | bytes 98312 | tf_op jit(solution)/shard_map/ppermute | solution.py:300
  28.8 19.9 %collective-permute-start.9 = (bf16[32,512]{1,0:T(8,128)(2,1)}, bf16[32,512]{1,0:T(8,128)(2,1)S(1)}, u32[]{:S(2)}, u32[]{:S(2)}) collective-permute-start(bf16[32,512]{1,0:T(8,128)(2,1)} %get-tuple-element.41.refs_9_.refs_10_), channel_id=1, source_target_pairs={{0,7},{1,2},{2,1},{3,4},{4,3},{5,6},{6,5},{7,0},{8,15},{9,10},{10,... | collective-permute-start | bytes 98312 | tf_op jit(solution)/shard_map/ppermute | solution.py:300
  38.4 12.7 %copy-start.1 = (bf16[32,512]{1,0:T(8,128)(2,1)}, bf16[32,512]{1,0:T(8,128)(2,1)S(1)}, u32[]{:S(2)}) copy-start(bf16[32,512]{1,0:T(8,128)(2,1)S(1)} %collective-permute-done.8.refs_12_.refs_13_) | copy-start | bytes 98308
  38.4 8.6 %copy-start.8 = (f32[48,512]{1,0:T(8,128)S(1)}, f32[48,512]{1,0:T(8,128)}, u32[]{:S(2)}) copy-start(f32[48,512]{1,0:T(8,128)} %get-tuple-element.47) | copy-start | bytes 294916
  38.4 16.3 %copy-start.11 = (bf16[48,512]{1,0:T(8,128)(2,1)S(1)}, bf16[48,512]{1,0:T(8,128)(2,1)}, u32[]{:S(2)}) copy-start(bf16[48,512]{1,0:T(8,128)(2,1)} %get-tuple-element.45) | copy-start | bytes 147460
  38.4 7.4 %collective-permute-start.10 = (bf16[8,512]{1,0:T(8,128)(2,1)S(1)}, bf16[8,512]{1,0:T(8,128)(2,1)S(1)}, u32[]{:S(2)}, u32[]{:S(2)}) collective-permute-start(bf16[8,512]{1,0:T(8,128)(2,1)S(1)} %pad_maximum_fusion.4), channel_id=1, source_target_pairs={{0,3},{1,2},{2,1},{3,0},{4,7},{5,6},{6,5},{7,4},{8,11},{9,10},{10,... | collective-permute-start | bytes 24584 | tf_op jit(solution)/shard_map/ppermute | solution.py:300
  45.8 5.3 %collective-permute-start.11 = (bf16[16,512]{1,0:T(8,128)(2,1)S(1)}, bf16[16,512]{1,0:T(8,128)(2,1)S(1)}, u32[]{:S(2)}, u32[]{:S(2)}) collective-permute-start(bf16[16,512]{1,0:T(8,128)(2,1)S(1)} %pad_maximum_fusion.3), channel_id=1, source_target_pairs={{0,7},{1,6},{2,5},{3,4},{4,3},{5,2},{6,1},{7,0},{8,15},{9,14},{10,... | collective-permute-start | bytes 49160 | tf_op jit(solution)/shard_map/ppermute | solution.py:300
  48.6 11.1 %copy-start.5 = (bf16[32,512]{1,0:T(8,128)(2,1)}, bf16[32,512]{1,0:T(8,128)(2,1)S(1)}, u32[]{:S(2)}) copy-start(bf16[32,512]{1,0:T(8,128)(2,1)S(1)} %collective-permute-done.9.refs_13_.refs_14_) | copy-start | bytes 98308
  51.1 6.5 %collective-permute-start.12 = (bf16[128,512]{1,0:T(8,128)(2,1)S(1)}, bf16[128,512]{1,0:T(8,128)(2,1)S(1)}, u32[]{:S(2)}, u32[]{:S(2)}) collective-permute-start(bf16[128,512]{1,0:T(8,128)(2,1)S(1)} %concatenate.26), channel_id=1, source_target_pairs={{0,8},{1,9},{2,10},{3,11},{4,12},{5,13},{6,14},{7,15},{8,0},{9,1},... | collective-permute-start | bytes 393224 | tf_op jit(solution)/shard_map/ppermute | solution.py:300
  52.3 7.4 %collective-permute-start.13 = (bf16[128,512]{1,0:T(8,128)(2,1)S(1)}, bf16[128,512]{1,0:T(8,128)(2,1)S(1)}, u32[]{:S(2)}, u32[]{:S(2)}) collective-permute-start(bf16[128,512]{1,0:T(8,128)(2,1)S(1)} %concatenate.26), channel_id=1, source_target_pairs={{0,24},{1,25},{2,26},{3,27},{4,28},{5,29},{6,30},{7,31},{8,16},{9,... | collective-permute-start | bytes 393224 | tf_op jit(solution)/shard_map/ppermute | solution.py:300
  53.0 6.7 %copy-start.2 = (bf16[32,512]{1,0:T(8,128)(2,1)}, bf16[32,512]{1,0:T(8,128)(2,1)S(1)}, u32[]{:S(2)}) copy-start(bf16[32,512]{1,0:T(8,128)(2,1)S(1)} %pad_maximum_fusion.2.refs_16_.refs_17_) | copy-start | bytes 98308
  53.1 4.6 %collective-permute-start.14 = (bf16[32,512]{1,0:T(8,128)(2,1)S(1)}, bf16[32,512]{1,0:T(8,128)(2,1)S(1)}, u32[]{:S(2)}, u32[]{:S(2)}) collective-permute-start(bf16[32,512]{1,0:T(8,128)(2,1)S(1)} %pad_maximum_fusion.2.refs_16_.refs_17_), channel_id=1, source_target_pairs={{0,16},{1,17},{2,18},{3,19},{4,20},{5,21},{6,22},{7,23},{8,24},{9,... | collective-permute-start | bytes 98312 | tf_op jit(solution)/shard_map/ppermute | solution.py:300
  57.6 2.1 %copy-start.12 = (bf16[32,512]{1,0:T(8,128)(2,1)}, bf16[32,512]{1,0:T(8,128)(2,1)S(1)}, u32[]{:S(2)}) copy-start(bf16[32,512]{1,0:T(8,128)(2,1)S(1)} %collective-permute-done.14.refs_17_.refs_18_) | copy-start | bytes 98308
  57.6 2.1 %copy-start.6 = (bf16[128,512]{1,0:T(8,128)(2,1)}, bf16[128,512]{1,0:T(8,128)(2,1)S(1)}, u32[]{:S(2)}) copy-start(bf16[128,512]{1,0:T(8,128)(2,1)S(1)} %collective-permute-done.12.refs_14_.refs_15_) | copy-start | bytes 393220
  65.2 2.8 %collective-permute-start.15 = (bf16[32,512]{1,0:T(8,128)(2,1)}, bf16[32,512]{1,0:T(8,128)(2,1)S(1)}, u32[]{:S(2)}, u32[]{:S(2)}) collective-permute-start(bf16[32,512]{1,0:T(8,128)(2,1)} %get-tuple-element.44.refs_8_), channel_id=1, source_target_pairs={{0,1},{1,0},{2,3},{3,2},{4,5},{5,4},{6,7},{7,6},{8,9},{9,8},{10,11... | collective-permute-start | bytes 98312 | tf_op jit(solution)/shard_map/ppermute | solution.py:300
  65.5 5.3 %collective-permute-start.16 = (bf16[32,512]{1,0:T(8,128)(2,1)}, bf16[32,512]{1,0:T(8,128)(2,1)S(1)}, u32[]{:S(2)}, u32[]{:S(2)}) collective-permute-start(bf16[32,512]{1,0:T(8,128)(2,1)} %get-tuple-element.44.refs_8_), channel_id=1, source_target_pairs={{0,7},{1,2},{2,1},{3,4},{4,3},{5,6},{6,5},{7,0},{8,15},{9,10},{10,... | collective-permute-start | bytes 98312 | tf_op jit(solution)/shard_map/ppermute | solution.py:300
  68.0 12.8 %copy-start.3 = (bf16[32,512]{1,0:T(8,128)(2,1)}, bf16[32,512]{1,0:T(8,128)(2,1)S(1)}, u32[]{:S(2)}) copy-start(bf16[32,512]{1,0:T(8,128)(2,1)S(1)} %collective-permute-done.15.refs_10_) | copy-start | bytes 98308
  70.8 9.9 %copy-start.4 = (bf16[32,512]{1,0:T(8,128)(2,1)}, bf16[32,512]{1,0:T(8,128)(2,1)S(1)}, u32[]{:S(2)}) copy-start(bf16[32,512]{1,0:T(8,128)(2,1)S(1)} %collective-permute-done.16.refs_11_) | copy-start | bytes 98308
  70.9 9.9 %collective-permute-start.17 = (bf16[96,512]{1,0:T(8,128)(2,1)S(1)}, bf16[96,512]{1,0:T(8,128)(2,1)S(1)}, u32[]{:S(2)}, u32[]{:S(2)}) collective-permute-start(bf16[96,512]{1,0:T(8,128)(2,1)S(1)} %constant_dynamic-update-slice_fusion), channel_id=1, source_target_pairs={{0,8},{1,9},{2,10},{3,11},{4,12},{5,13},{6,14},{7,15},{8,0},{9,1},... | collective-permute-start | bytes 294920 | tf_op jit(solution)/shard_map/ppermute | solution.py:300
  71.8 9.0 %collective-permute-start.18 = (bf16[96,512]{1,0:T(8,128)(2,1)S(1)}, bf16[96,512]{1,0:T(8,128)(2,1)S(1)}, u32[]{:S(2)}, u32[]{:S(2)}) collective-permute-start(bf16[96,512]{1,0:T(8,128)(2,1)S(1)} %constant_dynamic-update-slice_fusion), channel_id=1, source_target_pairs={{0,24},{1,25},{2,26},{3,27},{4,28},{5,29},{6,30},{7,31},{8,16},{9,... | collective-permute-start | bytes 294920 | tf_op jit(solution)/shard_map/ppermute | solution.py:300
  (8 other events, 5.6 us)

commit v2 on v1

v2 whole, which is shorter than its diff:
```python
import functools

import jax
import jax.numpy as jnp
from jax import lax
from jax.experimental import pallas as pl
from jax.experimental.pallas import tpu as pltpu
from jax.sharding import PartitionSpec as P

AXES = ("gx", "gy")
CM = 4
EPS = 1e-05
BF = jnp.bfloat16
F32 = jnp.float32
I32 = jnp.int32
SDS = jax.ShapeDtypeStruct


def mm(a, b):
    return jnp.dot(a, b, preferred_element_type=F32)


def half_silu(half):
    return (half + half * jnp.tanh(half)).astype(BF)


def inverse_norm(centred):
    spread = jnp.mean(centred * centred, axis=-1, keepdims=True)
    return lax.rsqrt(spread + EPS)


def centre(w):
    w = w.astype(F32)
    return (w - jnp.mean(w, axis=-1, keepdims=True)).astype(BF)


class Mover:
    def __init__(self, sems):
        self.sems = sems
        self.used = 0

    def start(self, source, target):
        copy = pltpu.make_async_copy(source, target, self.sems.at[self.used])
        self.used += 1
        copy.start()
        return copy


def launch(body, name, ins, outs, scratch, copies, flops, nbytes, far_ins=(), far_outs=(), mib=10):
    near = pl.BlockSpec(memory_space=pltpu.VMEM)
    far = pl.BlockSpec(memory_space=pltpu.HBM)
    sems = [pltpu.SemaphoreType.DMA((copies,))] if copies else []
    ins = [pltpu.with_memory_space_constraint(x, pltpu.HBM) if i in far_ins else x for i, x in enumerate(ins)]
    return pl.pallas_call(
        body,
        out_shape=outs,
        in_specs=[far if i in far_ins else near for i in range(len(ins))],
        out_specs=[far if i in far_outs else near for i in range(len(outs))],
        scratch_shapes=[pltpu.VMEM(s, d) for s, d in scratch] + sems,
        compiler_params=pltpu.CompilerParams(vmem_limit_bytes=mib << 20),
        cost_estimate=pl.CostEstimate(flops=flops, bytes_accessed=nbytes, transcendentals=0),
        name=name,
    )(*ins)


def glue(*parts):
    width = parts[0][0].shape[1]
    total = sum(rows for _, rows in parts)

    def body(*refs):
        out = refs[-1]
        if any(rows % 16 for _, rows in parts):
            values = [ref[pl.ds(0, rows), :].astype(F32) for ref, (_, rows) in zip(refs, parts)]
            out[...] = jnp.concatenate(values, axis=0).astype(BF)
        else:
            start = 0
            for ref, (_, rows) in zip(refs, parts):
                out[pl.ds(start, rows), :] = ref[pl.ds(0, rows), :]
                start += rows

    return launch(body, "glue", [x for x, _ in parts], [SDS((total, width), BF)], [], 0, 1 << 10, 1 << 18, mib=2)[0]


def border_kernel(x, w, out, x_v, w_v, sems):
    mover = Mover(sems)
    quarter = w_v.shape[0] // 4
    loads = [mover.start(x.at[pl.ds(0, x_v.shape[0])], x_v)]
    for i in range(4):
        part = pl.ds(i * quarter, quarter)
        loads.append(mover.start(w.at[0, part], w_v.at[part]))
    for load in loads:
        load.wait()
    out[...] = (mm(x_v[...], w_v[...]) * 0.5).astype(BF)


def split(value, by):
    if by & (by - 1) == 0:
        return value >> (by.bit_length() - 1), value & (by - 1)
    return value // by, value % by


def locate(ids, rows, border, coarse, sizes, places, early=False):
    size_x, size_y = sizes
    place_x, place_y = places
    owner, offset = split(jnp.maximum(ids, 0), rows)
    owner_x, owner_y = split(owner, size_y)
    step_x = owner_x - place_x
    step_x = jnp.where(step_x < 0, step_x + size_x, step_x)
    step_y = owner_y - place_y
    step_y = jnp.where(step_y < 0, step_y + size_y, step_y)
    ahead_x, ahead_y = (place_x & 1) == 0, (place_y & 1) == 0
    pair_x = jnp.where(ahead_x, 1, size_x - 1)
    pair_y = jnp.where(ahead_y, 1, size_y - 1)
    kind_x = jnp.where(step_x == 0, 0, jnp.where(step_x == pair_x, 1, 2))
    kind_y = jnp.where(step_y == 0, 0, jnp.where(step_y == pair_y, 1, 2))
    near_x = (step_x <= 1) | (step_x == size_x - 1)
    near_y = (step_y <= 1) | (step_y == size_y - 1)
    group = 3 * border + coarse * size_y
    first = jnp.where(kind_x == 0, rows - border, rows + 2 * border + (kind_x - 1) * group)
    found = first + kind_y * border + offset
    if early:
        slot = jnp.where(kind_x == 0, kind_y - 1, jnp.where(kind_y == 0, kind_x + 1, 2 * kind_x + kind_y + 1))
        found = rows + slot * border + offset
    if coarse:
        flip = owner_y ^ place_y
        column = jnp.where(kind_x == 0, 0, 3 * border)
        far = first + column
        tail = rows + 2 * border + 2 * group
        far = jnp.where(kind_x == 0, tail, far)
        far = jnp.where(near_x, far, tail + (step_x - 1) * coarse * size_y)
        far = far + (flip ^ (flip >> 1)) * coarse + offset
        nearby = near_x & near_y & (offset < border)
        found = jnp.where(nearby, found, far)
    found = jnp.where((step_x == 0) & (step_y == 0), offset, found)
    return jnp.where(ids >= 0, found, -1)


def turned(found):
    degree, count = found.shape
    pad = -degree % 8
    if pad:
        found = jnp.concatenate([found, jnp.full((pad, count), -1, I32)], axis=0)
    return found.astype(F32).T.astype(I32)


def prepare_kernel(
    sizes, shapes,
    grid, mesh, eids, mids, dids, ee, en, pe, pn, de, dn, eb, db,
    grid_o, mesh_o, own, ebase, dbase, eat, mat, dat, ee2, en2, pe2, pn2, de2, dn2, en01, pe01, pn01, de01, dn01,
    eids_v, mids_v, dids_v, w0_v, w1_v, eb_v, db_v, w2_v, sems,
):
    mover = Mover(sems)
    grid_rows, mesh_rows, grid_border, mesh_border = shapes
    heads = [
        mover.start(a, b)
        for a, b in (
            (eids, eids_v), (mids, mids_v), (dids, dids_v), (grid, grid_o), (mesh, mesh_o),
            (ee.at[0], w0_v), (ee.at[1], w1_v), (eb, eb_v), (db, db_v),
        )
    ]
    seconds = [mover.start(w.at[2], w2_v.at[i]) for i, w in enumerate((ee, en, pe, pn, de, dn))]
    pairs = [
        mover.start(w.at[pl.ds(0, 2)], out)
        for w, out in ((en, en01), (pe, pe01), (de, de01), (pn, pn01), (dn, dn01))
    ]
    for head in heads:
        head.wait()
    places = (lax.axis_index("gx"), lax.axis_index("gy"))
    eat[...] = turned(locate(eids_v[...], grid_rows, grid_border, 0, sizes, places, True))
    own[...] = (mm(grid_o[...], w0_v[...]) * 0.5).astype(BF)
    ebase[...] = (mm(mesh_o[...], w1_v[...]) + eb_v[0:1, :]) * 0.5
    mat[...] = turned(locate(mids_v[...], mesh_rows, mesh_border, CM, sizes, places))
    dat[...] = turned(locate(dids_v[...], mesh_rows, mesh_border, 0, sizes, places))
    for i, (second, out) in enumerate(zip(seconds, (ee2, en2, pe2, pn2, de2, dn2))):
        second.wait()
        out[...] = centre(w2_v[i])
    for pair in pairs:
        pair.wait()
    dbase[...] = (mm(grid_o[...], de01[1]) + db_v[0:1, :]) * 0.5


def chosen(places, ks, lanes):
    return jnp.concatenate([(places[:, k : k + 1] == lanes).astype(F32).astype(BF) for k in ks], axis=0)


def edge_sum(places, degree, table, base, w2, vectors, slots, lift=0, begun=None):
    rows, width = base.shape
    lanes = lift + lax.broadcasted_iota(I32, (rows, table.shape[0]), 1)
    groups = [range(k, min(k + slots, degree)) for k in range(0, degree, slots)]

    def gather(ks):
        half = mm(chosen(places, ks, lanes), table[...])
        if begun is not None:
            ref, start = begun
            half = half + ref[pl.ds(start + ks[0] * rows, len(ks) * rows), :].astype(F32)
        return half.reshape(len(ks), rows, width) + base[None]

    total = jnp.zeros((rows, width), F32)
    ahead = gather(groups[0])
    for i, ks in enumerate(groups):
        half = ahead
        if i + 1 < len(groups):
            ahead = gather(groups[i + 1])
        y = mm(half_silu(half.reshape(len(ks) * rows, width)), w2)
        scale = inverse_norm(y).reshape(len(ks), rows, 1)
        y = y.reshape(len(ks), rows, width)
        for j, k in enumerate(ks):
            live = (places[:, k : k + 1] >= 0).astype(F32)
            total = total + y[j] * (scale[j] * live)
    return total * (1.0 + vectors[1:2, :])


def begin(places, pieces, block, slots):
    count, degree = places.shape
    width = pieces[0].shape[1]
    table_rows = sum(p.shape[0] for p in pieces)

    def body(places, *refs):
        *pieces_in, out, table = refs
        lay(pieces_in, table)
        lanes = lax.broadcasted_iota(I32, (block, table_rows), 1)
        for at in range(0, count, block):
            near = places[pl.ds(at, block), :]
            for k in range(0, degree, slots):
                ks = range(k, min(k + slots, degree))
                picked = mm(chosen(near, ks, lanes), table[...])
                out[pl.ds(at * degree + k * block, len(ks) * block), :] = picked.astype(BF)

    return launch(
        body, "begin", [places] + pieces, [SDS((count * degree, width), BF)], [((table_rows, width), BF)], 0,
        2 * count * degree * table_rows * width, 4 << 20,
    )[0]


def lay(pieces, table):
    start = 0
    for piece in pieces:
        table[pl.ds(start, piece.shape[0]), :] = piece[...]
        start += piece.shape[0]


def node_update(x, summed, w0, w1, w2, vectors):
    half = (mm(x, w0) + mm(summed.astype(BF), w1) + vectors[0:1, :]) * 0.5
    y = mm(half_silu(half), w2)
    return (x.astype(F32) + y * inverse_norm(y) * (1.0 + vectors[1:2, :])).astype(BF)


def rows_of(refs, at, count):
    picked = []
    start = 0
    for ref in refs:
        low, high = max(at - start, 0), min(at + count - start, ref.shape[0])
        if low < high:
            picked.append(ref[pl.ds(low, high - low), :])
        start += ref.shape[0]
    return picked[0] if len(picked) == 1 else jnp.concatenate(picked, axis=0)


def mesh_stage(xs, places, base_place, at, count, pieces, keep, bases, ew2, ev, nw, nw2, nv, following, fv, joined, steps, name, lift=0, begun=None):
    width = xs[0].shape[1]
    degree = places.shape[1]
    table_rows = sum(p.shape[0] for p in pieces)
    groups = [xs, bases, pieces, [places, ew2, ev, nw, nw2, nv, following], [] if fv is None else [fv], joined, [] if begun is None else [begun]]
    ins = [x for group in groups for x in group]
    rows_out = count + sum(x.shape[0] for x in joined)
    outs = [SDS((rows_out, width), BF), SDS((count, width), BF)]
    outs += [] if fv is None else [SDS((count, width), F32)]
    outs += [SDS((table_rows, width), BF)] if keep else []

    def body(*refs):
        refs = list(refs)
        taken = []
        for group in groups:
            taken.append(refs[: len(group)])
            refs = refs[len(group) :]
        xs, bases, pieces_in, (places, ew2, ev, nw, nw2, nv, follow), fv, joined_in, begun_in = taken
        table = pieces_in[0]
        if keep:
            table = refs[-1]
            lay(pieces_in, table)
        summed = edge_sum(places[pl.ds(base_place + at, count), :], degree, table, rows_of(bases, at, count), ew2[...], ev, steps, lift, *[(ref, at * degree) for ref in begun_in])
        new = node_update(rows_of(xs, at, count), summed, nw[0], nw[1], nw2[...], nv)
        refs[0][pl.ds(rows_out - count, count), :] = new
        start = 0
        for ref in joined_in:
            refs[0][pl.ds(start, ref.shape[0]), :] = ref[...]
            start += ref.shape[0]
        refs[1][...] = (mm(new, follow[0]) * 0.5).astype(BF)
        for ref in fv:
            refs[2][...] = (mm(new, follow[1]) + ref[0:1, :]) * 0.5

    flops = count * degree * (2 * width * table_rows + 2 * width * width)
    return launch(body, name, ins, outs, [], 0, flops, 6 << 20)


def decode_stage(x, places, degree, pieces, base, ew2, ev, nw, nw2, nv, block):
    rows, width = x.shape
    table_rows = sum(p.shape[0] for p in pieces)
    ins = [x, places, base, ew2, ev, nw, nw2, nv] + pieces
    outs = [SDS((rows, width), BF)]

    def body(*refs):
        refs = list(refs)
        x, places, base, ew2, ev, nw, nw2, nv = refs[:8]
        pieces_in = refs[8 : 8 + len(pieces)]
        out, table, new, sems = refs[8 + len(pieces) :]
        mover = Mover(sems)
        lay(pieces_in, table)
        tails = []
        for at in range(0, rows, block):
            part = pl.ds(at, block)
            summed = edge_sum(places[part, :], degree, table, base[part, :], ew2[...], ev, degree)
            new[part, :] = node_update(x[part, :], summed, nw[0], nw[1], nw2[...], nv)
            tails.append(mover.start(new.at[part], out.at[part]))
        for tail in tails:
            tail.wait()

    flops = rows * degree * (2 * width * table_rows + 2 * width * width)
    scratch = [((table_rows, width), BF), ((rows, width), BF)]
    return launch(body, "decode", ins, outs, scratch, rows // block, flops, 6 << 20, far_outs=(0,))[0]


def sender(size_x, size_y):
    def send(rows, move):
        pairs = []
        for i in range(size_x):
            for j in range(size_y):
                a, b = move(i, j)
                pairs.append((i * size_y + j, (a % size_x) * size_y + b % size_y))
        return lax.ppermute(rows, AXES, pairs)

    return send


def next_pair(i):
    return i + 1 if i % 2 else i - 1


def per_device(
    grid_latent, mesh_latent, encode_senders, mesh_senders, decode_senders,
    encoder_edges, encoder_edgebias, encoder_nodes, encoder_nodebias,
    process_edges, process_edgebias, process_nodes, process_nodebias,
    decoder_edges, decoder_edgebias, decoder_nodes, decoder_nodebias,
):
    grid_rows, width = grid_latent.shape
    mesh_rows = mesh_latent.shape[0]
    grid_border = grid_rows // 4
    mesh_border = mesh_rows // 4
    size_x = lax.axis_size("gx")
    size_y = lax.axis_size("gy")
    square = 2 * width * width
    send = sender(size_x, size_y)
    pair_x = lambda i, j: (i ^ 1, j)
    next_x = lambda i, j: (next_pair(i), j)
    pair_y = lambda i, j: (i, j ^ 1)
    next_y = lambda i, j: (i, next_pair(j))

    border = launch(
        border_kernel, "project_border", [grid_latent, encoder_edges], [SDS((grid_border, width), BF)],
        [((grid_border, width), BF), ((width, width), BF)], 5, grid_border * square, 1 << 20, far_ins=(0, 1),
    )[0]
    e = send(border, pair_x)
    o = send(border, next_x)
    z = send(border, next_y)
    c = send(border, pair_y)

    degrees = [ids.shape[0] + -ids.shape[0] % 8 for ids in (encode_senders, mesh_senders, decode_senders)]
    square_shape = ((width, width), BF)
    outs = [
        ((grid_rows, width), BF), ((mesh_rows, width), BF), ((grid_rows, width), BF),
        ((mesh_rows, width), F32), ((grid_rows, width), F32),
        ((mesh_rows, degrees[0]), I32), ((mesh_rows, degrees[1]), I32), ((grid_rows, degrees[2]), I32),
    ] + [square_shape] * 6 + [((2, width, width), BF)] * 5
    (
        grid_latent, mesh_latent, own, base, grid_base, encode_at, mesh_at, decode_at,
        ee2, en2, pe2, pn2, de2, dn2, en01, pe01, pn01, de01, dn01,
    ) = launch(
        functools.partial(prepare_kernel, (size_x, size_y), (grid_rows, mesh_rows, grid_border, mesh_border)), "prepare",
        [
            grid_latent, mesh_latent, encode_senders, mesh_senders, decode_senders, encoder_edges, encoder_nodes,
            process_edges, process_nodes, decoder_edges, decoder_nodes, encoder_edgebias, decoder_edgebias,
        ],
        [SDS(s, d) for s, d in outs],
        [
            (encode_senders.shape, I32), (mesh_senders.shape, I32), (decode_senders.shape, I32), square_shape, square_shape,
            ((2, width), F32), ((2, width), F32), ((6, width, width), BF),
        ],
        20, 2 * grid_rows * square, 12 << 20, far_ins=range(13), mib=16,
    )
    e, o, z, own = lax.optimization_barrier((e, o, z, own))
    ec = send(e, pair_y)
    oc = send(o, pair_y)
    ez = send(z, pair_x)
    oz = send(z, next_x)
    begun = begin(encode_at, [own, c, z, e, o], mesh_border, 8)
    lift = grid_rows + 4 * grid_border
    pieces = [ec, ez, oc, oz]

    cuts = list(range(0, mesh_rows + 1, mesh_border))
    encoded = []
    for at, end in zip(cuts, cuts[1:]):
        part = mesh_stage(
            [mesh_latent], encode_at, 0, at, end - at, pieces, at == 0, [base], ee2, encoder_edgebias, en01, en2,
            encoder_nodebias, pe01, process_edgebias, [], 8, "encode", lift, begun,
        )
        if at == 0:
            pieces = [part[3]]
        encoded.append(part)

    border = encoded[0][1]
    c = send(border, pair_y)
    z = send(border, next_y)
    column = glue((border, CM), (c, CM))
    step = 2
    while step < size_y:
        flip = 2 * step - 1
        other = send(column, lambda i, j, flip=flip: (i, j ^ flip))
        column = glue((column, CM * step), (other, CM * step))
        step *= 2
    stack = glue((border, mesh_border), (c, mesh_border), (z, mesh_border), (column, CM * size_y))
    e = send(stack, pair_x)
    o = send(stack, next_x)
    far = [send(column, lambda i, j, d=d: (i - d, j)) for d in range(2, size_x - 1)]
    pieces = [part[1] for part in encoded] + [c, z, e, o, column] + far

    first = mesh_stage(
        [encoded[0][0]], mesh_at, 0, 0, mesh_border, pieces, True, [encoded[0][2]], pe2, process_edgebias, pn01, pn2,
        process_nodebias, de01, None, [], 8, "process",
    )
    border = first[1]
    c = send(border, pair_y)
    z = send(border, next_y)
    half = (mesh_rows - mesh_border) // 2
    xs, bases = ([part[i] for part in encoded[1:]] for i in (0, 2))
    tables, joined = [first[2]], [first[0]]
    projected = [border]
    for at in (0, half):
        part = mesh_stage(
            xs, mesh_at, mesh_border, at, half, tables, False, bases, pe2, process_edgebias, pn01, pn2, process_nodebias, de01, None,
            joined if at else [], 4, "process",
        )
        joined.append(part[0])
        projected.append(part[1])
        if at == 0:
            c, z, joined[-1] = lax.optimization_barrier((c, z, joined[-1]))
    processed = joined[-1]
    stack = glue((border, mesh_border), (c, mesh_border), (z, mesh_border))
    e = send(stack, pair_x)
    o = send(stack, next_x)
    decoded = decode_stage(
        grid_latent, decode_at, decode_senders.shape[0], projected + [c, z, e, o], grid_base, de2, decoder_edgebias,
        dn01, dn2, decoder_nodebias, 128,
    )
    return (decoded, processed)


def solution(mesh):
    rows = P(AXES, None)
    senders = P(None, AXES)
    return jax.shard_map(
        per_device,
        mesh=mesh,
        in_specs=(rows, rows, senders, senders, senders) + (P(),) * 12,
        out_specs=(rows, rows),
        check_vma=False,
    )
```

time: 90.2 us -> 65.3 us (0.72)
  Pallas kernels: 47.8 us -> 35.5 us
  waiting for transfers between devices: 14.2 us -> 8.04 us
  other arithmetic: 3.05 us -> 0 us
  local copies, waits for them, and re-layouts: 2.81 us -> 0.03 us
    pallas_call x8 -> x16, Pallas kernels: 47.8 us -> 35.5 us  [launch(): pl.pallas_call(body, out_shape=outs, in_specs=[far if i in far_ins else n...]
    ppermute x19, waiting for transfers between devices: 14.2 us -> 8.04 us  [send(): return lax.ppermute(rows, AXES, pairs)]
    concatenate x5 -> x0, other arithmetic: 3.05 us -> none  [the longest x1 1.58 us: per_device(): base = jnp.concatenate([part[2] for part in encoded[1:]], axis=0)]
    unnamed x44 -> x12, local copies, waits for them, and re-layouts: 2.76 us -> 0.03 us
  transfers between devices with their start and end apart: 19 -> 19, of which waited for: 7 -> 8; matrix products, arithmetic and copies ran while one was open for 4% -> 0% of each run, Pallas kernels for 30% -> 36%
where the time goes in v2:
time: 65.3 us; the launch traced here: 65 us
  Pallas kernels  35.5 us (54%)
  starting transfers between devices  20.5 us (31%)
  waiting for transfers between devices  8.04 us (12%)
  between operations  0.95 us (1%)
    pallas_call x16, Pallas kernels, launch(): pl.pallas_call(body, out_shape=outs, in_specs=[far if i in far_ins else n...  35.5 us
    ppermute x19, starting transfers between devices, send(): return lax.ppermute(rows, AXES, pairs)  20.5 us
    ppermute x19, waiting for transfers between devices, send(): return lax.ppermute(rows, AXES, pairs)  8.04 us
  transfers between devices with their start and end apart: 19, of which 8 were waited for; matrix products, arithmetic and copies ran while one was open for 0% of the time, Pallas kernels for 36%

profile of v2, /device:TPU:0, one launch (start us, length us, event | category | flops | bytes accessed | tf_op | source)
XLA Modules:
  0.0 65.0 jit_solution(12177355092959735108)
XLA Ops:
  0.6 1.4 %project_border.1 = bf16[128,512]{1,0:T(8,128)(2,1)S(1)} custom-call(bf16[512,512]{1,0:T(8,128)(2,1)} %x.1, bf16[3,512,512]{2,1,0:T(8,128)(2,1)} %w.1), custom_call_target="tpu_custom_call" | custom-call | flops 67108864 | bytes 1048576 | tf_op jit(solution)/shard_map/project_border/pallas_call | solution.py:54
  2.1 3.0 %collective-permute-start = (bf16[128,512]{1,0:T(8,128)(2,1)S(1)}, bf16[128,512]{1,0:T(8,128)(2,1)S(1)}, u32[]{:S(2)}, u32[]{:S(2)}) collective-permute-start(bf16[128,512]{1,0:T(8,128)(2,1)S(1)} %project_border.1), channel_id=1, source_target_pairs={{0,8},{1,9},{2,10},{3,11},{4,12},{5,13},{6,14},{7,15},{8,0},{9,1},... | collective-permute-start | bytes 393224 | tf_op jit(solution)/shard_map/ppermute | solution.py:330
  5.1 1.5 %collective-permute-start.1 = (bf16[128,512]{1,0:T(8,128)(2,1)S(1)}, bf16[128,512]{1,0:T(8,128)(2,1)S(1)}, u32[]{:S(2)}, u32[]{:S(2)}) collective-permute-start(bf16[128,512]{1,0:T(8,128)(2,1)S(1)} %project_border.1), channel_id=1, source_target_pairs={{0,24},{1,25},{2,26},{3,27},{4,28},{5,29},{6,30},{7,31},{8,16},{9,... | collective-permute-start | bytes 393224 | tf_op jit(solution)/shard_map/ppermute | solution.py:330
  6.6 2.5 %collective-permute-start.2 = (bf16[128,512]{1,0:T(8,128)(2,1)S(1)}, bf16[128,512]{1,0:T(8,128)(2,1)S(1)}, u32[]{:S(2)}, u32[]{:S(2)}) collective-permute-start(bf16[128,512]{1,0:T(8,128)(2,1)S(1)} %project_border.1), channel_id=1, source_target_pairs={{0,7},{1,2},{2,1},{3,4},{4,3},{5,6},{6,5},{7,0},{8,15},{9,10},{10,... | collective-permute-start | bytes 393224 | tf_op jit(solution)/shard_map/ppermute | solution.py:330
  9.1 4.6 %prepare.1 = (bf16[512,512]{1,0:T(8,128)(2,1)S(1)}, bf16[128,512]{1,0:T(8,128)(2,1)S(1)}, bf16[512,512]{1,0:T(8,128)(2,1)S(1)}, f32[128,512]{1,0:T(8,128)S(1)}, ...) custom-call(bf16[512,512]{1,0:T(8,128)(2,1)} %x.1, ...), custom_call_target="tpu_custom_call" | custom-call | flops 536870912 | bytes 12582912 | tf_op jit(solution)/shard_map/prepare/pallas_call | solution.py:54
  13.8 1.5 %collective-permute-start.4 = (bf16[128,512]{1,0:T(8,128)(2,1)S(1)}, bf16[128,512]{1,0:T(8,128)(2,1)S(1)}, u32[]{:S(2)}, u32[]{:S(2)}) collective-permute-start(bf16[128,512]{1,0:T(8,128)(2,1)S(1)} %collective-permute-done.2.refs_2_), channel_id=1, source_target_pairs={{0,8},{1,9},{2,10},{3,11},{4,12},{5,13},{6,14},{7,15},{8,0},{9,1},... | collective-permute-start | bytes 393224 | tf_op jit(solution)/shard_map/ppermute | solution.py:330
  15.3 0.4 collective-permute-start.6
  15.7 0.5 collective-permute-start.5
  16.3 4.6 %begin.1.refs_14_.refs_11_ = bf16[4096,512]{1,0:T(8,128)(2,1)S(1)} custom-call(s32[128,32]{1,0:T(8,128)S(1)} %get-tuple-element.60.places.refs_6_.refs_3_, bf16[512,512]{1,0:T(8,128)(2,1)S(1)} %get-tuple-element.65.refs_0_, bf16[128,512]{1,0:T(8,128)(2,1)S(1)} %collective-permute-done.7.refs_1_, bf16[128,512]{1,0:T(8,128)(2,1)S(1)} %collective-permute-done.2.refs_2_, ...), custom_call_target="tpu_custom_call" | custom-call | flops 4294967296 | bytes 4194304 | tf_op jit(solution)/shard_map/begin/pallas_call | solution.py:54
  20.8 1.6 %collective-permute-done.6.refs_5_ = bf16[128,512]{1,0:T(8,128)(2,1)S(1)} collective-permute-done((bf16[128,512]{1,0:T(8,128)(2,1)S(1)}, bf16[128,512]{1,0:T(8,128)(2,1)S(1)}, u32[]{:S(2)}, u32[]{:S(2)}) %collective-permute-start.6) | collective-permute-done | bytes 131104 | tf_op jit(solution)/shard_map/ppermute | solution.py:330
  22.5 2.5 %encode.4 = (bf16[32,512]{1,0:T(8,128)(2,1)S(1)}, bf16[32,512]{1,0:T(8,128)(2,1)S(1)}, f32[32,512]{1,0:T(8,128)S(1)}, bf16[512,512]{1,0:T(8,128)(2,1)S(1)}) custom-call(bf16[128,512]{1,0:T(8,128)(2,1)S(1)} %get-tuple-element.54.refs_0_, f32[128,512]{1,0:T(8,128)S(1)} %get-tuple-element.55.refs_1_, bf16[128,512]{1,0:T(8,128)(2,1)S(1)} %collective-permute-done.3.refs_2_, ...), custom_call_target="tpu_custom_call" | custom-call | flops 1073741824 | bytes 6291456 | tf_op jit(solution)/shard_map/encode/pallas_call | solution.py:54
  25.0 1.2 %collective-permute-done.8.refs_1_.refs_6_ = bf16[32,512]{1,0:T(8,128)(2,1)S(1)} collective-permute-done((bf16[32,512]{1,0:T(8,128)(2,1)S(1)}, bf16[32,512]{1,0:T(8,128)(2,1)S(1)}, u32[]{:S(2)}, u32[]{:S(2)}) %collective-permute-start.8) | collective-permute-done | bytes 32800 | tf_op jit(solution)/shard_map/ppermute | solution.py:330
  26.3 2.4 %collective-permute-start.9 = (bf16[32,512]{1,0:T(8,128)(2,1)S(1)}, bf16[32,512]{1,0:T(8,128)(2,1)S(1)}, u32[]{:S(2)}, u32[]{:S(2)}) collective-permute-start(bf16[32,512]{1,0:T(8,128)(2,1)S(1)} %get-tuple-element.68.refs_0_.refs_2_), channel_id=1, source_target_pairs={{0,7},{1,2},{2,1},{3,4},{4,3},{5,6},{6,5},{7,0},{8,15},{9,10},{10,... | collective-permute-start | bytes 98312 | tf_op jit(solution)/shard_map/ppermute | solution.py:330
  28.7 0.6 collective-permute-done.10.refs_1_
  29.3 1.3 %collective-permute-start.11 = (bf16[16,512]{1,0:T(8,128)(2,1)S(1)}, bf16[16,512]{1,0:T(8,128)(2,1)S(1)}, u32[]{:S(2)}, u32[]{:S(2)}) collective-permute-start(bf16[16,512]{1,0:T(8,128)(2,1)S(1)} %glue.6.refs_0_), channel_id=1, source_target_pairs={{0,7},{1,6},{2,5},{3,4},{4,3},{5,2},{6,1},{7,0},{8,15},{9,14},{10,... | collective-permute-start | bytes 49160 | tf_op jit(solution)/shard_map/ppermute | solution.py:330
  30.6 2.5 %encode.7 = (bf16[32,512]{1,0:T(8,128)(2,1)S(1)}, bf16[32,512]{1,0:T(8,128)(2,1)S(1)}, f32[32,512]{1,0:T(8,128)S(1)}) custom-call(bf16[128,512]{1,0:T(8,128)(2,1)S(1)} %get-tuple-element.54.refs_0_, f32[128,512]{1,0:T(8,128)S(1)} %get-tuple-element.55.refs_1_, bf16[512,512]{1,0:T(8,128)(2,1)S(1)} %get-tuple-element.69.refs_2_, ...), custom_call_target="tpu_custom_call" | custom-call | flops 1073741824 | bytes 6291456 | tf_op jit(solution)/shard_map/encode/pallas_call | solution.py:54
  33.1 1.1 %collective-permute-done.11.refs_1_ = bf16[16,512]{1,0:T(8,128)(2,1)S(1)} collective-permute-done((bf16[16,512]{1,0:T(8,128)(2,1)S(1)}, bf16[16,512]{1,0:T(8,128)(2,1)S(1)}, u32[]{:S(2)}, u32[]{:S(2)}) %collective-permute-start.11) | collective-permute-done | bytes 16416 | tf_op jit(solution)/shard_map/ppermute | solution.py:330
  34.3 1.6 %collective-permute-start.12 = (bf16[128,512]{1,0:T(8,128)(2,1)S(1)}, bf16[128,512]{1,0:T(8,128)(2,1)S(1)}, u32[]{:S(2)}, u32[]{:S(2)}) collective-permute-start(bf16[128,512]{1,0:T(8,128)(2,1)S(1)} %glue.8), channel_id=1, source_target_pairs={{0,8},{1,9},{2,10},{3,11},{4,12},{5,13},{6,14},{7,15},{8,0},{9,1},... | collective-permute-start | bytes 393224 | tf_op jit(solution)/shard_map/ppermute | solution.py:330
  35.8 1.5 %collective-permute-start.13 = (bf16[128,512]{1,0:T(8,128)(2,1)S(1)}, bf16[128,512]{1,0:T(8,128)(2,1)S(1)}, u32[]{:S(2)}, u32[]{:S(2)}) collective-permute-start(bf16[128,512]{1,0:T(8,128)(2,1)S(1)} %glue.8), channel_id=1, source_target_pairs={{0,24},{1,25},{2,26},{3,27},{4,28},{5,29},{6,30},{7,31},{8,16},{9,... | collective-permute-start | bytes 393224 | tf_op jit(solution)/shard_map/ppermute | solution.py:330
  37.3 2.7 %encode.6 = (bf16[32,512]{1,0:T(8,128)(2,1)S(1)}, bf16[32,512]{1,0:T(8,128)(2,1)S(1)}, f32[32,512]{1,0:T(8,128)S(1)}) custom-call(bf16[128,512]{1,0:T(8,128)(2,1)S(1)} %get-tuple-element.54.refs_0_, f32[128,512]{1,0:T(8,128)S(1)} %get-tuple-element.55.refs_1_, bf16[512,512]{1,0:T(8,128)(2,1)S(1)} %get-tuple-element.69.refs_2_, ...), custom_call_target="tpu_custom_call" | custom-call | flops 1073741824 | bytes 6291456 | tf_op jit(solution)/shard_map/encode/pallas_call | solution.py:54
  40.1 0.6 collective-permute-start.14
  40.6 2.5 %encode.5 = (bf16[32,512]{1,0:T(8,128)(2,1)S(1)}, bf16[32,512]{1,0:T(8,128)(2,1)S(1)}, f32[32,512]{1,0:T(8,128)S(1)}) custom-call(bf16[128,512]{1,0:T(8,128)(2,1)S(1)} %get-tuple-element.54.refs_0_, f32[128,512]{1,0:T(8,128)S(1)} %get-tuple-element.55.refs_1_, bf16[512,512]{1,0:T(8,128)(2,1)S(1)} %get-tuple-element.69.refs_2_, ...), custom_call_target="tpu_custom_call" | custom-call | flops 1073741824 | bytes 6291456 | tf_op jit(solution)/shard_map/encode/pallas_call | solution.py:54
  43.2 1.2 %collective-permute-done.14.refs_11_ = bf16[32,512]{1,0:T(8,128)(2,1)S(1)} collective-permute-done((bf16[32,512]{1,0:T(8,128)(2,1)S(1)}, bf16[32,512]{1,0:T(8,128)(2,1)S(1)}, u32[]{:S(2)}, u32[]{:S(2)}) %collective-permute-start.14) | collective-permute-done | bytes 32800 | tf_op jit(solution)/shard_map/ppermute | solution.py:330
  44.4 2.3 %process.3 = (bf16[32,512]{1,0:T(8,128)(2,1)S(1)}, bf16[32,512]{1,0:T(8,128)(2,1)S(1)}, bf16[512,512]{1,0:T(8,128)(2,1)S(1)}) custom-call(bf16[32,512]{1,0:T(8,128)(2,1)S(1)} %get-tuple-element.66.refs_0_, f32[32,512]{1,0:T(8,128)S(1)} %get-tuple-element.67.refs_1_, bf16[32,512]{1,0:T(8,128)(2,1)S(1)} %get-tuple-element.68.refs_0_.refs_2_, ...), custom_call_target="tpu_custom_call" | custom-call | flops 1073741824 | bytes 6291456 | tf_op jit(solution)/shard_map/process/pallas_call | solution.py:54
  46.7 1.6 %collective-permute-start.16 = (bf16[32,512]{1,0:T(8,128)(2,1)S(1)}, bf16[32,512]{1,0:T(8,128)(2,1)S(1)}, u32[]{:S(2)}, u32[]{:S(2)}) collective-permute-start(bf16[32,512]{1,0:T(8,128)(2,1)S(1)} %get-tuple-element.78.refs_0_.refs_8_), channel_id=1, source_target_pairs={{0,7},{1,2},{2,1},{3,4},{4,3},{5,6},{6,5},{7,0},{8,15},{9,10},{10,... | collective-permute-start | bytes 98312 | tf_op jit(solution)/shard_map/ppermute | solution.py:330
  48.3 3.0 %process.4 = (bf16[48,512]{1,0:T(8,128)(2,1)S(1)}, bf16[48,512]{1,0:T(8,128)(2,1)S(1)}) custom-call(bf16[32,512]{1,0:T(8,128)(2,1)S(1)} %get-tuple-element.79.refs_0_, bf16[32,512]{1,0:T(8,128)(2,1)S(1)} %get-tuple-element.80.refs_1_, bf16[32,512]{1,0:T(8,128)(2,1)S(1)} %get-tuple-element.81.refs_2_, f32[32,512]{1,0:T(8,128)S(1)} %get-tuple-element.82.refs_3_, ...), custom_call_target="tpu_custom_call" | custom-call | flops 1610612736 | bytes 6291456 | tf_op jit(solution)/shard_map/process/pallas_call | solution.py:54
  51.3 0.6 collective-permute-done.16.refs_2_.refs_12_
  51.9 1.6 %collective-permute-start.17 = (bf16[96,512]{1,0:T(8,128)(2,1)S(1)}, bf16[96,512]{1,0:T(8,128)(2,1)S(1)}, u32[]{:S(2)}, u32[]{:S(2)}) collective-permute-start(bf16[96,512]{1,0:T(8,128)(2,1)S(1)} %glue.9), channel_id=1, source_target_pairs={{0,8},{1,9},{2,10},{3,11},{4,12},{5,13},{6,14},{7,15},{8,0},{9,1},... | collective-permute-start | bytes 294920 | tf_op jit(solution)/shard_map/ppermute | solution.py:330
  53.5 0.5 collective-permute-start.18
  53.9 3.5 %process.5 = (bf16[128,512]{1,0:T(8,128)(2,1)}, bf16[48,512]{1,0:T(8,128)(2,1)S(1)}) custom-call(bf16[32,512]{1,0:T(8,128)(2,1)S(1)} %get-tuple-element.79.refs_0_, bf16[32,512]{1,0:T(8,128)(2,1)S(1)} %get-tuple-element.80.refs_1_, bf16[32,512]{1,0:T(8,128)(2,1)S(1)} %get-tuple-element.81.refs_2_, f32[32,512]{1,0:T(8,128)S(1)} %get-tuple-element.82.refs_3_, ...), custom_call_target="tpu_custom_call" | custom-call | flops 1610612736 | bytes 6291456 | tf_op jit(solution)/shard_map/process/pallas_call | solution.py:54
  57.4 1.5 %collective-permute-done.18.refs_14_ = bf16[96,512]{1,0:T(8,128)(2,1)S(1)} collective-permute-done((bf16[96,512]{1,0:T(8,128)(2,1)S(1)}, bf16[96,512]{1,0:T(8,128)(2,1)S(1)}, u32[]{:S(2)}, u32[]{:S(2)}) %collective-permute-start.18) | collective-permute-done | bytes 98336 | tf_op jit(solution)/shard_map/ppermute | solution.py:330
  59.0 5.9 %decode.1 = bf16[512,512]{1,0:T(8,128)(2,1)} custom-call(bf16[512,512]{1,0:T(8,128)(2,1)S(1)} %get-tuple-element.48.refs_0_, s32[512,8]{1,0:T(8,128)S(1)} %get-tuple-element.49.refs_1_, f32[512,512]{1,0:T(8,128)S(1)} %get-tuple-element.50.refs_2_, bf16[512,512]{1,0:T(8,128)(2,1)S(1)} %get-tuple-element.51.refs_3_, f32[2,512]{1,0:T(2,128)S(1)} %copy-done.3, ...), custom_call_target="tpu_custom_call" | custom-call | flops 1409286144 | bytes 6291456 | tf_op jit(solution)/shard_map/decode/pallas_call | solution.py:54
  (34 shorter events, 0.4 us)
Async XLA Ops:
  2.1 11.6 %collective-permute-start = (bf16[128,512]{1,0:T(8,128)(2,1)S(1)}, bf16[128,512]{1,0:T(8,128)(2,1)S(1)}, u32[]{:S(2)}, u32[]{:S(2)}) collective-permute-start(bf16[128,512]{1,0:T(8,128)(2,1)S(1)} %project_border.1), channel_id=1, source_target_pairs={{0,8},{1,9},{2,10},{3,11},{4,12},{5,13},{6,14},{7,15},{8,0},{9,1},... | collective-permute-start | bytes 393224 | tf_op jit(solution)/shard_map/ppermute | solution.py:330
  5.1 8.6 %collective-permute-start.1 = (bf16[128,512]{1,0:T(8,128)(2,1)S(1)}, bf16[128,512]{1,0:T(8,128)(2,1)S(1)}, u32[]{:S(2)}, u32[]{:S(2)}) collective-permute-start(bf16[128,512]{1,0:T(8,128)(2,1)S(1)} %project_border.1), channel_id=1, source_target_pairs={{0,24},{1,25},{2,26},{3,27},{4,28},{5,29},{6,30},{7,31},{8,16},{9,... | collective-permute-start | bytes 393224 | tf_op jit(solution)/shard_map/ppermute | solution.py:330
  6.6 7.2 %collective-permute-start.2 = (bf16[128,512]{1,0:T(8,128)(2,1)S(1)}, bf16[128,512]{1,0:T(8,128)(2,1)S(1)}, u32[]{:S(2)}, u32[]{:S(2)}) collective-permute-start(bf16[128,512]{1,0:T(8,128)(2,1)S(1)} %project_border.1), channel_id=1, source_target_pairs={{0,7},{1,2},{2,1},{3,4},{4,3},{5,6},{6,5},{7,0},{8,15},{9,10},{10,... | collective-permute-start | bytes 393224 | tf_op jit(solution)/shard_map/ppermute | solution.py:330
  9.1 7.2 %collective-permute-start.7 = (bf16[128,512]{1,0:T(8,128)(2,1)S(1)}, bf16[128,512]{1,0:T(8,128)(2,1)S(1)}, u32[]{:S(2)}, u32[]{:S(2)}) collective-permute-start(bf16[128,512]{1,0:T(8,128)(2,1)S(1)} %project_border.1), channel_id=1, source_target_pairs={{0,1},{1,0},{2,3},{3,2},{4,5},{5,4},{6,7},{7,6},{8,9},{9,8},{10,11... | collective-permute-start | bytes 393224 | tf_op jit(solution)/shard_map/ppermute | solution.py:330
  13.8 7.0 %collective-permute-start.4 = (bf16[128,512]{1,0:T(8,128)(2,1)S(1)}, bf16[128,512]{1,0:T(8,128)(2,1)S(1)}, u32[]{:S(2)}, u32[]{:S(2)}) collective-permute-start(bf16[128,512]{1,0:T(8,128)(2,1)S(1)} %collective-permute-done.2.refs_2_), channel_id=1, source_target_pairs={{0,8},{1,9},{2,10},{3,11},{4,12},{5,13},{6,14},{7,15},{8,0},{9,1},... | collective-permute-start | bytes 393224 | tf_op jit(solution)/shard_map/ppermute | solution.py:330
  15.3 7.1 %collective-permute-start.6 = (bf16[128,512]{1,0:T(8,128)(2,1)S(1)}, bf16[128,512]{1,0:T(8,128)(2,1)S(1)}, u32[]{:S(2)}, u32[]{:S(2)}) collective-permute-start(bf16[128,512]{1,0:T(8,128)(2,1)S(1)} %collective-permute-done.2.refs_2_), channel_id=1, source_target_pairs={{0,24},{1,25},{2,26},{3,27},{4,28},{5,29},{6,30},{7,31},{8,16},{9,... | collective-permute-start | bytes 393224 | tf_op jit(solution)/shard_map/ppermute | solution.py:330
  15.7 6.7 %collective-permute-start.3 = (bf16[128,512]{1,0:T(8,128)(2,1)S(1)}, bf16[128,512]{1,0:T(8,128)(2,1)S(1)}, u32[]{:S(2)}, u32[]{:S(2)}) collective-permute-start(bf16[128,512]{1,0:T(8,128)(2,1)S(1)} %collective-permute-done.refs_3_), channel_id=1, source_target_pairs={{0,1},{1,0},{2,3},{3,2},{4,5},{5,4},{6,7},{7,6},{8,9},{9,8},{10,11... | collective-permute-start | bytes 393224 | tf_op jit(solution)/shard_map/ppermute | solution.py:330
  15.7 6.7 %collective-permute-start.5 = (bf16[128,512]{1,0:T(8,128)(2,1)S(1)}, bf16[128,512]{1,0:T(8,128)(2,1)S(1)}, u32[]{:S(2)}, u32[]{:S(2)}) collective-permute-start(bf16[128,512]{1,0:T(8,128)(2,1)S(1)} %collective-permute-done.1.refs_4_), channel_id=1, source_target_pairs={{0,1},{1,0},{2,3},{3,2},{4,5},{5,4},{6,7},{7,6},{8,9},{9,8},{10,11... | collective-permute-start | bytes 393224 | tf_op jit(solution)/shard_map/ppermute | solution.py:330
  16.2 6.2 %copy-start = (f32[2,512]{1,0:T(2,128)S(1)}, f32[2,512]{1,0:T(2,128)}, u32[]{:S(2)}) copy-start(f32[2,512]{1,0:T(2,128)} %refs_5_.5) | copy-start | bytes 12292
  16.2 6.2 %copy-start.1 = (f32[2,512]{1,0:T(2,128)S(1)}, f32[2,512]{1,0:T(2,128)}, u32[]{:S(2)}) copy-start(f32[2,512]{1,0:T(2,128)} %refs_8_.7) | copy-start | bytes 12292
  16.2 6.2 %copy-start.2 = (f32[2,512]{1,0:T(2,128)S(1)}, f32[2,512]{1,0:T(2,128)}, u32[]{:S(2)}) copy-start(f32[2,512]{1,0:T(2,128)} %refs_9_.3) | copy-start | bytes 12292
  24.9 1.3 %collective-permute-start.8 = (bf16[32,512]{1,0:T(8,128)(2,1)S(1)}, bf16[32,512]{1,0:T(8,128)(2,1)S(1)}, u32[]{:S(2)}, u32[]{:S(2)}) collective-permute-start(bf16[32,512]{1,0:T(8,128)(2,1)S(1)} %get-tuple-element.68.refs_0_.refs_2_), channel_id=1, source_target_pairs={{0,1},{1,0},{2,3},{3,2},{4,5},{5,4},{6,7},{7,6},{8,9},{9,8},{10,11... | collective-permute-start | bytes 98312 | tf_op jit(solution)/shard_map/ppermute | solution.py:330
  26.2 3.1 %collective-permute-start.10 = (bf16[8,512]{1,0:T(8,128)(2,1)S(1)}, bf16[8,512]{1,0:T(8,128)(2,1)S(1)}, u32[]{:S(2)}, u32[]{:S(2)}) collective-permute-start(bf16[8,512]{1,0:T(8,128)(2,1)S(1)} %glue.5.refs_0_), channel_id=1, source_target_pairs={{0,3},{1,2},{2,1},{3,0},{4,7},{5,6},{6,5},{7,4},{8,11},{9,10},{10,... | collective-permute-start | bytes 24584 | tf_op jit(solution)/shard_map/ppermute | solution.py:330
  26.3 8.0 %collective-permute-start.9 = (bf16[32,512]{1,0:T(8,128)(2,1)S(1)}, bf16[32,512]{1,0:T(8,128)(2,1)S(1)}, u32[]{:S(2)}, u32[]{:S(2)}) collective-permute-start(bf16[32,512]{1,0:T(8,128)(2,1)S(1)} %get-tuple-element.68.refs_0_.refs_2_), channel_id=1, source_target_pairs={{0,7},{1,2},{2,1},{3,4},{4,3},{5,6},{6,5},{7,0},{8,15},{9,10},{10,... | collective-permute-start | bytes 98312 | tf_op jit(solution)/shard_map/ppermute | solution.py:330
  29.3 5.0 %collective-permute-start.11 = (bf16[16,512]{1,0:T(8,128)(2,1)S(1)}, bf16[16,512]{1,0:T(8,128)(2,1)S(1)}, u32[]{:S(2)}, u32[]{:S(2)}) collective-permute-start(bf16[16,512]{1,0:T(8,128)(2,1)S(1)} %glue.6.refs_0_), channel_id=1, source_target_pairs={{0,7},{1,6},{2,5},{3,4},{4,3},{5,2},{6,1},{7,0},{8,15},{9,14},{10,... | collective-permute-start | bytes 49160 | tf_op jit(solution)/shard_map/ppermute | solution.py:330
  34.3 10.1 %collective-permute-start.12 = (bf16[128,512]{1,0:T(8,128)(2,1)S(1)}, bf16[128,512]{1,0:T(8,128)(2,1)S(1)}, u32[]{:S(2)}, u32[]{:S(2)}) collective-permute-start(bf16[128,512]{1,0:T(8,128)(2,1)S(1)} %glue.8), channel_id=1, source_target_pairs={{0,8},{1,9},{2,10},{3,11},{4,12},{5,13},{6,14},{7,15},{8,0},{9,1},... | collective-permute-start | bytes 393224 | tf_op jit(solution)/shard_map/ppermute | solution.py:330
  35.8 8.6 %collective-permute-start.13 = (bf16[128,512]{1,0:T(8,128)(2,1)S(1)}, bf16[128,512]{1,0:T(8,128)(2,1)S(1)}, u32[]{:S(2)}, u32[]{:S(2)}) collective-permute-start(bf16[128,512]{1,0:T(8,128)(2,1)S(1)} %glue.8), channel_id=1, source_target_pairs={{0,24},{1,25},{2,26},{3,27},{4,28},{5,29},{6,30},{7,31},{8,16},{9,... | collective-permute-start | bytes 393224 | tf_op jit(solution)/shard_map/ppermute | solution.py:330
  40.1 4.3 %copy-start.4 = (f32[2,512]{1,0:T(2,128)S(1)}, f32[2,512]{1,0:T(2,128)}, u32[]{:S(2)}) copy-start(f32[2,512]{1,0:T(2,128)} %refs_12_.3) | copy-start | bytes 12292
  40.1 4.3 %collective-permute-start.14 = (bf16[32,512]{1,0:T(8,128)(2,1)S(1)}, bf16[32,512]{1,0:T(8,128)(2,1)S(1)}, u32[]{:S(2)}, u32[]{:S(2)}) collective-permute-start(bf16[32,512]{1,0:T(8,128)(2,1)S(1)} %glue.7.refs_3_.refs_10_), channel_id=1, source_target_pairs={{0,16},{1,17},{2,18},{3,19},{4,20},{5,21},{6,22},{7,23},{8,24},{9,... | collective-permute-start | bytes 98312 | tf_op jit(solution)/shard_map/ppermute | solution.py:330
  46.7 4.6 %collective-permute-start.15 = (bf16[32,512]{1,0:T(8,128)(2,1)S(1)}, bf16[32,512]{1,0:T(8,128)(2,1)S(1)}, u32[]{:S(2)}, u32[]{:S(2)}) collective-permute-start(bf16[32,512]{1,0:T(8,128)(2,1)S(1)} %get-tuple-element.78.refs_0_.refs_8_), channel_id=1, source_target_pairs={{0,1},{1,0},{2,3},{3,2},{4,5},{5,4},{6,7},{7,6},{8,9},{9,8},{10,11... | collective-permute-start | bytes 98312 | tf_op jit(solution)/shard_map/ppermute | solution.py:330
  46.7 5.2 %collective-permute-start.16 = (bf16[32,512]{1,0:T(8,128)(2,1)S(1)}, bf16[32,512]{1,0:T(8,128)(2,1)S(1)}, u32[]{:S(2)}, u32[]{:S(2)}) collective-permute-start(bf16[32,512]{1,0:T(8,128)(2,1)S(1)} %get-tuple-element.78.refs_0_.refs_8_), channel_id=1, source_target_pairs={{0,7},{1,2},{2,1},{3,4},{4,3},{5,6},{6,5},{7,0},{8,15},{9,10},{10,... | collective-permute-start | bytes 98312 | tf_op jit(solution)/shard_map/ppermute | solution.py:330
  51.9 5.5 %collective-permute-start.17 = (bf16[96,512]{1,0:T(8,128)(2,1)S(1)}, bf16[96,512]{1,0:T(8,128)(2,1)S(1)}, u32[]{:S(2)}, u32[]{:S(2)}) collective-permute-start(bf16[96,512]{1,0:T(8,128)(2,1)S(1)} %glue.9), channel_id=1, source_target_pairs={{0,8},{1,9},{2,10},{3,11},{4,12},{5,13},{6,14},{7,15},{8,0},{9,1},... | collective-permute-start | bytes 294920 | tf_op jit(solution)/shard_map/ppermute | solution.py:330
  53.5 5.5 %collective-permute-start.18 = (bf16[96,512]{1,0:T(8,128)(2,1)S(1)}, bf16[96,512]{1,0:T(8,128)(2,1)S(1)}, u32[]{:S(2)}, u32[]{:S(2)}) collective-permute-start(bf16[96,512]{1,0:T(8,128)(2,1)S(1)} %glue.9), channel_id=1, source_target_pairs={{0,24},{1,25},{2,26},{3,27},{4,28},{5,29},{6,30},{7,31},{8,16},{9,... | collective-permute-start | bytes 294920 | tf_op jit(solution)/shard_map/ppermute | solution.py:330
  53.9 5.1 %copy-start.3 = (f32[2,512]{1,0:T(2,128)S(1)}, f32[2,512]{1,0:T(2,128)}, u32[]{:S(2)}) copy-start(f32[2,512]{1,0:T(2,128)} %refs_4_.1) | copy-start | bytes 12292
  53.9 5.1 %copy-start.5 = (f32[2,512]{1,0:T(2,128)S(1)}, f32[2,512]{1,0:T(2,128)}, u32[]{:S(2)}) copy-start(f32[2,512]{1,0:T(2,128)} %refs_7_.1) | copy-start | bytes 12292

commit v3 on v2

--- a/solution.py
+++ b/solution.py
@@ -63,22 +63,31 @@
     )(*ins)
 
 
-def glue(*parts):
-    width = parts[0][0].shape[1]
-    total = sum(rows for _, rows in parts)
+def glue(parts, size_y=0):
+    flat = [p for part in parts for p in ([q for _, q in part] if isinstance(part, list) else [part])]
+    total = sum((part[0][1] if isinstance(part, list) else part)[2] for part in parts)
+    width = flat[0][0].shape[1]
 
     def body(*refs):
-        out = refs[-1]
-        if any(rows % 16 for _, rows in parts):
-            values = [ref[pl.ds(0, rows), :].astype(F32) for ref, (_, rows) in zip(refs, parts)]
-            out[...] = jnp.concatenate(values, axis=0).astype(BF)
-        else:
-            start = 0
-            for ref, (_, rows) in zip(refs, parts):
-                out[pl.ds(start, rows), :] = ref[pl.ds(0, rows), :]
-                start += rows
-
-    return launch(body, "glue", [x for x, _ in parts], [SDS((total, width), BF)], [], 0, 1 << 10, 1 << 18, mib=2)[0]
+        refs = list(refs)
+        out = refs.pop()
+        values = []
+        for part in parts:
+            if isinstance(part, list):
+                place = lax.axis_index("gy")
+                peer = jnp.where(place & 1 == 1, place + 1, place - 1)
+                peer = jnp.where(peer < 0, peer + size_y, jnp.where(peer >= size_y, peer - size_y, peer))
+                value = None
+                for flip, (_, start, rows) in part:
+                    option = refs.pop(0)[pl.ds(start, rows), :].astype(F32)
+                    value = option if value is None else jnp.where((place ^ peer) == flip, option, value)
+                values.append(value)
+            else:
+                _, start, rows = part
+                values.append(refs.pop(0)[pl.ds(start, rows), :].astype(F32))
+        out[...] = jnp.concatenate(values, axis=0).astype(BF)
+
+    return launch(body, "glue", [p[0] for p in flat], [SDS((total, width), BF)], [], 0, 1 << 10, 1 << 18, mib=2)[0]
 
 
 def border_kernel(x, w, out, x_v, w_v, sems):
@@ -145,38 +154,60 @@
 
 def prepare_kernel(
     sizes, shapes,
-    grid, mesh, eids, mids, dids, ee, en, pe, pn, de, dn, eb, db,
-    grid_o, mesh_o, own, ebase, dbase, eat, mat, dat, ee2, en2, pe2, pn2, de2, dn2, en01, pe01, pn01, de01, dn01,
-    eids_v, mids_v, dids_v, w0_v, w1_v, eb_v, db_v, w2_v, sems,
+    grid, mesh, eids, ee, en, pe, eb,
+    grid_o, mesh_o, own, ebase, eat, ee2, en2, en01, pe01,
+    eids_v, w0_v, w1_v, eb_v, w2_v, sems,
 ):
     mover = Mover(sems)
-    grid_rows, mesh_rows, grid_border, mesh_border = shapes
-    heads = [
-        mover.start(a, b)
-        for a, b in (
-            (eids, eids_v), (mids, mids_v), (dids, dids_v), (grid, grid_o), (mesh, mesh_o),
-            (ee.at[0], w0_v), (ee.at[1], w1_v), (eb, eb_v), (db, db_v),
-        )
-    ]
-    seconds = [mover.start(w.at[2], w2_v.at[i]) for i, w in enumerate((ee, en, pe, pn, de, dn))]
-    pairs = [
-        mover.start(w.at[pl.ds(0, 2)], out)
-        for w, out in ((en, en01), (pe, pe01), (de, de01), (pn, pn01), (dn, dn01))
-    ]
-    for head in heads:
-        head.wait()
+    grid_rows, _, grid_border, _ = shapes
+    pairs = (
+        (eids, eids_v), (grid, grid_o), (ee.at[0], w0_v), (mesh, mesh_o), (ee.at[1], w1_v), (eb, eb_v),
+        (ee.at[2], w2_v.at[0]), (en.at[2], w2_v.at[1]), (en.at[pl.ds(0, 2)], en01), (pe.at[pl.ds(0, 2)], pe01),
+    )
+    loads = [mover.start(a, b) for a, b in pairs]
     places = (lax.axis_index("gx"), lax.axis_index("gy"))
+    loads[0].wait()
     eat[...] = turned(locate(eids_v[...], grid_rows, grid_border, 0, sizes, places, True))
+    for load in loads[1:3]:
+        load.wait()
     own[...] = (mm(grid_o[...], w0_v[...]) * 0.5).astype(BF)
+    for load in loads[3:6]:
+        load.wait()
     ebase[...] = (mm(mesh_o[...], w1_v[...]) + eb_v[0:1, :]) * 0.5
+    for i, out in enumerate((ee2, en2)):
+        loads[6 + i].wait()
+        out[...] = centre(w2_v[i])
+    for load in loads[8:]:
+        load.wait()
+
+
+def prepare_later_kernel(
+    sizes, shapes,
+    mids, dids, pe, pn, de, dn, db, grid,
+    dbase, mat, dat, pe2, pn2, de2, dn2, pn01, de01, dn01,
+    mids_v, dids_v, db_v, w2_v, sems,
+):
+    mover = Mover(sems)
+    _, mesh_rows, _, mesh_border = shapes
+    pairs = (
+        (mids, mids_v), (dids, dids_v), (db, db_v),
+        (pe.at[2], w2_v.at[0]), (pn.at[2], w2_v.at[1]), (de.at[2], w2_v.at[2]), (dn.at[2], w2_v.at[3]),
+        (de.at[pl.ds(0, 2)], de01), (pn.at[pl.ds(0, 2)], pn01), (dn.at[pl.ds(0, 2)], dn01),
+    )
+    loads = [mover.start(a, b) for a, b in pairs]
+    places = (lax.axis_index("gx"), lax.axis_index("gy"))
+    loads[0].wait()
     mat[...] = turned(locate(mids_v[...], mesh_rows, mesh_border, CM, sizes, places))
+    loads[1].wait()
     dat[...] = turned(locate(dids_v[...], mesh_rows, mesh_border, 0, sizes, places))
-    for i, (second, out) in enumerate(zip(seconds, (ee2, en2, pe2, pn2, de2, dn2))):
-        second.wait()
+    loads[2].wait()
+    for i, out in enumerate((pe2, pn2, de2, dn2)):
+        loads[3 + i].wait()
         out[...] = centre(w2_v[i])
-    for pair in pairs:
-        pair.wait()
-    dbase[...] = (mm(grid_o[...], de01[1]) + db_v[0:1, :]) * 0.5
+    loads[7].wait()
+    dbase[...] = (mm(grid[...], de01[1]) + db_v[0:1, :]) * 0.5
+    for load in loads[8:]:
+        load.wait()
 
 
 def chosen(places, ks, lanes):
@@ -190,10 +221,11 @@
 
     def gather(ks):
         half = mm(chosen(places, ks, lanes), table[...])
+        half = half.reshape(len(ks), rows, width)
         if begun is not None:
             ref, start = begun
-            half = half + ref[pl.ds(start + ks[0] * rows, len(ks) * rows), :].astype(F32)
-        return half.reshape(len(ks), rows, width) + base[None]
+            half = half + ref[pl.ds(ks[0], len(ks)), pl.ds(start, rows), :].astype(F32)
+        return half + base[None]
 
     total = jnp.zeros((rows, width), F32)
     ahead = gather(groups[0])
@@ -223,20 +255,25 @@
             near = places[pl.ds(at, block), :]
             for k in range(0, degree, slots):
                 ks = range(k, min(k + slots, degree))
-                picked = mm(chosen(near, ks, lanes), table[...])
-                out[pl.ds(at * degree + k * block, len(ks) * block), :] = picked.astype(BF)
+                picked = mm(chosen(near, ks, lanes), table[...]).astype(BF)
+                out[pl.ds(k, len(ks)), pl.ds(at, block), :] = picked.reshape(len(ks), block, width)
 
     return launch(
-        body, "begin", [places] + pieces, [SDS((count * degree, width), BF)], [((table_rows, width), BF)], 0,
+        body, "begin", [places] + pieces, [SDS((degree, count, width), BF)], [((table_rows, width), BF)], 0,
         2 * count * degree * table_rows * width, 4 << 20,
     )[0]
 
 
-def lay(pieces, table):
-    start = 0
-    for piece in pieces:
-        table[pl.ds(start, piece.shape[0]), :] = piece[...]
-        start += piece.shape[0]
+def ranged(pieces):
+    return [p if isinstance(p, tuple) else (p, 0, p.shape[0]) for p in pieces]
+
+
+def lay(refs, table, pieces=None):
+    at = 0
+    for i, ref in enumerate(refs):
+        start, rows = (0, ref.shape[0]) if pieces is None else pieces[i][1:]
+        table[pl.ds(at, rows), :] = ref[pl.ds(start, rows), :]
+        at += rows
 
 
 def node_update(x, summed, w0, w1, w2, vectors):
@@ -259,8 +296,9 @@
 def mesh_stage(xs, places, base_place, at, count, pieces, keep, bases, ew2, ev, nw, nw2, nv, following, fv, joined, steps, name, lift=0, begun=None):
     width = xs[0].shape[1]
     degree = places.shape[1]
-    table_rows = sum(p.shape[0] for p in pieces)
-    groups = [xs, bases, pieces, [places, ew2, ev, nw, nw2, nv, following], [] if fv is None else [fv], joined, [] if begun is None else [begun]]
+    pieces = ranged(pieces)
+    table_rows = sum(p[2] for p in pieces)
+    groups = [xs, bases, [p[0] for p in pieces], [places, ew2, ev, nw, nw2, nv, following], [] if fv is None else [fv], joined, [] if begun is None else [begun]]
     ins = [x for group in groups for x in group]
     rows_out = count + sum(x.shape[0] for x in joined)
     outs = [SDS((rows_out, width), BF), SDS((count, width), BF)]
@@ -277,8 +315,8 @@
         table = pieces_in[0]
         if keep:
             table = refs[-1]
-            lay(pieces_in, table)
-        summed = edge_sum(places[pl.ds(base_place + at, count), :], degree, table, rows_of(bases, at, count), ew2[...], ev, steps, lift, *[(ref, at * degree) for ref in begun_in])
+            lay(pieces_in, table, pieces)
+        summed = edge_sum(places[pl.ds(base_place + at, count), :], degree, table, rows_of(bases, at, count), ew2[...], ev, steps, lift, *[(ref, at) for ref in begun_in])
         new = node_update(rows_of(xs, at, count), summed, nw[0], nw[1], nw2[...], nv)
         refs[0][pl.ds(rows_out - count, count), :] = new
         start = 0
@@ -293,30 +331,81 @@
     return launch(body, name, ins, outs, [], 0, flops, 6 << 20)
 
 
+def edge_stage(places, first, at, count, table, bases, ew2, ev, slots, lift=0, begun=None):
+    width = table.shape[1]
+    degree = places.shape[1]
+    groups = [bases, [places, table, ew2, ev], [] if begun is None else [begun]]
+
+    def body(*refs):
+        refs = list(refs)
+        taken = []
+        for group in groups:
+            taken.append(refs[: len(group)])
+            refs = refs[len(group) :]
+        bases, (places, table, ew2, ev), begun_in = taken
+        summed = edge_sum(
+            places[pl.ds(first + at, count), :], degree, table, rows_of(bases, at, count), ew2[...], ev, slots, lift,
+            *[(ref, first + at) for ref in begun_in],
+        )
+        refs[0][...] = summed.astype(BF)
+
+    flops = count * degree * (2 * width * table.shape[0] + 2 * width * width)
+    return launch(body, "edges", [x for g in groups for x in g], [SDS((count, width), BF)], [], 0, flops, 4 << 20)[0]
+
+
+def node_stage(xs, at, sums, nw, nw2, nv, following, fv, joined):
+    width = xs[0].shape[1]
+    count = sum(x.shape[0] for x in sums)
+    groups = [xs, sums, [nw, nw2, nv, following], [] if fv is None else [fv], joined]
+    rows_out = count + sum(x.shape[0] for x in joined)
+    outs = [SDS((rows_out, width), BF), SDS((count, width), BF)]
+    outs += [] if fv is None else [SDS((count, width), F32)]
+
+    def body(*refs):
+        refs = list(refs)
+        taken = []
+        for group in groups:
+            taken.append(refs[: len(group)])
+            refs = refs[len(group) :]
+        xs, sums, (nw, nw2, nv, follow), fv, joined_in = taken
+        new = node_update(rows_of(xs, at, count), rows_of(sums, 0, count), nw[0], nw[1], nw2[...], nv)
+        lay(joined_in, refs[0])
+        refs[0][pl.ds(rows_out - count, count), :] = new
+        refs[1][...] = (mm(new, follow[0]) * 0.5).astype(BF)
+        for ref in fv:
+            refs[2][...] = (mm(new, follow[1]) + ref[0:1, :]) * 0.5
+
+    return launch(body, "nodes", [x for g in groups for x in g], outs, [], 0, 10 * count * width * width, 4 << 20)
+
+
 def decode_stage(x, places, degree, pieces, base, ew2, ev, nw, nw2, nv, block):
     rows, width = x.shape
-    table_rows = sum(p.shape[0] for p in pieces)
-    ins = [x, places, base, ew2, ev, nw, nw2, nv] + pieces
+    pieces = ranged(pieces)
+    table_rows = sum(p[2] for p in pieces)
+    ins = [x, places, base, ew2, ev, nw, nw2, nv] + [p[0] for p in pieces]
     outs = [SDS((rows, width), BF)]
 
     def body(*refs):
         refs = list(refs)
         x, places, base, ew2, ev, nw, nw2, nv = refs[:8]
         pieces_in = refs[8 : 8 + len(pieces)]
-        out, table, new, sems = refs[8 + len(pieces) :]
+        out, table, sums, new, sems = refs[8 + len(pieces) :]
         mover = Mover(sems)
-        lay(pieces_in, table)
+        lay(pieces_in, table, pieces)
         tails = []
         for at in range(0, rows, block):
             part = pl.ds(at, block)
-            summed = edge_sum(places[part, :], degree, table, base[part, :], ew2[...], ev, degree)
-            new[part, :] = node_update(x[part, :], summed, nw[0], nw[1], nw2[...], nv)
+            summed = edge_sum(places[part, :], degree, table, base[part, :], ew2[...], ev, 1)
+            sums[part, :] = summed.astype(BF)
+        for at in range(0, rows, block):
+            part = pl.ds(at, block)
+            new[part, :] = node_update(x[part, :], sums[part, :], nw[0], nw[1], nw2[...], nv)
             tails.append(mover.start(new.at[part], out.at[part]))
         for tail in tails:
             tail.wait()
 
     flops = rows * degree * (2 * width * table_rows + 2 * width * width)
-    scratch = [((table_rows, width), BF), ((rows, width), BF)]
+    scratch = [((table_rows, width), BF), ((rows, width), BF), ((rows, width), BF)]
     return launch(body, "decode", ins, outs, scratch, rows // block, flops, 6 << 20, far_outs=(0,))[0]
 
 
@@ -366,26 +455,18 @@
 
     degrees = [ids.shape[0] + -ids.shape[0] % 8 for ids in (encode_senders, mesh_senders, decode_senders)]
     square_shape = ((width, width), BF)
+    pair_shape = ((2, width, width), BF)
+    facts = ((size_x, size_y), (grid_rows, mesh_rows, grid_border, mesh_border))
     outs = [
-        ((grid_rows, width), BF), ((mesh_rows, width), BF), ((grid_rows, width), BF),
-        ((mesh_rows, width), F32), ((grid_rows, width), F32),
-        ((mesh_rows, degrees[0]), I32), ((mesh_rows, degrees[1]), I32), ((grid_rows, degrees[2]), I32),
-    ] + [square_shape] * 6 + [((2, width, width), BF)] * 5
-    (
-        grid_latent, mesh_latent, own, base, grid_base, encode_at, mesh_at, decode_at,
-        ee2, en2, pe2, pn2, de2, dn2, en01, pe01, pn01, de01, dn01,
-    ) = launch(
-        functools.partial(prepare_kernel, (size_x, size_y), (grid_rows, mesh_rows, grid_border, mesh_border)), "prepare",
-        [
-            grid_latent, mesh_latent, encode_senders, mesh_senders, decode_senders, encoder_edges, encoder_nodes,
-            process_edges, process_nodes, decoder_edges, decoder_nodes, encoder_edgebias, decoder_edgebias,
-        ],
+        ((grid_rows, width), BF), ((mesh_rows, width), BF), ((grid_rows, width), BF), ((mesh_rows, width), F32),
+        ((mesh_rows, degrees[0]), I32), square_shape, square_shape, pair_shape, pair_shape,
+    ]
+    grid_latent, mesh_latent, own, base, encode_at, ee2, en2, en01, pe01 = launch(
+        functools.partial(prepare_kernel, *facts), "prepare",
+        [grid_latent, mesh_latent, encode_senders, encoder_edges, encoder_nodes, process_edges, encoder_edgebias],
         [SDS(s, d) for s, d in outs],
-        [
-            (encode_senders.shape, I32), (mesh_senders.shape, I32), (decode_senders.shape, I32), square_shape, square_shape,
-            ((2, width), F32), ((2, width), F32), ((6, width, width), BF),
-        ],
-        20, 2 * grid_rows * square, 12 << 20, far_ins=range(13), mib=16,
+        [(encode_senders.shape, I32), square_shape, square_shape, ((2, width), F32), pair_shape],
+        10, grid_rows * square, 6 << 20, far_ins=range(7), mib=12,
     )
     e, o, z, own = lax.optimization_barrier((e, o, z, own))
     ec = send(e, pair_y)
@@ -396,60 +477,71 @@
     lift = grid_rows + 4 * grid_border
     pieces = [ec, ez, oc, oz]
 
-    cuts = list(range(0, mesh_rows + 1, mesh_border))
-    encoded = []
-    for at, end in zip(cuts, cuts[1:]):
-        part = mesh_stage(
-            [mesh_latent], encode_at, 0, at, end - at, pieces, at == 0, [base], ee2, encoder_edgebias, en01, en2,
-            encoder_nodebias, pe01, process_edgebias, [], 8, "encode", lift, begun,
-        )
-        if at == 0:
-            pieces = [part[3]]
-        encoded.append(part)
-
-    border = encoded[0][1]
+    encoded = mesh_stage(
+        [mesh_latent], encode_at, 0, 0, mesh_border, pieces, True, [base], ee2, encoder_edgebias, en01, en2,
+        encoder_nodebias, pe01, process_edgebias, [], 8, "encode", lift, begun,
+    )
+    cuts = [mesh_rows * k // 8 for k in (2, 3, 4, 6, 8)]
+    sums = [
+        edge_stage(encode_at, 0, at, end - at, encoded[3], [base], ee2, encoder_edgebias, 256 // (end - at), lift, begun)
+        for at, end in zip(cuts, cuts[1:])
+    ]
+    outs = [
+        ((grid_rows, width), F32), ((mesh_rows, degrees[1]), I32), ((grid_rows, degrees[2]), I32),
+    ] + [square_shape] * 4 + [pair_shape] * 3
+    border = encoded[1]
     c = send(border, pair_y)
-    z = send(border, next_y)
-    column = glue((border, CM), (c, CM))
+    c, sums[0] = lax.optimization_barrier((c, sums[0]))
+    column = [(border, 0, CM), (c, 0, CM)]
+    others = []
     step = 2
     while step < size_y:
         flip = 2 * step - 1
-        other = send(column, lambda i, j, flip=flip: (i, j ^ flip))
-        column = glue((column, CM * step), (other, CM * step))
+        other = send(glue([(border, 0, mesh_border)] + column), lambda i, j, flip=flip: (i, j ^ flip))
+        if step == 2:
+            other, sums[1] = lax.optimization_barrier((other, sums[1]))
+        if step == 2:
+            later_in, other = lax.optimization_barrier((grid_latent, other))
+            later = list(launch(
+                functools.partial(prepare_later_kernel, *facts), "prepare_later",
+                [mesh_senders, decode_senders, process_edges, process_nodes, decoder_edges, decoder_nodes, decoder_edgebias, later_in],
+                [SDS(s, d) for s, d in outs],
+                [(mesh_senders.shape, I32), (decode_senders.shape, I32), ((2, width), F32), ((4, width, width), BF)],
+                10, grid_rows * square, 6 << 20, far_ins=range(7), mib=12,
+            ))
+        if step == 4:
+            other, sums[2], later[0] = lax.optimization_barrier((other, sums[2], later[0]))
+        others.append((flip, (other, 0, mesh_border)))
+        column = column + [(other, mesh_border, CM * step)]
         step *= 2
-    stack = glue((border, mesh_border), (c, mesh_border), (z, mesh_border), (column, CM * size_y))
+    stack = glue([(border, 0, mesh_border), (c, 0, mesh_border), others] + column, size_y)
+    column = glue(column)
     e = send(stack, pair_x)
     o = send(stack, next_x)
     far = [send(column, lambda i, j, d=d: (i - d, j)) for d in range(2, size_x - 1)]
-    pieces = [part[1] for part in encoded] + [c, z, e, o, column] + far
+    rest = node_stage([mesh_latent], mesh_border, sums, en01, en2, encoder_nodebias, pe01, process_edgebias, [])
+    pieces = [encoded[1], rest[1], (stack, mesh_border, 2 * mesh_border), e, o, column] + far
+    grid_base, mesh_at, decode_at, pe2, pn2, de2, dn2, pn01, de01, dn01 = later
 
     first = mesh_stage(
-        [encoded[0][0]], mesh_at, 0, 0, mesh_border, pieces, True, [encoded[0][2]], pe2, process_edgebias, pn01, pn2,
+        [encoded[0]], mesh_at, 0, 0, mesh_border, pieces, True, [encoded[2]], pe2, process_edgebias, pn01, pn2,
         process_nodebias, de01, None, [], 8, "process",
     )
     border = first[1]
     c = send(border, pair_y)
     z = send(border, next_y)
     half = (mesh_rows - mesh_border) // 2
-    xs, bases = ([part[i] for part in encoded[1:]] for i in (0, 2))
-    tables, joined = [first[2]], [first[0]]
-    projected = [border]
-    for at in (0, half):
-        part = mesh_stage(
-            xs, mesh_at, mesh_border, at, half, tables, False, bases, pe2, process_edgebias, pn01, pn2, process_nodebias, de01, None,
-            joined if at else [], 4, "process",
-        )
-        joined.append(part[0])
-        projected.append(part[1])
-        if at == 0:
-            c, z, joined[-1] = lax.optimization_barrier((c, z, joined[-1]))
-    processed = joined[-1]
-    stack = glue((border, mesh_border), (c, mesh_border), (z, mesh_border))
+    sums = [
+        edge_stage(mesh_at, mesh_border, at, half, first[2], [rest[2]], pe2, process_edgebias, 4) for at in (0, half)
+    ]
+    c, z, sums[0] = lax.optimization_barrier((c, z, sums[0]))
+    processed, projected = node_stage([rest[0]], 0, sums, pn01, pn2, process_nodebias, de01, None, [first[0]])
+    stack = glue([(border, 0, mesh_border), (c, 0, mesh_border), (z, 0, mesh_border)])
     e = send(stack, pair_x)
     o = send(stack, next_x)
     decoded = decode_stage(
-        grid_latent, decode_at, decode_senders.shape[0], projected + [c, z, e, o], grid_base, de2, decoder_edgebias,
-        dn01, dn2, decoder_nodebias, 128,
+        grid_latent, decode_at, decode_senders.shape[0], [border, projected, (stack, mesh_border, 2 * mesh_border), e, o], grid_base, de2, decoder_edgebias,
+        dn01, dn2, decoder_nodebias, grid_rows // 2,
     )
     return (decoded, processed)
 

time: 65.3 us -> 63.8 us (0.977)
  Pallas kernels: 35.5 us -> 32.9 us
  waiting for transfers between devices: 8.04 us -> 8.81 us
    pallas_call x16 -> x20, Pallas kernels: 35.5 us -> 32.9 us  [launch(): pl.pallas_call(body, out_shape=outs, in_specs=[far if i in far_ins else n...]
    ppermute x19 -> x18, waiting for transfers between devices: 8.04 us -> 8.81 us  [send(): return lax.ppermute(rows, AXES, pairs)]
    ppermute x19 -> x18, starting transfers between devices: 20.5 us -> 20.8 us  [send(): return lax.ppermute(rows, AXES, pairs)]
  transfers between devices with their start and end apart: 19 -> 18, of which waited for: 8 -> 8; matrix products, arithmetic and copies ran while one was open for 0% -> 0% of each run, Pallas kernels for 36% -> 35%
where the time goes in v3:
time: 63.8 us; the launch traced here: 63.5 us
  Pallas kernels  32.9 us (52%)
  starting transfers between devices  20.8 us (33%)
  waiting for transfers between devices  8.81 us (14%)
  between operations  1.01 us (2%)
    pallas_call x20, Pallas kernels, launch(): pl.pallas_call(body, out_shape=outs, in_specs=[far if i in far_ins else n...  32.9 us
    ppermute x18, starting transfers between devices, send(): return lax.ppermute(rows, AXES, pairs)  20.8 us
    ppermute x18, waiting for transfers between devices, send(): return lax.ppermute(rows, AXES, pairs)  8.81 us
  transfers between devices with their start and end apart: 18, of which 8 were waited for; matrix products, arithmetic and copies ran while one was open for 0% of the time, Pallas kernels for 35%

profile of v3, /device:TPU:0, one launch (start us, length us, event | category | flops | bytes accessed | tf_op | source)
XLA Modules:
  0.0 63.5 jit_solution(10947121636642755757)
XLA Ops:
  0.6 1.4 %project_border.1 = bf16[128,512]{1,0:T(8,128)(2,1)S(1)} custom-call(bf16[512,512]{1,0:T(8,128)(2,1)} %x.1, bf16[3,512,512]{2,1,0:T(8,128)(2,1)} %w.1), custom_call_target="tpu_custom_call" | custom-call | flops 67108864 | bytes 1048576 | tf_op jit(solution)/shard_map/project_border/pallas_call | solution.py:54
  2.1 4.6 %collective-permute-start.2 = (bf16[128,512]{1,0:T(8,128)(2,1)S(1)}, bf16[128,512]{1,0:T(8,128)(2,1)S(1)}, u32[]{:S(2)}, u32[]{:S(2)}) collective-permute-start(bf16[128,512]{1,0:T(8,128)(2,1)S(1)} %project_border.1), channel_id=1, source_target_pairs={{0,7},{1,2},{2,1},{3,4},{4,3},{5,6},{6,5},{7,0},{8,15},{9,10},{10,... | collective-permute-start | bytes 393224 | tf_op jit(solution)/shard_map/ppermute | solution.py:419
  6.7 2.4 %collective-permute-start.1 = (bf16[128,512]{1,0:T(8,128)(2,1)S(1)}, bf16[128,512]{1,0:T(8,128)(2,1)S(1)}, u32[]{:S(2)}, u32[]{:S(2)}) collective-permute-start(bf16[128,512]{1,0:T(8,128)(2,1)S(1)} %project_border.1), channel_id=1, source_target_pairs={{0,24},{1,25},{2,26},{3,27},{4,28},{5,29},{6,30},{7,31},{8,16},{9,... | collective-permute-start | bytes 393224 | tf_op jit(solution)/shard_map/ppermute | solution.py:419
  9.1 0.5 collective-permute-start
  9.6 2.5 %prepare.1 = (bf16[512,512]{1,0:T(8,128)(2,1)S(1)}, bf16[128,512]{1,0:T(8,128)(2,1)S(1)}, bf16[512,512]{1,0:T(8,128)(2,1)S(1)}, f32[128,512]{1,0:T(8,128)S(1)}, ...) custom-call(bf16[512,512]{1,0:T(8,128)(2,1)} %x.1, ...), custom_call_target="tpu_custom_call" | custom-call | flops 268435456 | bytes 6291456 | tf_op jit(solution)/shard_map/prepare/pallas_call | solution.py:54
  12.2 0.9 %collective-permute-done.1.refs_4_ = bf16[128,512]{1,0:T(8,128)(2,1)S(1)} collective-permute-done((bf16[128,512]{1,0:T(8,128)(2,1)S(1)}, bf16[128,512]{1,0:T(8,128)(2,1)S(1)}, u32[]{:S(2)}, u32[]{:S(2)}) %collective-permute-start.1) | collective-permute-done | bytes 131104 | tf_op jit(solution)/shard_map/ppermute | solution.py:419
  13.0 1.5 %collective-permute-done.refs_3_ = bf16[128,512]{1,0:T(8,128)(2,1)S(1)} collective-permute-done((bf16[128,512]{1,0:T(8,128)(2,1)S(1)}, bf16[128,512]{1,0:T(8,128)(2,1)S(1)}, u32[]{:S(2)}, u32[]{:S(2)}) %collective-permute-start) | collective-permute-done | bytes 131104 | tf_op jit(solution)/shard_map/ppermute | solution.py:419
  14.5 1.4 %collective-permute-start.6 = (bf16[128,512]{1,0:T(8,128)(2,1)S(1)}, bf16[128,512]{1,0:T(8,128)(2,1)S(1)}, u32[]{:S(2)}, u32[]{:S(2)}) collective-permute-start(bf16[128,512]{1,0:T(8,128)(2,1)S(1)} %collective-permute-done.2.refs_2_), channel_id=1, source_target_pairs={{0,24},{1,25},{2,26},{3,27},{4,28},{5,29},{6,30},{7,31},{8,16},{9,... | collective-permute-start | bytes 393224 | tf_op jit(solution)/shard_map/ppermute | solution.py:419
  15.9 0.5 collective-permute-start.4
  17.0 4.5 %begin.1.refs_14_.refs_5_ = bf16[32,128,512]{2,1,0:T(8,128)(2,1)S(1)} custom-call(s32[128,32]{1,0:T(8,128)S(1)} %get-tuple-element.56.places.refs_6_.refs_1_, bf16[512,512]{1,0:T(8,128)(2,1)S(1)} %get-tuple-element.61.refs_0_, bf16[128,512]{1,0:T(8,128)(2,1)S(1)} %collective-permute-done.7.refs_1_, bf16[128,512]{1,0:T(8,128)(2,1)S(1)} %collective-permute-done.2.refs_2_, ...), custom_call_target="tpu_custom_call" | custom-call | flops 4294967296 | bytes 4194304 | tf_op jit(solution)/shard_map/begin/pallas_call | solution.py:54
  21.6 2.5 %encode.1 = (bf16[32,512]{1,0:T(8,128)(2,1)S(1)}, bf16[32,512]{1,0:T(8,128)(2,1)S(1)}, f32[32,512]{1,0:T(8,128)S(1)}, bf16[512,512]{1,0:T(8,128)(2,1)S(1)}) custom-call(bf16[128,512]{1,0:T(8,128)(2,1)S(1)} %get-tuple-element.50.refs_0_, f32[128,512]{1,0:T(8,128)S(1)} %get-tuple-element.51.refs_1_.refs_0_, ...), custom_call_target="tpu_custom_call" | custom-call | flops 1073741824 | bytes 6291456 | tf_op jit(solution)/shard_map/encode/pallas_call | solution.py:54
  24.2 1.1 %edges.6.refs_1_ = bf16[16,512]{1,0:T(8,128)(2,1)S(1)} custom-call(f32[128,512]{1,0:T(8,128)S(1)} %get-tuple-element.51.refs_1_.refs_0_, s32[128,32]{1,0:T(8,128)S(1)} %get-tuple-element.56.places.refs_6_.refs_1_, bf16[512,512]{1,0:T(8,128)(2,1)S(1)} %get-tuple-element.63.refs_2_, bf16[512,512]{1,0:T(8,128)(2,1)S(1)} %get-tuple-element.57.refs_7_.refs_3_, ...), custom_call_target="tpu_custom_call" | custom-call | flops 536870912 | bytes 4194304 | tf_op jit(solution)/shard_map/edges/pallas_call | solution.py:54
  25.4 1.9 %collective-permute-start.9 = (bf16[40,512]{1,0:T(8,128)(2,1)S(1)}, bf16[40,512]{1,0:T(8,128)(2,1)S(1)}, u32[]{:S(2)}, u32[]{:S(2)}) collective-permute-start(bf16[40,512]{1,0:T(8,128)(2,1)S(1)} %glue.5), channel_id=1, source_target_pairs={{0,3},{1,2},{2,1},{3,0},{4,7},{5,6},{6,5},{7,4},{8,11},{9,10},{10,... | collective-permute-start | bytes 122888 | tf_op jit(solution)/shard_map/ppermute | solution.py:419
  27.3 1.1 %edges.7.refs_2_ = bf16[16,512]{1,0:T(8,128)(2,1)S(1)} custom-call(f32[128,512]{1,0:T(8,128)S(1)} %get-tuple-element.51.refs_1_.refs_0_, s32[128,32]{1,0:T(8,128)S(1)} %get-tuple-element.56.places.refs_6_.refs_1_, bf16[512,512]{1,0:T(8,128)(2,1)S(1)} %get-tuple-element.63.refs_2_, bf16[512,512]{1,0:T(8,128)(2,1)S(1)} %get-tuple-element.57.refs_7_.refs_3_, ...), custom_call_target="tpu_custom_call" | custom-call | flops 536870912 | bytes 4194304 | tf_op jit(solution)/shard_map/edges/pallas_call | solution.py:54
  28.4 0.6 collective-permute-done.9.refs_3_.refs_2_.refs_6_
  29.0 2.5 %collective-permute-start.10 = (bf16[48,512]{1,0:T(8,128)(2,1)S(1)}, bf16[48,512]{1,0:T(8,128)(2,1)S(1)}, u32[]{:S(2)}, u32[]{:S(2)}) collective-permute-start(bf16[48,512]{1,0:T(8,128)(2,1)S(1)} %glue.6), channel_id=1, source_target_pairs={{0,7},{1,6},{2,5},{3,4},{4,3},{5,2},{6,1},{7,0},{8,15},{9,14},{10,... | collective-permute-start | bytes 147464 | tf_op jit(solution)/shard_map/ppermute | solution.py:419
  31.5 1.8 %edges.8.refs_3_ = bf16[32,512]{1,0:T(8,128)(2,1)S(1)} custom-call(f32[128,512]{1,0:T(8,128)S(1)} %get-tuple-element.51.refs_1_.refs_0_, s32[128,32]{1,0:T(8,128)S(1)} %get-tuple-element.56.places.refs_6_.refs_1_, bf16[512,512]{1,0:T(8,128)(2,1)S(1)} %get-tuple-element.63.refs_2_, bf16[512,512]{1,0:T(8,128)(2,1)S(1)} %get-tuple-element.57.refs_7_.refs_3_, ...), custom_call_target="tpu_custom_call" | custom-call | flops 1073741824 | bytes 4194304 | tf_op jit(solution)/shard_map/edges/pallas_call | solution.py:54
  33.3 2.6 %prepare_later.1 = (f32[512,512]{1,0:T(8,128)S(1)}, s32[128,32]{1,0:T(8,128)S(1)}, s32[512,8]{1,0:T(8,128)S(1)}, bf16[512,512]{1,0:T(8,128)(2,1)S(1)}, bf16[512,...) custom-call(s32[32,128]{1,0:T(8,128)} %mids.1, ...), custom_call_target="tpu_custom_call" | custom-call | flops 268435456 | bytes 6291456 | tf_op jit(solution)/shard_map/prepare_later/pallas_call | solution.py:54
  36.1 2.7 %collective-permute-start.12 = (bf16[128,512]{1,0:T(8,128)(2,1)S(1)}, bf16[128,512]{1,0:T(8,128)(2,1)S(1)}, u32[]{:S(2)}, u32[]{:S(2)}) collective-permute-start(bf16[128,512]{1,0:T(8,128)(2,1)S(1)} %glue.7.refs_4_), channel_id=1, source_target_pairs={{0,24},{1,25},{2,26},{3,27},{4,28},{5,29},{6,30},{7,31},{8,16},{9,... | collective-permute-start | bytes 393224 | tf_op jit(solution)/shard_map/ppermute | solution.py:419
  38.8 0.5 collective-permute-start.11
  39.7 1.8 %edges.9.refs_4_ = bf16[32,512]{1,0:T(8,128)(2,1)S(1)} custom-call(f32[128,512]{1,0:T(8,128)S(1)} %get-tuple-element.51.refs_1_.refs_0_, s32[128,32]{1,0:T(8,128)S(1)} %get-tuple-element.56.places.refs_6_.refs_1_, bf16[512,512]{1,0:T(8,128)(2,1)S(1)} %get-tuple-element.63.refs_2_, bf16[512,512]{1,0:T(8,128)(2,1)S(1)} %get-tuple-element.57.refs_7_.refs_3_, ...), custom_call_target="tpu_custom_call" | custom-call | flops 1073741824 | bytes 4194304 | tf_op jit(solution)/shard_map/edges/pallas_call | solution.py:54
  41.5 0.8 %nodes.2 = (bf16[96,512]{1,0:T(8,128)(2,1)S(1)}, bf16[96,512]{1,0:T(8,128)(2,1)S(1)}, f32[96,512]{1,0:T(8,128)S(1)}) custom-call(bf16[128,512]{1,0:T(8,128)(2,1)S(1)} %get-tuple-element.50.refs_0_, bf16[16,512]{1,0:T(8,128)(2,1)S(1)} %edges.6.refs_1_, bf16[16,512]{1,0:T(8,128)(2,1)S(1)} %edges.7.refs_2_, bf16[32,512]{1,0:T(8,128)(2,1)S(1)} %edges.8.refs_3_, ...), custom_call_target="tpu_custom_call" | custom-call | flops 251658240 | bytes 4194304 | tf_op jit(solution)/shard_map/nodes/pallas_call | solution.py:54
  42.4 1.2 %collective-permute-done.13.refs_8_ = bf16[32,512]{1,0:T(8,128)(2,1)S(1)} collective-permute-done((bf16[32,512]{1,0:T(8,128)(2,1)S(1)}, bf16[32,512]{1,0:T(8,128)(2,1)S(1)}, u32[]{:S(2)}, u32[]{:S(2)}) %collective-permute-start.13) | collective-permute-done | bytes 32800 | tf_op jit(solution)/shard_map/ppermute | solution.py:419
  43.6 2.1 %collective-permute-done.11.refs_5_ = bf16[128,512]{1,0:T(8,128)(2,1)S(1)} collective-permute-done((bf16[128,512]{1,0:T(8,128)(2,1)S(1)}, bf16[128,512]{1,0:T(8,128)(2,1)S(1)}, u32[]{:S(2)}, u32[]{:S(2)}) %collective-permute-start.11) | collective-permute-done | bytes 131104 | tf_op jit(solution)/shard_map/ppermute | solution.py:419
  45.7 2.3 %process.1 = (bf16[32,512]{1,0:T(8,128)(2,1)S(1)}, bf16[32,512]{1,0:T(8,128)(2,1)S(1)}, bf16[512,512]{1,0:T(8,128)(2,1)S(1)}) custom-call(bf16[32,512]{1,0:T(8,128)(2,1)S(1)} %get-tuple-element.74.refs_0_, f32[32,512]{1,0:T(8,128)S(1)} %get-tuple-element.75.refs_1_, bf16[32,512]{1,0:T(8,128)(2,1)S(1)} %get-tuple-element.62.refs_0_.refs_1_.refs_4_.refs_2_, ...), custom_call_target="tpu_custom_call" | custom-call | flops 1073741824 | bytes 6291456 | tf_op jit(solution)/shard_map/process/pallas_call | solution.py:54
  48.1 0.7 %collective-permute-start.14 = (bf16[32,512]{1,0:T(8,128)(2,1)S(1)}, bf16[32,512]{1,0:T(8,128)(2,1)S(1)}, u32[]{:S(2)}, u32[]{:S(2)}) collective-permute-start(bf16[32,512]{1,0:T(8,128)(2,1)S(1)} %get-tuple-element.86.refs_0_.refs_8_), channel_id=1, source_target_pairs={{0,1},{1,0},{2,3},{3,2},{4,5},{5,4},{6,7},{7,6},{8,9},{9,8},{10,11... | collective-permute-start | bytes 98312 | tf_op jit(solution)/shard_map/ppermute | solution.py:419
  48.7 2.4 %edges.10.refs_1_ = bf16[48,512]{1,0:T(8,128)(2,1)S(1)} custom-call(f32[96,512]{1,0:T(8,128)S(1)} %get-tuple-element.88.refs_0_, s32[128,32]{1,0:T(8,128)S(1)} %get-tuple-element.81.refs_9_.refs_1_, bf16[512,512]{1,0:T(8,128)(2,1)S(1)} %get-tuple-element.89.refs_2_, bf16[512,512]{1,0:T(8,128)(2,1)S(1)} %get-tuple-element.82.refs_10_.refs_3_, ...), custom_call_target="tpu_custom_call" | custom-call | flops 1610612736 | bytes 4194304 | tf_op jit(solution)/shard_map/edges/pallas_call | solution.py:54
  51.1 2.0 %collective-permute-done.15.refs_2_ = bf16[32,512]{1,0:T(8,128)(2,1)S(1)} collective-permute-done((bf16[32,512]{1,0:T(8,128)(2,1)S(1)}, bf16[32,512]{1,0:T(8,128)(2,1)S(1)}, u32[]{:S(2)}, u32[]{:S(2)}) %collective-permute-start.15) | collective-permute-done | bytes 32800 | tf_op jit(solution)/shard_map/ppermute | solution.py:419
  53.1 1.5 %collective-permute-start.17 = (bf16[96,512]{1,0:T(8,128)(2,1)S(1)}, bf16[96,512]{1,0:T(8,128)(2,1)S(1)}, u32[]{:S(2)}, u32[]{:S(2)}) collective-permute-start(bf16[96,512]{1,0:T(8,128)(2,1)S(1)} %glue.9.refs_10_), channel_id=1, source_target_pairs={{0,24},{1,25},{2,26},{3,27},{4,28},{5,29},{6,30},{7,31},{8,16},{9,... | collective-permute-start | bytes 294920 | tf_op jit(solution)/shard_map/ppermute | solution.py:419
  55.0 2.4 %edges.11.refs_2_ = bf16[48,512]{1,0:T(8,128)(2,1)S(1)} custom-call(f32[96,512]{1,0:T(8,128)S(1)} %get-tuple-element.88.refs_0_, s32[128,32]{1,0:T(8,128)S(1)} %get-tuple-element.81.refs_9_.refs_1_, bf16[512,512]{1,0:T(8,128)(2,1)S(1)} %get-tuple-element.89.refs_2_, bf16[512,512]{1,0:T(8,128)(2,1)S(1)} %get-tuple-element.82.refs_10_.refs_3_, ...), custom_call_target="tpu_custom_call" | custom-call | flops 1610612736 | bytes 4194304 | tf_op jit(solution)/shard_map/edges/pallas_call | solution.py:54
  57.4 1.3 %nodes.3 = (bf16[128,512]{1,0:T(8,128)(2,1)}, bf16[96,512]{1,0:T(8,128)(2,1)S(1)}) custom-call(bf16[96,512]{1,0:T(8,128)(2,1)S(1)} %get-tuple-element.87.refs_0_, bf16[48,512]{1,0:T(8,128)(2,1)S(1)} %edges.10.refs_1_, bf16[48,512]{1,0:T(8,128)(2,1)S(1)} %edges.11.refs_2_, bf16[2,512,512]{2,1,0:T(8,128)(2,1)S(1)} %get-tuple-element.83.refs_12_.refs_3_, ...), custom_call_target="tpu_custom_call" | custom-call | flops 251658240 | bytes 4194304 | tf_op jit(solution)/shard_map/nodes/pallas_call | solution.py:54
  59.2 4.1 %decode.1 = bf16[512,512]{1,0:T(8,128)(2,1)} custom-call(bf16[512,512]{1,0:T(8,128)(2,1)S(1)} %get-tuple-element.66.grid.refs_0_, s32[512,8]{1,0:T(8,128)S(1)} %get-tuple-element.67.refs_1_, f32[512,512]{1,0:T(8,128)S(1)} %get-tuple-element.70.refs_2_, bf16[512,512]{1,0:T(8,128)(2,1)S(1)} %get-tuple-element.71.refs_3_, f32[2,512]{1,0:T(2,128)S(1)} %copy-done.4, ...), custom_call_target="tpu_custom_call" | custom-call | flops 1409286144 | bytes 6291456 | tf_op jit(solution)/shard_map/decode/pallas_call | solution.py:54
  (36 shorter events, 2.4 us)
Async XLA Ops:
  2.1 10.1 %collective-permute-start.2 = (bf16[128,512]{1,0:T(8,128)(2,1)S(1)}, bf16[128,512]{1,0:T(8,128)(2,1)S(1)}, u32[]{:S(2)}, u32[]{:S(2)}) collective-permute-start(bf16[128,512]{1,0:T(8,128)(2,1)S(1)} %project_border.1), channel_id=1, source_target_pairs={{0,7},{1,2},{2,1},{3,4},{4,3},{5,6},{6,5},{7,0},{8,15},{9,10},{10,... | collective-permute-start | bytes 393224 | tf_op jit(solution)/shard_map/ppermute | solution.py:419
  6.7 6.4 %collective-permute-start.1 = (bf16[128,512]{1,0:T(8,128)(2,1)S(1)}, bf16[128,512]{1,0:T(8,128)(2,1)S(1)}, u32[]{:S(2)}, u32[]{:S(2)}) collective-permute-start(bf16[128,512]{1,0:T(8,128)(2,1)S(1)} %project_border.1), channel_id=1, source_target_pairs={{0,24},{1,25},{2,26},{3,27},{4,28},{5,29},{6,30},{7,31},{8,16},{9,... | collective-permute-start | bytes 393224 | tf_op jit(solution)/shard_map/ppermute | solution.py:419
  9.1 5.4 %collective-permute-start = (bf16[128,512]{1,0:T(8,128)(2,1)S(1)}, bf16[128,512]{1,0:T(8,128)(2,1)S(1)}, u32[]{:S(2)}, u32[]{:S(2)}) collective-permute-start(bf16[128,512]{1,0:T(8,128)(2,1)S(1)} %project_border.1), channel_id=1, source_target_pairs={{0,8},{1,9},{2,10},{3,11},{4,12},{5,13},{6,14},{7,15},{8,0},{9,1},... | collective-permute-start | bytes 393224 | tf_op jit(solution)/shard_map/ppermute | solution.py:419
  9.6 7.3 %collective-permute-start.7 = (bf16[128,512]{1,0:T(8,128)(2,1)S(1)}, bf16[128,512]{1,0:T(8,128)(2,1)S(1)}, u32[]{:S(2)}, u32[]{:S(2)}) collective-permute-start(bf16[128,512]{1,0:T(8,128)(2,1)S(1)} %project_border.1), channel_id=1, source_target_pairs={{0,1},{1,0},{2,3},{3,2},{4,5},{5,4},{6,7},{7,6},{8,9},{9,8},{10,11... | collective-permute-start | bytes 393224 | tf_op jit(solution)/shard_map/ppermute | solution.py:419
  14.5 7.1 %collective-permute-start.6 = (bf16[128,512]{1,0:T(8,128)(2,1)S(1)}, bf16[128,512]{1,0:T(8,128)(2,1)S(1)}, u32[]{:S(2)}, u32[]{:S(2)}) collective-permute-start(bf16[128,512]{1,0:T(8,128)(2,1)S(1)} %collective-permute-done.2.refs_2_), channel_id=1, source_target_pairs={{0,24},{1,25},{2,26},{3,27},{4,28},{5,29},{6,30},{7,31},{8,16},{9,... | collective-permute-start | bytes 393224 | tf_op jit(solution)/shard_map/ppermute | solution.py:419
  15.9 5.6 %collective-permute-start.4 = (bf16[128,512]{1,0:T(8,128)(2,1)S(1)}, bf16[128,512]{1,0:T(8,128)(2,1)S(1)}, u32[]{:S(2)}, u32[]{:S(2)}) collective-permute-start(bf16[128,512]{1,0:T(8,128)(2,1)S(1)} %collective-permute-done.2.refs_2_), channel_id=1, source_target_pairs={{0,8},{1,9},{2,10},{3,11},{4,12},{5,13},{6,14},{7,15},{8,0},{9,1},... | collective-permute-start | bytes 393224 | tf_op jit(solution)/shard_map/ppermute | solution.py:419
  16.5 5.1 %collective-permute-start.3 = (bf16[128,512]{1,0:T(8,128)(2,1)S(1)}, bf16[128,512]{1,0:T(8,128)(2,1)S(1)}, u32[]{:S(2)}, u32[]{:S(2)}) collective-permute-start(bf16[128,512]{1,0:T(8,128)(2,1)S(1)} %collective-permute-done.refs_3_), channel_id=1, source_target_pairs={{0,1},{1,0},{2,3},{3,2},{4,5},{5,4},{6,7},{7,6},{8,9},{9,8},{10,11... | collective-permute-start | bytes 393224 | tf_op jit(solution)/shard_map/ppermute | solution.py:419
  16.5 5.1 %collective-permute-start.5 = (bf16[128,512]{1,0:T(8,128)(2,1)S(1)}, bf16[128,512]{1,0:T(8,128)(2,1)S(1)}, u32[]{:S(2)}, u32[]{:S(2)}) collective-permute-start(bf16[128,512]{1,0:T(8,128)(2,1)S(1)} %collective-permute-done.1.refs_4_), channel_id=1, source_target_pairs={{0,1},{1,0},{2,3},{3,2},{4,5},{5,4},{6,7},{7,6},{8,9},{9,8},{10,11... | collective-permute-start | bytes 393224 | tf_op jit(solution)/shard_map/ppermute | solution.py:419
  17.0 4.6 %copy-start = (f32[2,512]{1,0:T(2,128)S(1)}, f32[2,512]{1,0:T(2,128)}, u32[]{:S(2)}) copy-start(f32[2,512]{1,0:T(2,128)} %refs_4_.10) | copy-start | bytes 12292
  17.0 4.6 %copy-start.1 = (f32[2,512]{1,0:T(2,128)S(1)}, f32[2,512]{1,0:T(2,128)}, u32[]{:S(2)}) copy-start(f32[2,512]{1,0:T(2,128)} %refs_7_.2) | copy-start | bytes 12292
  17.0 4.6 %copy-start.2 = (f32[2,512]{1,0:T(2,128)S(1)}, f32[2,512]{1,0:T(2,128)}, u32[]{:S(2)}) copy-start(f32[2,512]{1,0:T(2,128)} %refs_4_.12) | copy-start | bytes 12292
  24.1 1.3 %collective-permute-start.8 = (bf16[32,512]{1,0:T(8,128)(2,1)S(1)}, bf16[32,512]{1,0:T(8,128)(2,1)S(1)}, u32[]{:S(2)}, u32[]{:S(2)}) collective-permute-start(bf16[32,512]{1,0:T(8,128)(2,1)S(1)} %get-tuple-element.62.refs_0_.refs_1_.refs_4_.refs_2_), channel_id=1, source_target_pairs={{0,1},{1,0},{2,3},{3,2},{4,5},{5,4},{6,7},{7,6},{8,9},{9,8},{10,11... | collective-permute-start | bytes 98312 | tf_op jit(solution)/shard_map/ppermute | solution.py:419
  25.4 3.6 %collective-permute-start.9 = (bf16[40,512]{1,0:T(8,128)(2,1)S(1)}, bf16[40,512]{1,0:T(8,128)(2,1)S(1)}, u32[]{:S(2)}, u32[]{:S(2)}) collective-permute-start(bf16[40,512]{1,0:T(8,128)(2,1)S(1)} %glue.5), channel_id=1, source_target_pairs={{0,3},{1,2},{2,1},{3,0},{4,7},{5,6},{6,5},{7,4},{8,11},{9,10},{10,... | collective-permute-start | bytes 122888 | tf_op jit(solution)/shard_map/ppermute | solution.py:419
  29.0 7.0 %collective-permute-start.10 = (bf16[48,512]{1,0:T(8,128)(2,1)S(1)}, bf16[48,512]{1,0:T(8,128)(2,1)S(1)}, u32[]{:S(2)}, u32[]{:S(2)}) collective-permute-start(bf16[48,512]{1,0:T(8,128)(2,1)S(1)} %glue.6), channel_id=1, source_target_pairs={{0,7},{1,6},{2,5},{3,4},{4,3},{5,2},{6,1},{7,0},{8,15},{9,14},{10,... | collective-permute-start | bytes 147464 | tf_op jit(solution)/shard_map/ppermute | solution.py:419
  36.1 7.4 %collective-permute-start.12 = (bf16[128,512]{1,0:T(8,128)(2,1)S(1)}, bf16[128,512]{1,0:T(8,128)(2,1)S(1)}, u32[]{:S(2)}, u32[]{:S(2)}) collective-permute-start(bf16[128,512]{1,0:T(8,128)(2,1)S(1)} %glue.7.refs_4_), channel_id=1, source_target_pairs={{0,24},{1,25},{2,26},{3,27},{4,28},{5,29},{6,30},{7,31},{8,16},{9,... | collective-permute-start | bytes 393224 | tf_op jit(solution)/shard_map/ppermute | solution.py:419
  38.8 6.8 %collective-permute-start.11 = (bf16[128,512]{1,0:T(8,128)(2,1)S(1)}, bf16[128,512]{1,0:T(8,128)(2,1)S(1)}, u32[]{:S(2)}, u32[]{:S(2)}) collective-permute-start(bf16[128,512]{1,0:T(8,128)(2,1)S(1)} %glue.7.refs_4_), channel_id=1, source_target_pairs={{0,8},{1,9},{2,10},{3,11},{4,12},{5,13},{6,14},{7,15},{8,0},{9,1},... | collective-permute-start | bytes 393224 | tf_op jit(solution)/shard_map/ppermute | solution.py:419
  39.4 4.2 %collective-permute-start.13 = (bf16[32,512]{1,0:T(8,128)(2,1)S(1)}, bf16[32,512]{1,0:T(8,128)(2,1)S(1)}, u32[]{:S(2)}, u32[]{:S(2)}) collective-permute-start(bf16[32,512]{1,0:T(8,128)(2,1)S(1)} %glue.8.refs_7_), channel_id=1, source_target_pairs={{0,16},{1,17},{2,18},{3,19},{4,20},{5,21},{6,22},{7,23},{8,24},{9,... | collective-permute-start | bytes 98312 | tf_op jit(solution)/shard_map/ppermute | solution.py:419
  41.5 4.2 %copy-start.3 = (f32[2,512]{1,0:T(2,128)S(1)}, f32[2,512]{1,0:T(2,128)}, u32[]{:S(2)}) copy-start(f32[2,512]{1,0:T(2,128)} %refs_5_.1) | copy-start | bytes 12292
  47.9 5.2 %collective-permute-start.15 = (bf16[32,512]{1,0:T(8,128)(2,1)S(1)}, bf16[32,512]{1,0:T(8,128)(2,1)S(1)}, u32[]{:S(2)}, u32[]{:S(2)}) collective-permute-start(bf16[32,512]{1,0:T(8,128)(2,1)S(1)} %get-tuple-element.86.refs_0_.refs_8_), channel_id=1, source_target_pairs={{0,7},{1,2},{2,1},{3,4},{4,3},{5,6},{6,5},{7,0},{8,15},{9,10},{10,... | collective-permute-start | bytes 98312 | tf_op jit(solution)/shard_map/ppermute | solution.py:419
  48.1 5.0 %collective-permute-start.14 = (bf16[32,512]{1,0:T(8,128)(2,1)S(1)}, bf16[32,512]{1,0:T(8,128)(2,1)S(1)}, u32[]{:S(2)}, u32[]{:S(2)}) collective-permute-start(bf16[32,512]{1,0:T(8,128)(2,1)S(1)} %get-tuple-element.86.refs_0_.refs_8_), channel_id=1, source_target_pairs={{0,1},{1,0},{2,3},{3,2},{4,5},{5,4},{6,7},{7,6},{8,9},{9,8},{10,11... | collective-permute-start | bytes 98312 | tf_op jit(solution)/shard_map/ppermute | solution.py:419
  53.1 5.6 %collective-permute-start.17 = (bf16[96,512]{1,0:T(8,128)(2,1)S(1)}, bf16[96,512]{1,0:T(8,128)(2,1)S(1)}, u32[]{:S(2)}, u32[]{:S(2)}) collective-permute-start(bf16[96,512]{1,0:T(8,128)(2,1)S(1)} %glue.9.refs_10_), channel_id=1, source_target_pairs={{0,24},{1,25},{2,26},{3,27},{4,28},{5,29},{6,30},{7,31},{8,16},{9,... | collective-permute-start | bytes 294920 | tf_op jit(solution)/shard_map/ppermute | solution.py:419
  54.6 4.6 %collective-permute-start.16 = (bf16[96,512]{1,0:T(8,128)(2,1)S(1)}, bf16[96,512]{1,0:T(8,128)(2,1)S(1)}, u32[]{:S(2)}, u32[]{:S(2)}) collective-permute-start(bf16[96,512]{1,0:T(8,128)(2,1)S(1)} %glue.9.refs_10_), channel_id=1, source_target_pairs={{0,8},{1,9},{2,10},{3,11},{4,12},{5,13},{6,14},{7,15},{8,0},{9,1},... | collective-permute-start | bytes 294920 | tf_op jit(solution)/shard_map/ppermute | solution.py:419
  57.4 1.8 %copy-start.4 = (f32[2,512]{1,0:T(2,128)S(1)}, f32[2,512]{1,0:T(2,128)}, u32[]{:S(2)}) copy-start(f32[2,512]{1,0:T(2,128)} %refs_4_.13) | copy-start | bytes 12292
  57.4 1.8 %copy-start.5 = (f32[2,512]{1,0:T(2,128)S(1)}, f32[2,512]{1,0:T(2,128)}, u32[]{:S(2)}) copy-start(f32[2,512]{1,0:T(2,128)} %refs_7_.3) | copy-start | bytes 12292

commit v4 on v3

v4 whole, which is shorter than its diff:
```python
import functools

import jax
import jax.numpy as jnp
from jax import lax
from jax.experimental import pallas as pl
from jax.experimental.pallas import tpu as pltpu
from jax.sharding import PartitionSpec as P

AXES = ("gx", "gy")
CM = 4
EPS = 1e-05
BF = jnp.bfloat16
F32 = jnp.float32
I32 = jnp.int32
SDS = jax.ShapeDtypeStruct


def mm(a, b):
    return jnp.dot(a, b, preferred_element_type=F32)


def half_silu(half):
    return (half + half * jnp.tanh(half)).astype(BF)


def inverse_norm(centred):
    spread = jnp.mean(centred * centred, axis=-1, keepdims=True)
    return lax.rsqrt(spread + EPS)


def centre(w):
    w = w.astype(F32)
    return (w - jnp.mean(w, axis=-1, keepdims=True)).astype(BF)


class Mover:
    def __init__(self, sems):
        self.sems = sems
        self.used = 0

    def start(self, source, target):
        copy = pltpu.make_async_copy(source, target, self.sems.at[self.used])
        self.used += 1
        copy.start()
        return copy


def launch(body, name, ins, outs, scratch, copies, flops, nbytes, far_ins=(), far_outs=(), mib=10):
    near = pl.BlockSpec(memory_space=pltpu.VMEM)
    far = pl.BlockSpec(memory_space=pltpu.HBM)
    sems = [pltpu.SemaphoreType.DMA((copies,))] if copies else []
    ins = [pltpu.with_memory_space_constraint(x, pltpu.HBM) if i in far_ins else x for i, x in enumerate(ins)]
    return pl.pallas_call(
        body,
        out_shape=outs,
        in_specs=[far if i in far_ins else near for i in range(len(ins))],
        out_specs=[far if i in far_outs else near for i in range(len(outs))],
        scratch_shapes=[pltpu.VMEM(s, d) for s, d in scratch] + sems,
        compiler_params=pltpu.CompilerParams(vmem_limit_bytes=mib << 20),
        cost_estimate=pl.CostEstimate(flops=flops, bytes_accessed=nbytes, transcendentals=0),
        name=name,
    )(*ins)


def glue(parts, size_y=0):
    flat = [p for part in parts for p in ([q for _, q in part] if isinstance(part, list) else [part])]
    total = sum((part[0][1] if isinstance(part, list) else part)[2] for part in parts)
    width = flat[0][0].shape[1]

    def body(*refs):
        refs = list(refs)
        out = refs.pop()
        values = []
        for part in parts:
            if isinstance(part, list):
                place = lax.axis_index("gy")
                peer = jnp.where(place & 1 == 1, place + 1, place - 1)
                peer = jnp.where(peer < 0, peer + size_y, jnp.where(peer >= size_y, peer - size_y, peer))
                value = None
                for flip, (_, start, rows) in part:
                    option = refs.pop(0)[pl.ds(start, rows), :].astype(F32)
                    value = option if value is None else jnp.where((place ^ peer) == flip, option, value)
                values.append(value)
            else:
                _, start, rows = part
                values.append(refs.pop(0)[pl.ds(start, rows), :].astype(F32))
        out[...] = jnp.concatenate(values, axis=0).astype(BF)

    return launch(body, "glue", [p[0] for p in flat], [SDS((total, width), BF)], [], 0, 1 << 10, 1 << 18, mib=2)[0]


def border_kernel(x, w, out, x_v, w_v, sems):
    mover = Mover(sems)
    quarter = w_v.shape[0] // 4
    loads = [mover.start(x.at[pl.ds(0, x_v.shape[0])], x_v)]
    for i in range(4):
        part = pl.ds(i * quarter, quarter)
        loads.append(mover.start(w.at[0, part], w_v.at[part]))
    for load in loads:
        load.wait()
    out[...] = (mm(x_v[...], w_v[...]) * 0.5).astype(BF)


def split(value, by):
    if by & (by - 1) == 0:
        return value >> (by.bit_length() - 1), value & (by - 1)
    return value // by, value % by


def locate(ids, rows, border, coarse, sizes, places, early=False):
    size_x, size_y = sizes
    place_x, place_y = places
    owner, offset = split(jnp.maximum(ids, 0), rows)
    owner_x, owner_y = split(owner, size_y)
    step_x = owner_x - place_x
    step_x = jnp.where(step_x < 0, step_x + size_x, step_x)
    step_y = owner_y - place_y
    step_y = jnp.where(step_y < 0, step_y + size_y, step_y)
    ahead_x, ahead_y = (place_x & 1) == 0, (place_y & 1) == 0
    pair_x = jnp.where(ahead_x, 1, size_x - 1)
    pair_y = jnp.where(ahead_y, 1, size_y - 1)
    kind_x = jnp.where(step_x == 0, 0, jnp.where(step_x == pair_x, 1, 2))
    kind_y = jnp.where(step_y == 0, 0, jnp.where(step_y == pair_y, 1, 2))
    near_x = (step_x <= 1) | (step_x == size_x - 1)
    near_y = (step_y <= 1) | (step_y == size_y - 1)
    line = coarse * size_y
    group = 3 * border + line
    tail = rows + 2 * border
    groups = tail + line * (size_x - 2)
    first = jnp.where(kind_x == 0, rows - border, groups + (kind_x - 1) * group)
    found = first + kind_y * border + offset
    if early:
        slot = jnp.where(kind_x == 0, kind_y - 1, jnp.where(kind_y == 0, kind_x + 1, 2 * kind_x + kind_y + 1))
        found = rows + slot * border + offset
    if coarse:
        flip = owner_y ^ place_y
        far = jnp.where(kind_x == 0, tail, first + 3 * border)
        far = jnp.where(near_x, far, tail + (step_x - 1) * line)
        index = jnp.where(flip & 1 == 1, 1 + (flip >> 1), jnp.where(flip == 0, 0, size_y // 2 + (flip >> 1)))
        far = far + index * coarse + offset
        nearby = near_x & near_y & (offset < border)
        found = jnp.where(nearby, found, far)
    found = jnp.where((step_x == 0) & (step_y == 0), offset, found)
    return jnp.where(ids >= 0, found, -1)


def turned(found):
    degree, count = found.shape
    pad = -degree % 8
    if pad:
        found = jnp.concatenate([found, jnp.full((pad, count), -1, I32)], axis=0)
    return found.astype(F32).T.astype(I32)


def prepare_kernel(
    sizes, shapes,
    grid, mesh, eids, ee, en, pe, eb, nb,
    grid_o, mesh_o, own, ebase, eself, eat, ee2, en2, en01, pe01,
    eids_v, w0_v, w1_v, eb_v, nb_v, w2_v, sems,
):
    mover = Mover(sems)
    grid_rows, _, grid_border, _ = shapes
    pairs = (
        (eids, eids_v), (grid, grid_o), (ee.at[0], w0_v), (mesh, mesh_o), (ee.at[1], w1_v), (eb, eb_v),
        (ee.at[2], w2_v.at[0]), (en.at[2], w2_v.at[1]), (nb, nb_v), (en.at[pl.ds(0, 2)], en01), (pe.at[pl.ds(0, 2)], pe01),
    )
    loads = [mover.start(a, b) for a, b in pairs]
    places = (lax.axis_index("gx"), lax.axis_index("gy"))
    loads[0].wait()
    eat[...] = turned(locate(eids_v[...], grid_rows, grid_border, 0, sizes, places, True))
    for load in loads[1:3]:
        load.wait()
    own[...] = (mm(grid_o[...], w0_v[...]) * 0.5).astype(BF)
    for load in loads[3:6]:
        load.wait()
    ebase[...] = (mm(mesh_o[...], w1_v[...]) + eb_v[0:1, :]) * 0.5
    for i, out in enumerate((ee2, en2)):
        loads[6 + i].wait()
        out[...] = centre(w2_v[i])
    for load in loads[8:]:
        load.wait()
    eself[...] = mm(mesh_o[...], en01[0]) + nb_v[0:1, :]


def prepare_mesh_kernel(
    sizes, shapes,
    mids, pe, pn, de,
    mat, pe2, pn2, pn01, de01,
    mids_v, w2_v, sems,
):
    mover = Mover(sems)
    _, mesh_rows, _, mesh_border = shapes
    pairs = (
        (mids, mids_v), (pe.at[2], w2_v.at[0]), (pn.at[2], w2_v.at[1]), (pn.at[pl.ds(0, 2)], pn01), (de.at[pl.ds(0, 2)], de01),
    )
    loads = [mover.start(a, b) for a, b in pairs]
    loads[0].wait()
    places = (lax.axis_index("gx"), lax.axis_index("gy"))
    mat[...] = turned(locate(mids_v[...], mesh_rows, mesh_border, CM, sizes, places))
    for i, out in enumerate((pe2, pn2)):
        loads[1 + i].wait()
        out[...] = centre(w2_v[i])
    for load in loads[3:]:
        load.wait()


def prepare_grid_kernel(
    sizes, shapes,
    dids, de, dn, db, nb, grid, de01,
    dbase, dself, dat, de2, dn2, dn01,
    dids_v, db_v, nb_v, w2_v, sems,
):
    mover = Mover(sems)
    _, mesh_rows, _, mesh_border = shapes
    pairs = (
        (dids, dids_v), (db, db_v), (nb, nb_v), (de.at[2], w2_v.at[0]), (dn.at[2], w2_v.at[1]), (dn.at[pl.ds(0, 2)], dn01),
    )
    loads = [mover.start(a, b) for a, b in pairs]
    loads[0].wait()
    places = (lax.axis_index("gx"), lax.axis_index("gy"))
    dat[...] = turned(locate(dids_v[...], mesh_rows, mesh_border, 0, sizes, places))
    for load in loads[1:3]:
        load.wait()
    dbase[...] = (mm(grid[...], de01[1]) + db_v[0:1, :]) * 0.5
    for i, out in enumerate((de2, dn2)):
        loads[3 + i].wait()
        out[...] = centre(w2_v[i])
    loads[5].wait()
    dself[...] = mm(grid[...], dn01[0]) + nb_v[0:1, :]


def chosen(places, ks, lanes):
    return jnp.concatenate([(places[:, k : k + 1] == lanes).astype(F32).astype(BF) for k in ks], axis=0)


def edge_sum(places, degree, table, base, w2, vectors, slots, lift=0, begun=None):
    rows, width = base.shape
    lanes = lift + lax.broadcasted_iota(I32, (rows, table.shape[0]), 1)
    groups = [range(k, min(k + slots, degree)) for k in range(0, degree, slots)]

    def gather(ks):
        half = mm(chosen(places, ks, lanes), table[...])
        half = half.reshape(len(ks), rows, width)
        if begun is not None:
            ref, start = begun
            half = half + ref[pl.ds(ks[0], len(ks)), pl.ds(start, rows), :].astype(F32)
        return half + base[None]

    total = jnp.zeros((rows, width), F32)
    ahead = gather(groups[0])
    for i, ks in enumerate(groups):
        half = ahead
        if i + 1 < len(groups):
            ahead = gather(groups[i + 1])
        y = mm(half_silu(half.reshape(len(ks) * rows, width)), w2)
        scale = inverse_norm(y).reshape(len(ks), rows, 1)
        y = y.reshape(len(ks), rows, width)
        for j, k in enumerate(ks):
            live = (places[:, k : k + 1] >= 0).astype(F32)
            total = total + y[j] * (scale[j] * live)
    return total * (1.0 + vectors[1:2, :])


def begin(places, pieces, block, slots, latents=(), ew=None, ev=None, nw=None, nv=None):
    count, degree = places.shape
    pieces = ranged(pieces)
    width = pieces[0][0].shape[1]
    table_rows = sum(p[2] for p in pieces)
    groups = [[p[0] for p in pieces], list(latents), [ew, ev, nw, nv] if latents else []]
    outs = [SDS((degree, count, width), BF)] + [SDS((count, width), F32)] * (2 if latents else 0)

    def body(places, *refs):
        (pieces_in, latents, extra), refs = taken(groups, refs)
        out, table = refs[0], refs[-1]
        lay(pieces_in, table, pieces)
        lanes = lax.broadcasted_iota(I32, (block, table_rows), 1)
        for at in range(0, count, block):
            near = places[pl.ds(at, block), :]
            for k in range(0, degree, slots):
                ks = range(k, min(k + slots, degree))
                picked = mm(chosen(near, ks, lanes), table[...]).astype(BF)
                out[pl.ds(k, len(ks)), pl.ds(at, block), :] = picked.reshape(len(ks), block, width)
        if latents:
            ew, ev, nw, nv = extra
            x = rows_of(latents, 0, count)
            refs[1][...] = (mm(x, ew[1]) + ev[0:1, :]) * 0.5
            refs[2][...] = mm(x, nw[0]) + nv[0:1, :]

    return launch(
        body, "begin", [places] + [x for g in groups for x in g], outs, [((table_rows, width), BF)], 0,
        2 * count * degree * table_rows * width, 4 << 20,
    )


def taken(groups, refs):
    refs = list(refs)
    split_refs = []
    for group in groups:
        split_refs.append(refs[: len(group)])
        refs = refs[len(group) :]
    return split_refs, refs


def ranged(pieces):
    return [p if isinstance(p, tuple) else (p, 0, p.shape[0]) for p in pieces]


def lay(refs, table, pieces=None):
    at = 0
    for i, ref in enumerate(refs):
        start, rows = (0, ref.shape[0]) if pieces is None else pieces[i][1:]
        table[pl.ds(at, rows), :] = ref[pl.ds(start, rows), :]
        at += rows


def node_update(x, own, summed, w1, w2, vectors):
    half = (own + mm(summed.astype(BF), w1)) * 0.5
    y = mm(half_silu(half), w2)
    return (x.astype(F32) + y * inverse_norm(y) * (1.0 + vectors[1:2, :])).astype(BF)


def rows_of(refs, at, count):
    picked = []
    start = 0
    for ref in refs:
        low, high = max(at - start, 0), min(at + count - start, ref.shape[0])
        if low < high:
            picked.append(ref[pl.ds(low, high - low), :])
        start += ref.shape[0]
    return picked[0] if len(picked) == 1 else jnp.concatenate(picked, axis=0)


def mesh_stage(x, own, places, count, pieces, base, ew2, ev, nw, nw2, nv, following, slots, name, lift, begun):
    width = x.shape[1]
    degree = places.shape[1]
    table_rows = sum(p.shape[0] for p in pieces)
    part = pl.ds(0, count)

    def body(x, own, places, base, ew2, ev, nw, nw2, nv, follow, begun, *refs):
        *pieces_in, new_o, proj, table = refs
        lay(pieces_in, table)
        summed = edge_sum(places[part, :], degree, table, base[part, :], ew2[...], ev, slots, lift, (begun, 0))
        new = node_update(x[part, :], own[part, :], summed, nw[1], nw2[...], nv)
        new_o[...] = new
        proj[...] = (mm(new, follow[0]) * 0.5).astype(BF)

    flops = count * degree * (2 * width * table_rows + 2 * width * width)
    outs = [SDS((count, width), BF), SDS((count, width), BF), SDS((table_rows, width), BF)]
    ins = [x, own, places, base, ew2, ev, nw, nw2, nv, following, begun] + pieces
    return launch(body, name, ins, outs, [], 0, flops, 6 << 20)


def edge_stage(places, at, count, table, base, ew2, ev, slots, lift, begun):
    width = table.shape[1]
    degree = places.shape[1]
    part = pl.ds(at, count)

    def body(places, table, base, ew2, ev, begun, out):
        summed = edge_sum(places[part, :], degree, table, base[part, :], ew2[...], ev, slots, lift, (begun, at))
        out[...] = summed.astype(BF)

    flops = count * degree * (2 * width * table.shape[0] + 2 * width * width)
    return launch(
        body, "edges", [places, table, base, ew2, ev, begun], [SDS((count, width), BF)], [], 0, flops, 4 << 20
    )[0]


def node_stage(xs, own, at, sums, nw, nw2, nv, following, joined=()):
    width = own.shape[1]
    count = sum(x.shape[0] for x in sums)
    groups = [xs, sums, [own, nw, nw2, nv, following], list(joined)]
    rows_out = count + sum(x.shape[0] for x in joined)
    outs = [SDS((rows_out, width), BF), SDS((count, width), BF)]
    x_at = at if xs[0].shape[0] > count else 0

    def body(*refs):
        (xs, sums, (own, nw, nw2, nv, follow), joined_in), (new_o, proj) = taken(groups, refs)
        new = node_update(
            rows_of(xs, x_at, count), own[pl.ds(at, count), :], rows_of(sums, 0, count), nw[1], nw2[...], nv
        )
        lay(joined_in, new_o)
        new_o[pl.ds(rows_out - count, count), :] = new
        proj[...] = (mm(new, follow[0]) * 0.5).astype(BF)

    return launch(body, "nodes", [x for g in groups for x in g], outs, [], 0, 10 * count * width * width, 4 << 20)


def decode_stage(x, own, places, degree, pieces, base, ew2, ev, nw, nw2, nv, passed, block):
    rows, width = x.shape
    pieces = ranged(pieces)
    table_rows = sum(p[2] for p in pieces)
    ins = [x, own, places, base, ew2, ev, nw, nw2, nv, passed] + [p[0] for p in pieces]
    outs = [SDS((rows, width), BF), SDS(passed.shape, BF)]

    def body(x, own, places, base, ew2, ev, nw, nw2, nv, passed, *refs):
        *pieces_in, out, passed_o, table, sums, new, sems = refs
        mover = Mover(sems)
        tails = [mover.start(passed, passed_o)]
        lay(pieces_in, table, pieces)
        for at in range(0, rows, block):
            part = pl.ds(at, block)
            summed = edge_sum(places[part, :], degree, table, base[part, :], ew2[...], ev, 1)
            sums[part, :] = summed.astype(BF)
        for at in range(0, rows, block):
            part = pl.ds(at, block)
            new[part, :] = node_update(x[part, :], own[part, :], sums[part, :], nw[1], nw2[...], nv)
            tails.append(mover.start(new.at[part], out.at[part]))
        for tail in tails:
            tail.wait()

    flops = rows * degree * (2 * width * table_rows + 2 * width * width)
    scratch = [((table_rows, width), BF), ((rows, width), BF), ((rows, width), BF)]
    return launch(body, "decode", ins, outs, scratch, 1 + rows // block, flops, 6 << 20, far_outs=(0, 1))


def sender(size_x, size_y):
    def send(rows, move):
        pairs = []
        for i in range(size_x):
            for j in range(size_y):
                a, b = move(i, j)
                pairs.append((i * size_y + j, (a % size_x) * size_y + b % size_y))
        return lax.ppermute(rows, AXES, pairs)

    return send


def next_pair(i):
    return i + 1 if i % 2 else i - 1


def per_device(
    grid_latent, mesh_latent, encode_senders, mesh_senders, decode_senders,
    encoder_edges, encoder_edgebias, encoder_nodes, encoder_nodebias,
    process_edges, process_edgebias, process_nodes, process_nodebias,
    decoder_edges, decoder_edgebias, decoder_nodes, decoder_nodebias,
):
    grid_rows, width = grid_latent.shape
    mesh_rows = mesh_latent.shape[0]
    grid_border = grid_rows // 4
    mesh_border = mesh_rows // 4
    size_x = lax.axis_size("gx")
    size_y = lax.axis_size("gy")
    square = 2 * width * width
    send = sender(size_x, size_y)
    pair_x = lambda i, j: (i ^ 1, j)
    next_x = lambda i, j: (next_pair(i), j)
    pair_y = lambda i, j: (i, j ^ 1)
    next_y = lambda i, j: (i, next_pair(j))

    border = launch(
        border_kernel, "project_border", [grid_latent, encoder_edges], [SDS((grid_border, width), BF)],
        [((grid_border, width), BF), ((width, width), BF)], 5, grid_border * square, 1 << 20, far_ins=(0, 1),
    )[0]
    e = send(border, pair_x)
    o = send(border, next_x)
    z = send(border, next_y)
    c = send(border, pair_y)

    degrees = [ids.shape[0] + -ids.shape[0] % 8 for ids in (encode_senders, mesh_senders, decode_senders)]
    square_shape = ((width, width), BF)
    pair_shape = ((2, width, width), BF)
    vectors_shape = ((2, width), F32)
    facts = ((size_x, size_y), (grid_rows, mesh_rows, grid_border, mesh_border))
    outs = [
        ((grid_rows, width), BF), ((mesh_rows, width), BF), ((grid_rows, width), BF), ((mesh_rows, width), F32),
        ((mesh_rows, width), F32), ((mesh_rows, degrees[0]), I32), square_shape, square_shape, pair_shape, pair_shape,
    ]
    grid_latent, mesh_latent, own, base, self_part, encode_at, ee2, en2, en01, pe01 = launch(
        functools.partial(prepare_kernel, *facts), "prepare",
        [
            grid_latent, mesh_latent, encode_senders, encoder_edges, encoder_nodes, process_edges, encoder_edgebias,
            encoder_nodebias,
        ],
        [SDS(s, d) for s, d in outs],
        [(encode_senders.shape, I32), square_shape, square_shape, vectors_shape, vectors_shape, pair_shape],
        11, grid_rows * square, 6 << 20, far_ins=range(8), mib=12,
    )
    outs = [((mesh_rows, degrees[1]), I32), square_shape, square_shape, pair_shape, pair_shape]
    mesh_at, pe2, pn2, pn01, de01 = launch(
        functools.partial(prepare_mesh_kernel, *facts), "prepare_mesh",
        [mesh_senders, process_edges, process_nodes, decoder_edges], [SDS(s, d) for s, d in outs],
        [(mesh_senders.shape, I32), pair_shape], 5, 1 << 20, 4 << 20, far_ins=range(4), mib=8,
    )
    e, o, z, own, mesh_at = lax.optimization_barrier((e, o, z, own, mesh_at))
    ec = send(e, pair_y)
    oc = send(o, pair_y)
    ez = send(z, pair_x)
    oz = send(o, next_y)
    begun = begin(encode_at, [own, c, z, e, o], mesh_border, 8)[0]
    lift = grid_rows + 4 * grid_border
    encoded, border, table = mesh_stage(
        mesh_latent, self_part, encode_at, mesh_border, [ec, ez, oc, oz], base, ee2, encoder_edgebias, en01, en2,
        encoder_nodebias, pe01, 8, "encode", lift, begun,
    )
    cuts = [mesh_rows * k // 8 for k in (2, 4, 5, 8)]
    sums = []

    def advance(arrived):
        at, end = cuts[len(sums)], cuts[len(sums) + 1]
        arrived, ready = lax.optimization_barrier((arrived, base))
        sums.append(
            edge_stage(encode_at, at, end - at, table, ready, ee2, encoder_edgebias, max(4, 256 // (end - at)), lift, begun)
        )
        return arrived

    direct = []
    for flip in reversed(range(3, size_y, 2)):
        rows = mesh_border if flip & (flip + 1) == 0 else CM
        sent = border if rows == mesh_border else glue([(border, 0, rows)])
        direct.append((flip, rows, send(sent, lambda i, j, flip=flip: (i, j ^ flip))))
    direct.reverse()
    c = send(border, pair_y)
    c = advance(c)
    heads = [(other, 0, CM) for _, _, other in direct]
    relay = glue(heads)
    relay, sums[0] = lax.optimization_barrier((relay, sums[0]))
    relayed = send(relay, pair_y)
    relay = advance(relay)
    relayed, sums[1] = lax.optimization_barrier((relayed, sums[1]))
    column = [(border, 0, CM), (c, 0, CM)] + heads + [(relayed, 0, CM * len(heads))]
    others = [(flip, (other, 0, mesh_border)) for flip, rows, other in direct if rows == mesh_border]
    stack = glue([(border, 0, mesh_border), (c, 0, mesh_border), others] + column, size_y)
    column = glue(column)
    e = send(stack, pair_x)
    o = send(stack, next_x)
    far = [send(column, lambda i, j, d=d: (i - d, j)) for d in range(2, size_x - 1)]
    while len(sums) < len(cuts) - 1:
        column = advance(column)
    rest, projected = node_stage([mesh_latent], self_part, mesh_border, sums, en01, en2, encoder_nodebias, pe01)
    near = [border, projected, (stack, mesh_border, 2 * mesh_border), column] + far
    begun, base, self_part = begin(
        mesh_at, near, mesh_border, 8, [encoded, rest], pe01, process_edgebias, pn01, process_nodebias
    )
    lift = mesh_rows + 2 * mesh_border + CM * size_y * (size_x - 2)
    first, border, table = mesh_stage(
        encoded, self_part, mesh_at, mesh_border, [e, o], base, pe2, process_edgebias, pn01, pn2, process_nodebias,
        de01, 8, "process", lift, begun,
    )
    c = send(border, pair_y)
    z = send(border, next_y)
    half = (mesh_rows - mesh_border) // 2
    sums = [
        edge_stage(mesh_at, at, half, table, base, pe2, process_edgebias, 4, lift, begun)
        for at in (mesh_border, mesh_border + half)
    ]
    c, z, sums[0] = lax.optimization_barrier((c, z, sums[0]))
    z, senders = lax.optimization_barrier((z, decode_senders))
    outs = [
        ((grid_rows, width), F32), ((grid_rows, width), F32), ((grid_rows, degrees[2]), I32),
        square_shape, square_shape, pair_shape,
    ]
    grid_base, grid_self, decode_at, de2, dn2, dn01 = launch(
        functools.partial(prepare_grid_kernel, *facts), "prepare_grid",
        [senders, decoder_edges, decoder_nodes, decoder_edgebias, decoder_nodebias, grid_latent, de01],
        [SDS(s, d) for s, d in outs],
        [(decode_senders.shape, I32), vectors_shape, vectors_shape, pair_shape],
        6, 2 * grid_rows * square, 4 << 20, far_ins=range(5), mib=10,
    )
    processed, projected = node_stage([rest], self_part, mesh_border, sums, pn01, pn2, process_nodebias, de01, [first])
    stack = glue([(border, 0, mesh_border), (c, 0, mesh_border), (z, 0, mesh_border)])
    e = send(stack, pair_x)
    o = send(stack, next_x)
    decoded, processed = decode_stage(
        grid_latent, grid_self, decode_at, decode_senders.shape[0],
        [border, projected, (stack, mesh_border, 2 * mesh_border), e, o], grid_base, de2, decoder_edgebias, dn01, dn2,
        decoder_nodebias, processed, grid_rows // 2,
    )
    return (decoded, processed)


def solution(mesh):
    rows = P(AXES, None)
    senders = P(None, AXES)
    return jax.shard_map(
        per_device,
        mesh=mesh,
        in_specs=(rows, rows, senders, senders, senders) + (P(),) * 12,
        out_specs=(rows, rows),
        check_vma=False,
    )
```

time: 63.8 us -> 61.3 us (0.961)
  waiting for transfers between devices: 8.81 us -> 3.5 us
  starting transfers between devices: 20.8 us -> 22.7 us
  Pallas kernels: 32.9 us -> 33.6 us
    ppermute x18 -> x20, waiting for transfers between devices: 8.81 us -> 3.5 us  [send(): return lax.ppermute(rows, AXES, pairs)]
    ppermute x18 -> x20, starting transfers between devices: 20.8 us -> 22.7 us  [send(): return lax.ppermute(rows, AXES, pairs)]
    pallas_call x20 -> x21, Pallas kernels: 32.9 us -> 33.6 us  [launch(): pl.pallas_call(body, out_shape=outs, in_specs=[far if i in far_ins else n...]
  transfers between devices with their start and end apart: 18 -> 20, of which waited for: 8 -> 4; matrix products, arithmetic and copies ran while one was open for 0% -> 0% of each run, Pallas kernels for 35% -> 39%
where the time goes in v4:
time: 61.3 us; the launch traced here: 60.9 us
  Pallas kernels  33.6 us (55%)
  starting transfers between devices  22.7 us (37%)
  waiting for transfers between devices  3.5 us (6%)
  between operations  1.06 us (2%)
    pallas_call x21, Pallas kernels, launch(): pl.pallas_call(body, out_shape=outs, in_specs=[far if i in far_ins else n...  33.6 us
    ppermute x20, starting transfers between devices, send(): return lax.ppermute(rows, AXES, pairs)  22.7 us
    ppermute x20, waiting for transfers between devices, send(): return lax.ppermute(rows, AXES, pairs)  3.5 us
  transfers between devices with their start and end apart: 20, of which 4 were waited for; matrix products, arithmetic and copies ran while one was open for 0% of the time, Pallas kernels for 39%

profile of v4, /device:TPU:0, one launch (start us, length us, event | category | flops | bytes accessed | tf_op | source)
XLA Modules:
  0.0 60.9 jit_solution(16195853898651007683)
XLA Ops:
  0.6 1.4 %project_border.1 = bf16[128,512]{1,0:T(8,128)(2,1)S(1)} custom-call(bf16[512,512]{1,0:T(8,128)(2,1)} %x.1, bf16[3,512,512]{2,1,0:T(8,128)(2,1)} %w.1), custom_call_target="tpu_custom_call" | custom-call | flops 67108864 | bytes 1048576 | tf_op jit(solution)/shard_map/project_border/pallas_call | solution.py:54
  2.1 3.0 %collective-permute-start = (bf16[128,512]{1,0:T(8,128)(2,1)S(1)}, bf16[128,512]{1,0:T(8,128)(2,1)S(1)}, u32[]{:S(2)}, u32[]{:S(2)}) collective-permute-start(bf16[128,512]{1,0:T(8,128)(2,1)S(1)} %project_border.1), channel_id=1, source_target_pairs={{0,8},{1,9},{2,10},{3,11},{4,12},{5,13},{6,14},{7,15},{8,0},{9,1},... | collective-permute-start | bytes 393224 | tf_op jit(solution)/shard_map/ppermute | solution.py:424
  5.1 1.5 %collective-permute-start.1 = (bf16[128,512]{1,0:T(8,128)(2,1)S(1)}, bf16[128,512]{1,0:T(8,128)(2,1)S(1)}, u32[]{:S(2)}, u32[]{:S(2)}) collective-permute-start(bf16[128,512]{1,0:T(8,128)(2,1)S(1)} %project_border.1), channel_id=1, source_target_pairs={{0,24},{1,25},{2,26},{3,27},{4,28},{5,29},{6,30},{7,31},{8,16},{9,... | collective-permute-start | bytes 393224 | tf_op jit(solution)/shard_map/ppermute | solution.py:424
  6.6 2.5 %collective-permute-start.2 = (bf16[128,512]{1,0:T(8,128)(2,1)S(1)}, bf16[128,512]{1,0:T(8,128)(2,1)S(1)}, u32[]{:S(2)}, u32[]{:S(2)}) collective-permute-start(bf16[128,512]{1,0:T(8,128)(2,1)S(1)} %project_border.1), channel_id=1, source_target_pairs={{0,7},{1,2},{2,1},{3,4},{4,3},{5,6},{6,5},{7,0},{8,15},{9,10},{10,... | collective-permute-start | bytes 393224 | tf_op jit(solution)/shard_map/ppermute | solution.py:424
  9.1 1.9 %prepare_mesh.1 = (s32[128,32]{1,0:T(8,128)S(1)}, bf16[512,512]{1,0:T(8,128)(2,1)S(1)}, bf16[512,512]{1,0:T(8,128)(2,1)S(1)}, bf16[2,512,512]{2,1,0:T(8,128)(2,1)S(1)}, bf16[2,512,512]{2,1,0:T(8,128)(2,1)S(1)}) custom-call(s32[32,128]{1,0:T(8,128)} %mids.1, bf16[3,512,512]{2,1,0:T(8,128)(2,1)} %pe.3, bf16[3,512,512]{2,1,0:T(8,128)(2,1)} %pn.1, ...), custom_call_target="tpu_custom_call" | custom-call | flops 1048576 | bytes 4194304 | tf_op jit(solution)/shard_map/prepare_mesh/pallas_call | solution.py:54
  11.0 2.8 %prepare.1 = (bf16[512,512]{1,0:T(8,128)(2,1)S(1)}, bf16[128,512]{1,0:T(8,128)(2,1)S(1)}, bf16[512,512]{1,0:T(8,128)(2,1)S(1)}, f32[128,512]{1,0:T(8,128)S(1)}, ...) custom-call(bf16[512,512]{1,0:T(8,128)(2,1)} %x.1, ...), custom_call_target="tpu_custom_call" | custom-call | flops 268435456 | bytes 6291456 | tf_op jit(solution)/shard_map/prepare/pallas_call | solution.py:54
  13.8 0.5 collective-permute-start.6
  14.4 2.0 %collective-permute-start.7 = (bf16[128,512]{1,0:T(8,128)(2,1)S(1)}, bf16[128,512]{1,0:T(8,128)(2,1)S(1)}, u32[]{:S(2)}, u32[]{:S(2)}) collective-permute-start(bf16[128,512]{1,0:T(8,128)(2,1)S(1)} %collective-permute-done.1.refs_4_), channel_id=1, source_target_pairs={{0,7},{1,2},{2,1},{3,4},{4,3},{5,6},{6,5},{7,0},{8,15},{9,10},{10,... | collective-permute-start | bytes 393224 | tf_op jit(solution)/shard_map/ppermute | solution.py:424
  16.3 1.5 %collective-permute-start.5 = (bf16[128,512]{1,0:T(8,128)(2,1)S(1)}, bf16[128,512]{1,0:T(8,128)(2,1)S(1)}, u32[]{:S(2)}, u32[]{:S(2)}) collective-permute-start(bf16[128,512]{1,0:T(8,128)(2,1)S(1)} %collective-permute-done.2.refs_2_), channel_id=1, source_target_pairs={{0,8},{1,9},{2,10},{3,11},{4,12},{5,13},{6,14},{7,15},{8,0},{9,1},... | collective-permute-start | bytes 393224 | tf_op jit(solution)/shard_map/ppermute | solution.py:424
  17.8 4.5 %begin.2.begun = bf16[32,128,512]{2,1,0:T(8,128)(2,1)S(1)} custom-call(s32[128,32]{1,0:T(8,128)S(1)} %get-tuple-element.58.places, bf16[512,512]{1,0:T(8,128)(2,1)S(1)} %get-tuple-element.66.refs_0_, bf16[128,512]{1,0:T(8,128)(2,1)S(1)} %collective-permute-done.3.refs_1_, bf16[128,512]{1,0:T(8,128)(2,1)S(1)} %collective-permute-done.2.refs_2_, ...), custom_call_target="tpu_custom_call" | custom-call | flops 4294967296 | bytes 4194304 | tf_op jit(solution)/shard_map/begin/pallas_call | solution.py:54
  22.5 2.3 %encode.1 = (bf16[32,512]{1,0:T(8,128)(2,1)S(1)}, bf16[32,512]{1,0:T(8,128)(2,1)S(1)}, bf16[512,512]{1,0:T(8,128)(2,1)S(1)}) custom-call(bf16[128,512]{1,0:T(8,128)(2,1)S(1)} %get-tuple-element.56.x.refs_0_, f32[128,512]{1,0:T(8,128)S(1)} %get-tuple-element.57.own.refs_4_, s32[128,32]{1,0:T(8,128)S(1)} %get-tuple-element.58.places, ...), custom_call_target="tpu_custom_call" | custom-call | flops 1073741824 | bytes 6291456 | tf_op jit(solution)/shard_map/encode/pallas_call | solution.py:54
  25.0 1.9 %collective-permute-start.10 = (bf16[32,512]{1,0:T(8,128)(2,1)S(1)}, bf16[32,512]{1,0:T(8,128)(2,1)S(1)}, u32[]{:S(2)}, u32[]{:S(2)}) collective-permute-start(bf16[32,512]{1,0:T(8,128)(2,1)S(1)} %get-tuple-element.72.refs_0_.refs_4_), channel_id=1, source_target_pairs={{0,7},{1,6},{2,5},{3,4},{4,3},{5,2},{6,1},{7,0},{8,15},{9,14},{10,... | collective-permute-start | bytes 98312 | tf_op jit(solution)/shard_map/ppermute | solution.py:424
  26.9 2.1 %collective-permute-start.9 = (bf16[4,512]{1,0:T(4,128)(2,1)S(1)}, bf16[4,512]{1,0:T(4,128)(2,1)S(1)}, u32[]{:S(2)}, u32[]{:S(2)}) collective-permute-start(bf16[4,512]{1,0:T(4,128)(2,1)S(1)} %glue.5), channel_id=1, source_target_pairs={{0,5},{1,4},{2,7},{3,6},{4,1},{5,0},{6,3},{7,2},{8,13},{9,12},{10,... | collective-permute-start | bytes 12296 | tf_op jit(solution)/shard_map/ppermute | solution.py:424
  29.0 1.8 %edges.5.refs_1_ = bf16[32,512]{1,0:T(8,128)(2,1)S(1)} custom-call(s32[128,32]{1,0:T(8,128)S(1)} %get-tuple-element.58.places, bf16[512,512]{1,0:T(8,128)(2,1)S(1)} %get-tuple-element.73.table, f32[128,512]{1,0:T(8,128)S(1)} %get-tuple-element.81.base, bf16[512,512]{1,0:T(8,128)(2,1)S(1)} %get-tuple-element.60.ew2, f32[2,512]{1,0:T(2,128)S(1)} %copy-done, ...), custom_call_target="tpu_custom_call" | custom-call | flops 1073741824 | bytes 4194304 | tf_op jit(solution)/shard_map/edges/pallas_call | solution.py:54
  31.4 1.1 %edges.6.refs_2_ = bf16[16,512]{1,0:T(8,128)(2,1)S(1)} custom-call(s32[128,32]{1,0:T(8,128)S(1)} %get-tuple-element.58.places, bf16[512,512]{1,0:T(8,128)(2,1)S(1)} %get-tuple-element.73.table, f32[128,512]{1,0:T(8,128)S(1)} %get-tuple-element.81.base, bf16[512,512]{1,0:T(8,128)(2,1)S(1)} %get-tuple-element.60.ew2, f32[2,512]{1,0:T(2,128)S(1)} %copy-done, ...), custom_call_target="tpu_custom_call" | custom-call | flops 536870912 | bytes 4194304 | tf_op jit(solution)/shard_map/edges/pallas_call | solution.py:54
  32.5 0.6 collective-permute-start.13
  33.1 0.9 %collective-permute-start.14 = (bf16[128,512]{1,0:T(8,128)(2,1)S(1)}, bf16[128,512]{1,0:T(8,128)(2,1)S(1)}, u32[]{:S(2)}, u32[]{:S(2)}) collective-permute-start(bf16[128,512]{1,0:T(8,128)(2,1)S(1)} %glue.8.refs_2_), channel_id=1, source_target_pairs={{0,8},{1,9},{2,10},{3,11},{4,12},{5,13},{6,14},{7,15},{8,0},{9,1},... | collective-permute-start | bytes 393224 | tf_op jit(solution)/shard_map/ppermute | solution.py:424
  34.1 2.1 %collective-permute-start.15 = (bf16[128,512]{1,0:T(8,128)(2,1)S(1)}, bf16[128,512]{1,0:T(8,128)(2,1)S(1)}, u32[]{:S(2)}, u32[]{:S(2)}) collective-permute-start(bf16[128,512]{1,0:T(8,128)(2,1)S(1)} %glue.8.refs_2_), channel_id=1, source_target_pairs={{0,24},{1,25},{2,26},{3,27},{4,28},{5,29},{6,30},{7,31},{8,16},{9,... | collective-permute-start | bytes 393224 | tf_op jit(solution)/shard_map/ppermute | solution.py:424
  36.2 2.7 %edges.7.refs_3_ = bf16[48,512]{1,0:T(8,128)(2,1)S(1)} custom-call(s32[128,32]{1,0:T(8,128)S(1)} %get-tuple-element.58.places, bf16[512,512]{1,0:T(8,128)(2,1)S(1)} %get-tuple-element.73.table, f32[128,512]{1,0:T(8,128)S(1)} %get-tuple-element.81.base, bf16[512,512]{1,0:T(8,128)(2,1)S(1)} %get-tuple-element.60.ew2, f32[2,512]{1,0:T(2,128)S(1)} %copy-done, ...), custom_call_target="tpu_custom_call" | custom-call | flops 1610612736 | bytes 4194304 | tf_op jit(solution)/shard_map/edges/pallas_call | solution.py:54
  38.9 0.7 %nodes.2 = (bf16[96,512]{1,0:T(8,128)(2,1)S(1)}, bf16[96,512]{1,0:T(8,128)(2,1)S(1)}) custom-call(bf16[128,512]{1,0:T(8,128)(2,1)S(1)} %get-tuple-element.56.x.refs_0_, bf16[32,512]{1,0:T(8,128)(2,1)S(1)} %edges.5.refs_1_, bf16[16,512]{1,0:T(8,128)(2,1)S(1)} %edges.6.refs_2_, bf16[48,512]{1,0:T(8,128)(2,1)S(1)} %edges.7.refs_3_, ...), custom_call_target="tpu_custom_call" | custom-call | flops 251658240 | bytes 4194304 | tf_op jit(solution)/shard_map/nodes/pallas_call | solution.py:54
  39.6 1.5 %begin.3 = (bf16[32,128,512]{2,1,0:T(8,128)(2,1)S(1)}, f32[128,512]{1,0:T(8,128)S(1)}, f32[128,512]{1,0:T(8,128)S(1)}) custom-call(s32[128,32]{1,0:T(8,128)S(1)} %get-tuple-element.71.places, bf16[32,512]{1,0:T(8,128)(2,1)S(1)} %get-tuple-element.72.refs_0_.refs_4_, bf16[96,512]{1,0:T(8,128)(2,1)S(1)} %get-tuple-element.82.refs_1_, ...), custom_call_target="tpu_custom_call" | custom-call | flops 1073741824 | bytes 4194304 | tf_op jit(solution)/shard_map/begin/pallas_call | solution.py:54
  41.1 1.4 %collective-permute-done.15.refs_1_ = bf16[128,512]{1,0:T(8,128)(2,1)S(1)} collective-permute-done((bf16[128,512]{1,0:T(8,128)(2,1)S(1)}, bf16[128,512]{1,0:T(8,128)(2,1)S(1)}, u32[]{:S(2)}, u32[]{:S(2)}) %collective-permute-start.15) | collective-permute-done | bytes 131104 | tf_op jit(solution)/shard_map/ppermute | solution.py:424
  42.5 2.0 %process.1 = (bf16[32,512]{1,0:T(8,128)(2,1)S(1)}, bf16[32,512]{1,0:T(8,128)(2,1)S(1)}, bf16[256,512]{1,0:T(8,128)(2,1)S(1)}) custom-call(bf16[32,512]{1,0:T(8,128)(2,1)S(1)} %get-tuple-element.70.refs_5_.x, f32[128,512]{1,0:T(8,128)S(1)} %get-tuple-element.86.own.refs_3_, s32[128,32]{1,0:T(8,128)S(1)} %get-tuple-element.71.places, ...), custom_call_target="tpu_custom_call" | custom-call | flops 805306368 | bytes 6291456 | tf_op jit(solution)/shard_map/process/pallas_call | solution.py:54
  44.5 1.7 %collective-permute-start.17 = (bf16[32,512]{1,0:T(8,128)(2,1)S(1)}, bf16[32,512]{1,0:T(8,128)(2,1)S(1)}, u32[]{:S(2)}, u32[]{:S(2)}) collective-permute-start(bf16[32,512]{1,0:T(8,128)(2,1)S(1)} %get-tuple-element.92.refs_0_), channel_id=1, source_target_pairs={{0,7},{1,2},{2,1},{3,4},{4,3},{5,6},{6,5},{7,0},{8,15},{9,10},{10,... | collective-permute-start | bytes 98312 | tf_op jit(solution)/shard_map/ppermute | solution.py:424
  46.2 2.1 %edges.8.refs_1_ = bf16[48,512]{1,0:T(8,128)(2,1)S(1)} custom-call(s32[128,32]{1,0:T(8,128)S(1)} %get-tuple-element.71.places, bf16[256,512]{1,0:T(8,128)(2,1)S(1)} %get-tuple-element.93.table, f32[128,512]{1,0:T(8,128)S(1)} %get-tuple-element.87.base, bf16[512,512]{1,0:T(8,128)(2,1)S(1)} %get-tuple-element.88.ew2, f32[2,512]{1,0:T(2,128)S(1)} %copy-done.2, ...), custom_call_target="tpu_custom_call" | custom-call | flops 1207959552 | bytes 4194304 | tf_op jit(solution)/shard_map/edges/pallas_call | solution.py:54
  48.4 1.6 %collective-permute-done.17.refs_2_ = bf16[32,512]{1,0:T(8,128)(2,1)S(1)} collective-permute-done((bf16[32,512]{1,0:T(8,128)(2,1)S(1)}, bf16[32,512]{1,0:T(8,128)(2,1)S(1)}, u32[]{:S(2)}, u32[]{:S(2)}) %collective-permute-start.17) | collective-permute-done | bytes 32800 | tf_op jit(solution)/shard_map/ppermute | solution.py:424
  49.9 0.7 %collective-permute-start.18 = (bf16[96,512]{1,0:T(8,128)(2,1)S(1)}, bf16[96,512]{1,0:T(8,128)(2,1)S(1)}, u32[]{:S(2)}, u32[]{:S(2)}) collective-permute-start(bf16[96,512]{1,0:T(8,128)(2,1)S(1)} %glue.9.refs_2_), channel_id=1, source_target_pairs={{0,8},{1,9},{2,10},{3,11},{4,12},{5,13},{6,14},{7,15},{8,0},{9,1},... | collective-permute-start | bytes 294920 | tf_op jit(solution)/shard_map/ppermute | solution.py:424
  50.7 1.3 %collective-permute-start.19 = (bf16[96,512]{1,0:T(8,128)(2,1)S(1)}, bf16[96,512]{1,0:T(8,128)(2,1)S(1)}, u32[]{:S(2)}, u32[]{:S(2)}) collective-permute-start(bf16[96,512]{1,0:T(8,128)(2,1)S(1)} %glue.9.refs_2_), channel_id=1, source_target_pairs={{0,24},{1,25},{2,26},{3,27},{4,28},{5,29},{6,30},{7,31},{8,16},{9,... | collective-permute-start | bytes 294920 | tf_op jit(solution)/shard_map/ppermute | solution.py:424
  52.0 2.1 %edges.9.refs_2_ = bf16[48,512]{1,0:T(8,128)(2,1)S(1)} custom-call(s32[128,32]{1,0:T(8,128)S(1)} %get-tuple-element.71.places, bf16[256,512]{1,0:T(8,128)(2,1)S(1)} %get-tuple-element.93.table, f32[128,512]{1,0:T(8,128)S(1)} %get-tuple-element.87.base, bf16[512,512]{1,0:T(8,128)(2,1)S(1)} %get-tuple-element.88.ew2, f32[2,512]{1,0:T(2,128)S(1)} %copy-done.2, ...), custom_call_target="tpu_custom_call" | custom-call | flops 1207959552 | bytes 4194304 | tf_op jit(solution)/shard_map/edges/pallas_call | solution.py:54
  54.1 0.7 %nodes.3 = (bf16[128,512]{1,0:T(8,128)(2,1)S(1)}, bf16[96,512]{1,0:T(8,128)(2,1)S(1)}) custom-call(bf16[96,512]{1,0:T(8,128)(2,1)S(1)} %get-tuple-element.84.refs_6_.refs_0_, bf16[48,512]{1,0:T(8,128)(2,1)S(1)} %edges.8.refs_1_, bf16[48,512]{1,0:T(8,128)(2,1)S(1)} %edges.9.refs_2_, f32[128,512]{1,0:T(8,128)S(1)} %get-tuple-element.86.own.refs_3_, ...), custom_call_target="tpu_custom_call" | custom-call | flops 251658240 | bytes 4194304 | tf_op jit(solution)/shard_map/nodes/pallas_call | solution.py:54
  54.8 2.1 %prepare_grid.1 = (f32[512,512]{1,0:T(8,128)S(1)}, f32[512,512]{1,0:T(8,128)S(1)}, s32[512,8]{1,0:T(8,128)S(1)}, bf16[512,512]{1,0:T(8,128)(2,1)S(1)}, bf16[512,...) custom-call(s32[3,512]{1,0:T(4,128)} %dids, bf16[3,512,512]{2,1,0:T(8,128)(2,1)} %de.3, bf16[3,512,512]{2,1,0:T(8,128)(2,1)} %dn.1, ...), custom_call_target="tpu_custom_call" | custom-call | flops 536870912 | bytes 4194304 | tf_op jit(solution)/shard_map/prepare_grid/pallas_call | solution.py:54
  57.0 3.8 %decode.1 = (bf16[512,512]{1,0:T(8,128)(2,1)}, bf16[128,512]{1,0:T(8,128)(2,1)}) custom-call(bf16[512,512]{1,0:T(8,128)(2,1)S(1)} %get-tuple-element.55.grid.x, f32[512,512]{1,0:T(8,128)S(1)} %get-tuple-element.96.own, s32[512,8]{1,0:T(8,128)S(1)} %get-tuple-element.97.places, f32[512,512]{1,0:T(8,128)S(1)} %get-tuple-element.98.base, ...), custom_call_target="tpu_custom_call" | custom-call | flops 1409286144 | bytes 6291456 | tf_op jit(solution)/shard_map/decode/pallas_call | solution.py:54
  (41 shorter events, 1.0 us)
Async XLA Ops:
  2.1 11.7 %collective-permute-start = (bf16[128,512]{1,0:T(8,128)(2,1)S(1)}, bf16[128,512]{1,0:T(8,128)(2,1)S(1)}, u32[]{:S(2)}, u32[]{:S(2)}) collective-permute-start(bf16[128,512]{1,0:T(8,128)(2,1)S(1)} %project_border.1), channel_id=1, source_target_pairs={{0,8},{1,9},{2,10},{3,11},{4,12},{5,13},{6,14},{7,15},{8,0},{9,1},... | collective-permute-start | bytes 393224 | tf_op jit(solution)/shard_map/ppermute | solution.py:424
  5.1 8.7 %collective-permute-start.1 = (bf16[128,512]{1,0:T(8,128)(2,1)S(1)}, bf16[128,512]{1,0:T(8,128)(2,1)S(1)}, u32[]{:S(2)}, u32[]{:S(2)}) collective-permute-start(bf16[128,512]{1,0:T(8,128)(2,1)S(1)} %project_border.1), channel_id=1, source_target_pairs={{0,24},{1,25},{2,26},{3,27},{4,28},{5,29},{6,30},{7,31},{8,16},{9,... | collective-permute-start | bytes 393224 | tf_op jit(solution)/shard_map/ppermute | solution.py:424
  6.6 7.2 %collective-permute-start.2 = (bf16[128,512]{1,0:T(8,128)(2,1)S(1)}, bf16[128,512]{1,0:T(8,128)(2,1)S(1)}, u32[]{:S(2)}, u32[]{:S(2)}) collective-permute-start(bf16[128,512]{1,0:T(8,128)(2,1)S(1)} %project_border.1), channel_id=1, source_target_pairs={{0,7},{1,2},{2,1},{3,4},{4,3},{5,6},{6,5},{7,0},{8,15},{9,10},{10,... | collective-permute-start | bytes 393224 | tf_op jit(solution)/shard_map/ppermute | solution.py:424
  9.1 8.8 %collective-permute-start.3 = (bf16[128,512]{1,0:T(8,128)(2,1)S(1)}, bf16[128,512]{1,0:T(8,128)(2,1)S(1)}, u32[]{:S(2)}, u32[]{:S(2)}) collective-permute-start(bf16[128,512]{1,0:T(8,128)(2,1)S(1)} %project_border.1), channel_id=1, source_target_pairs={{0,1},{1,0},{2,3},{3,2},{4,5},{5,4},{6,7},{7,6},{8,9},{9,8},{10,11... | collective-permute-start | bytes 393224 | tf_op jit(solution)/shard_map/ppermute | solution.py:424
  13.8 8.6 %collective-permute-start.6 = (bf16[128,512]{1,0:T(8,128)(2,1)S(1)}, bf16[128,512]{1,0:T(8,128)(2,1)S(1)}, u32[]{:S(2)}, u32[]{:S(2)}) collective-permute-start(bf16[128,512]{1,0:T(8,128)(2,1)S(1)} %collective-permute-done.1.refs_4_), channel_id=1, source_target_pairs={{0,1},{1,0},{2,3},{3,2},{4,5},{5,4},{6,7},{7,6},{8,9},{9,8},{10,11... | collective-permute-start | bytes 393224 | tf_op jit(solution)/shard_map/ppermute | solution.py:424
  14.4 8.0 %collective-permute-start.7 = (bf16[128,512]{1,0:T(8,128)(2,1)S(1)}, bf16[128,512]{1,0:T(8,128)(2,1)S(1)}, u32[]{:S(2)}, u32[]{:S(2)}) collective-permute-start(bf16[128,512]{1,0:T(8,128)(2,1)S(1)} %collective-permute-done.1.refs_4_), channel_id=1, source_target_pairs={{0,7},{1,2},{2,1},{3,4},{4,3},{5,6},{6,5},{7,0},{8,15},{9,10},{10,... | collective-permute-start | bytes 393224 | tf_op jit(solution)/shard_map/ppermute | solution.py:424
  16.3 6.1 %collective-permute-start.4 = (bf16[128,512]{1,0:T(8,128)(2,1)S(1)}, bf16[128,512]{1,0:T(8,128)(2,1)S(1)}, u32[]{:S(2)}, u32[]{:S(2)}) collective-permute-start(bf16[128,512]{1,0:T(8,128)(2,1)S(1)} %collective-permute-done.refs_3_), channel_id=1, source_target_pairs={{0,1},{1,0},{2,3},{3,2},{4,5},{5,4},{6,7},{7,6},{8,9},{9,8},{10,11... | collective-permute-start | bytes 393224 | tf_op jit(solution)/shard_map/ppermute | solution.py:424
  16.3 6.1 %collective-permute-start.5 = (bf16[128,512]{1,0:T(8,128)(2,1)S(1)}, bf16[128,512]{1,0:T(8,128)(2,1)S(1)}, u32[]{:S(2)}, u32[]{:S(2)}) collective-permute-start(bf16[128,512]{1,0:T(8,128)(2,1)S(1)} %collective-permute-done.2.refs_2_), channel_id=1, source_target_pairs={{0,8},{1,9},{2,10},{3,11},{4,12},{5,13},{6,14},{7,15},{8,0},{9,1},... | collective-permute-start | bytes 393224 | tf_op jit(solution)/shard_map/ppermute | solution.py:424
  17.8 4.6 %copy-start = (f32[2,512]{1,0:T(2,128)S(1)}, f32[2,512]{1,0:T(2,128)}, u32[]{:S(2)}) copy-start(f32[2,512]{1,0:T(2,128)} %ev.11) | copy-start | bytes 12292
  17.8 4.6 %copy-start.1 = (f32[2,512]{1,0:T(2,128)S(1)}, f32[2,512]{1,0:T(2,128)}, u32[]{:S(2)}) copy-start(f32[2,512]{1,0:T(2,128)} %refs_7_.1) | copy-start | bytes 12292
  24.8 4.2 %collective-permute-start.11 = (bf16[32,512]{1,0:T(8,128)(2,1)S(1)}, bf16[32,512]{1,0:T(8,128)(2,1)S(1)}, u32[]{:S(2)}, u32[]{:S(2)}) collective-permute-start(bf16[32,512]{1,0:T(8,128)(2,1)S(1)} %get-tuple-element.72.refs_0_.refs_4_), channel_id=1, source_target_pairs={{0,1},{1,0},{2,3},{3,2},{4,5},{5,4},{6,7},{7,6},{8,9},{9,8},{10,11... | collective-permute-start | bytes 98312 | tf_op jit(solution)/shard_map/ppermute | solution.py:424
  25.0 5.9 %collective-permute-start.10 = (bf16[32,512]{1,0:T(8,128)(2,1)S(1)}, bf16[32,512]{1,0:T(8,128)(2,1)S(1)}, u32[]{:S(2)}, u32[]{:S(2)}) collective-permute-start(bf16[32,512]{1,0:T(8,128)(2,1)S(1)} %get-tuple-element.72.refs_0_.refs_4_), channel_id=1, source_target_pairs={{0,7},{1,6},{2,5},{3,4},{4,3},{5,2},{6,1},{7,0},{8,15},{9,14},{10,... | collective-permute-start | bytes 98312 | tf_op jit(solution)/shard_map/ppermute | solution.py:424
  26.9 4.4 %collective-permute-start.8 = (bf16[32,512]{1,0:T(8,128)(2,1)S(1)}, bf16[32,512]{1,0:T(8,128)(2,1)S(1)}, u32[]{:S(2)}, u32[]{:S(2)}) collective-permute-start(bf16[32,512]{1,0:T(8,128)(2,1)S(1)} %get-tuple-element.72.refs_0_.refs_4_), channel_id=1, source_target_pairs={{0,3},{1,2},{2,1},{3,0},{4,7},{5,6},{6,5},{7,4},{8,11},{9,10},{10,... | collective-permute-start | bytes 98312 | tf_op jit(solution)/shard_map/ppermute | solution.py:424
  26.9 4.0 %collective-permute-start.9 = (bf16[4,512]{1,0:T(4,128)(2,1)S(1)}, bf16[4,512]{1,0:T(4,128)(2,1)S(1)}, u32[]{:S(2)}, u32[]{:S(2)}) collective-permute-start(bf16[4,512]{1,0:T(4,128)(2,1)S(1)} %glue.5), channel_id=1, source_target_pairs={{0,5},{1,4},{2,7},{3,6},{4,1},{5,0},{6,3},{7,2},{8,13},{9,12},{10,... | collective-permute-start | bytes 12296 | tf_op jit(solution)/shard_map/ppermute | solution.py:424
  31.3 1.2 %collective-permute-start.12 = (bf16[12,512]{1,0:T(8,128)(2,1)S(1)}, bf16[12,512]{1,0:T(8,128)(2,1)S(1)}, u32[]{:S(2)}, u32[]{:S(2)}) collective-permute-start(bf16[12,512]{1,0:T(8,128)(2,1)S(1)} %glue.6), channel_id=1, source_target_pairs={{0,1},{1,0},{2,3},{3,2},{4,5},{5,4},{6,7},{7,6},{8,9},{9,8},{10,11... | collective-permute-start | bytes 36872 | tf_op jit(solution)/shard_map/ppermute | solution.py:424
  32.5 7.1 %collective-permute-start.13 = (bf16[32,512]{1,0:T(8,128)(2,1)S(1)}, bf16[32,512]{1,0:T(8,128)(2,1)S(1)}, u32[]{:S(2)}, u32[]{:S(2)}) collective-permute-start(bf16[32,512]{1,0:T(8,128)(2,1)S(1)} %glue.7.refs_3_), channel_id=1, source_target_pairs={{0,16},{1,17},{2,18},{3,19},{4,20},{5,21},{6,22},{7,23},{8,24},{9,... | collective-permute-start | bytes 98312 | tf_op jit(solution)/shard_map/ppermute | solution.py:424
  33.1 8.0 %collective-permute-start.14 = (bf16[128,512]{1,0:T(8,128)(2,1)S(1)}, bf16[128,512]{1,0:T(8,128)(2,1)S(1)}, u32[]{:S(2)}, u32[]{:S(2)}) collective-permute-start(bf16[128,512]{1,0:T(8,128)(2,1)S(1)} %glue.8.refs_2_), channel_id=1, source_target_pairs={{0,8},{1,9},{2,10},{3,11},{4,12},{5,13},{6,14},{7,15},{8,0},{9,1},... | collective-permute-start | bytes 393224 | tf_op jit(solution)/shard_map/ppermute | solution.py:424
  34.1 8.4 %collective-permute-start.15 = (bf16[128,512]{1,0:T(8,128)(2,1)S(1)}, bf16[128,512]{1,0:T(8,128)(2,1)S(1)}, u32[]{:S(2)}, u32[]{:S(2)}) collective-permute-start(bf16[128,512]{1,0:T(8,128)(2,1)S(1)} %glue.8.refs_2_), channel_id=1, source_target_pairs={{0,24},{1,25},{2,26},{3,27},{4,28},{5,29},{6,30},{7,31},{8,16},{9,... | collective-permute-start | bytes 393224 | tf_op jit(solution)/shard_map/ppermute | solution.py:424
  38.9 0.7 %copy-start.2 = (f32[2,512]{1,0:T(2,128)S(1)}, f32[2,512]{1,0:T(2,128)}, u32[]{:S(2)}) copy-start(f32[2,512]{1,0:T(2,128)} %ev.14) | copy-start | bytes 12292
  38.9 0.7 %copy-start.3 = (f32[2,512]{1,0:T(2,128)S(1)}, f32[2,512]{1,0:T(2,128)}, u32[]{:S(2)}) copy-start(f32[2,512]{1,0:T(2,128)} %refs_6_.1) | copy-start | bytes 12292
  44.5 3.9 %collective-permute-start.16 = (bf16[32,512]{1,0:T(8,128)(2,1)S(1)}, bf16[32,512]{1,0:T(8,128)(2,1)S(1)}, u32[]{:S(2)}, u32[]{:S(2)}) collective-permute-start(bf16[32,512]{1,0:T(8,128)(2,1)S(1)} %get-tuple-element.92.refs_0_), channel_id=1, source_target_pairs={{0,1},{1,0},{2,3},{3,2},{4,5},{5,4},{6,7},{7,6},{8,9},{9,8},{10,11... | collective-permute-start | bytes 98312 | tf_op jit(solution)/shard_map/ppermute | solution.py:424
  44.5 5.4 %collective-permute-start.17 = (bf16[32,512]{1,0:T(8,128)(2,1)S(1)}, bf16[32,512]{1,0:T(8,128)(2,1)S(1)}, u32[]{:S(2)}, u32[]{:S(2)}) collective-permute-start(bf16[32,512]{1,0:T(8,128)(2,1)S(1)} %get-tuple-element.92.refs_0_), channel_id=1, source_target_pairs={{0,7},{1,2},{2,1},{3,4},{4,3},{5,6},{6,5},{7,0},{8,15},{9,10},{10,... | collective-permute-start | bytes 98312 | tf_op jit(solution)/shard_map/ppermute | solution.py:424
  49.9 7.0 %collective-permute-start.18 = (bf16[96,512]{1,0:T(8,128)(2,1)S(1)}, bf16[96,512]{1,0:T(8,128)(2,1)S(1)}, u32[]{:S(2)}, u32[]{:S(2)}) collective-permute-start(bf16[96,512]{1,0:T(8,128)(2,1)S(1)} %glue.9.refs_2_), channel_id=1, source_target_pairs={{0,8},{1,9},{2,10},{3,11},{4,12},{5,13},{6,14},{7,15},{8,0},{9,1},... | collective-permute-start | bytes 294920 | tf_op jit(solution)/shard_map/ppermute | solution.py:424
  50.7 6.3 %collective-permute-start.19 = (bf16[96,512]{1,0:T(8,128)(2,1)S(1)}, bf16[96,512]{1,0:T(8,128)(2,1)S(1)}, u32[]{:S(2)}, u32[]{:S(2)}) collective-permute-start(bf16[96,512]{1,0:T(8,128)(2,1)S(1)} %glue.9.refs_2_), channel_id=1, source_target_pairs={{0,24},{1,25},{2,26},{3,27},{4,28},{5,29},{6,30},{7,31},{8,16},{9,... | collective-permute-start | bytes 294920 | tf_op jit(solution)/shard_map/ppermute | solution.py:424
  54.8 2.2 %copy-start.4 = (f32[2,512]{1,0:T(2,128)S(1)}, f32[2,512]{1,0:T(2,128)}, u32[]{:S(2)}) copy-start(f32[2,512]{1,0:T(2,128)} %ev.15) | copy-start | bytes 12292
  54.8 2.2 %copy-start.5 = (f32[2,512]{1,0:T(2,128)S(1)}, f32[2,512]{1,0:T(2,128)}, u32[]{:S(2)}) copy-start(f32[2,512]{1,0:T(2,128)} %nv.5) | copy-start | bytes 12292

commit v5 on v4

--- a/solution.py
+++ b/solution.py
@@ -22,6 +22,11 @@
 
 def half_silu(half):
     return (half + half * jnp.tanh(half)).astype(BF)
+
+
+def half_silu_edges(half):
+    half = half.astype(BF)
+    return half + half * jnp.tanh(half)
 
 
 def inverse_norm(centred):
@@ -155,79 +160,45 @@
 
 def prepare_kernel(
     sizes, shapes,
-    grid, mesh, eids, ee, en, pe, eb, nb,
-    grid_o, mesh_o, own, ebase, eself, eat, ee2, en2, en01, pe01,
-    eids_v, w0_v, w1_v, eb_v, nb_v, w2_v, sems,
+    grid, mesh, eids, mids, ee, en, pe, pn, de, dn, eb, nb,
+    grid_o, mesh_o, own, ebase, eself, eat, mat, ee2, en2, pe2, pn2, de2, dn2, en01, pe01, pn01, de01, dn01,
+    eids_v, mids_v, w0_v, w1_v, eb_v, nb_v, w2_v, sems,
 ):
     mover = Mover(sems)
-    grid_rows, _, grid_border, _ = shapes
+    grid_rows, mesh_rows, grid_border, mesh_border = shapes
     pairs = (
-        (eids, eids_v), (grid, grid_o), (ee.at[0], w0_v), (mesh, mesh_o), (ee.at[1], w1_v), (eb, eb_v),
-        (ee.at[2], w2_v.at[0]), (en.at[2], w2_v.at[1]), (nb, nb_v), (en.at[pl.ds(0, 2)], en01), (pe.at[pl.ds(0, 2)], pe01),
+        (eids, eids_v), (mids, mids_v), (grid, grid_o), (ee.at[0], w0_v), (mesh, mesh_o), (ee.at[1], w1_v), (eb, eb_v),
+        (ee.at[2], w2_v.at[0]), (en.at[2], w2_v.at[1]), (nb, nb_v), (pe.at[2], w2_v.at[2]), (pn.at[2], w2_v.at[3]), (de.at[2], w2_v.at[4]), (dn.at[2], w2_v.at[5]),
+        (en.at[pl.ds(0, 2)], en01), (pe.at[pl.ds(0, 2)], pe01), (pn.at[pl.ds(0, 2)], pn01), (de.at[pl.ds(0, 2)], de01), (dn.at[pl.ds(0, 2)], dn01),
     )
     loads = [mover.start(a, b) for a, b in pairs]
     places = (lax.axis_index("gx"), lax.axis_index("gy"))
     loads[0].wait()
     eat[...] = turned(locate(eids_v[...], grid_rows, grid_border, 0, sizes, places, True))
-    for load in loads[1:3]:
+    loads[1].wait()
+    mat[...] = turned(locate(mids_v[...], mesh_rows, mesh_border, CM, sizes, places))
+    for load in loads[2:4]:
         load.wait()
     own[...] = (mm(grid_o[...], w0_v[...]) * 0.5).astype(BF)
-    for load in loads[3:6]:
+    for load in loads[4:7]:
         load.wait()
     ebase[...] = (mm(mesh_o[...], w1_v[...]) + eb_v[0:1, :]) * 0.5
-    for i, out in enumerate((ee2, en2)):
-        loads[6 + i].wait()
+    loads[9].wait()
+    for i, out in enumerate((ee2, en2, pe2, pn2, de2, dn2)):
+        loads[7 + i + (i > 1)].wait()
         out[...] = centre(w2_v[i])
-    for load in loads[8:]:
+    loads[14].wait()
+    eself[...] = mm(mesh_o[...], en01[0]) + nb_v[0:1, :]
+    for load in loads[15:]:
         load.wait()
-    eself[...] = mm(mesh_o[...], en01[0]) + nb_v[0:1, :]
-
-
-def prepare_mesh_kernel(
-    sizes, shapes,
-    mids, pe, pn, de,
-    mat, pe2, pn2, pn01, de01,
-    mids_v, w2_v, sems,
-):
-    mover = Mover(sems)
+
+
+def prepare_grid_kernel(sizes, shapes, dids, db, nb, grid, de01, dn01, dbase, dself, dat):
     _, mesh_rows, _, mesh_border = shapes
-    pairs = (
-        (mids, mids_v), (pe.at[2], w2_v.at[0]), (pn.at[2], w2_v.at[1]), (pn.at[pl.ds(0, 2)], pn01), (de.at[pl.ds(0, 2)], de01),
-    )
-    loads = [mover.start(a, b) for a, b in pairs]
-    loads[0].wait()
     places = (lax.axis_index("gx"), lax.axis_index("gy"))
-    mat[...] = turned(locate(mids_v[...], mesh_rows, mesh_border, CM, sizes, places))
-    for i, out in enumerate((pe2, pn2)):
-        loads[1 + i].wait()
-        out[...] = centre(w2_v[i])
-    for load in loads[3:]:
-        load.wait()
-
-
-def prepare_grid_kernel(
-    sizes, shapes,
-    dids, de, dn, db, nb, grid, de01,
-    dbase, dself, dat, de2, dn2, dn01,
-    dids_v, db_v, nb_v, w2_v, sems,
-):
-    mover = Mover(sems)
-    _, mesh_rows, _, mesh_border = shapes
-    pairs = (
-        (dids, dids_v), (db, db_v), (nb, nb_v), (de.at[2], w2_v.at[0]), (dn.at[2], w2_v.at[1]), (dn.at[pl.ds(0, 2)], dn01),
-    )
-    loads = [mover.start(a, b) for a, b in pairs]
-    loads[0].wait()
-    places = (lax.axis_index("gx"), lax.axis_index("gy"))
-    dat[...] = turned(locate(dids_v[...], mesh_rows, mesh_border, 0, sizes, places))
-    for load in loads[1:3]:
-        load.wait()
-    dbase[...] = (mm(grid[...], de01[1]) + db_v[0:1, :]) * 0.5
-    for i, out in enumerate((de2, dn2)):
-        loads[3 + i].wait()
-        out[...] = centre(w2_v[i])
-    loads[5].wait()
-    dself[...] = mm(grid[...], dn01[0]) + nb_v[0:1, :]
+    dat[...] = turned(locate(dids[...], mesh_rows, mesh_border, 0, sizes, places))
+    dbase[...] = (mm(grid[...], de01[1]) + db[0:1, :]) * 0.5
+    dself[...] = mm(grid[...], dn01[0]) + nb[0:1, :]
 
 
 def chosen(places, ks, lanes):
@@ -235,17 +206,17 @@
 
 
 def edge_sum(places, degree, table, base, w2, vectors, slots, lift=0, begun=None):
-    rows, width = base.shape
+    rows, width = places.shape[0], table.shape[1]
     lanes = lift + lax.broadcasted_iota(I32, (rows, table.shape[0]), 1)
     groups = [range(k, min(k + slots, degree)) for k in range(0, degree, slots)]
 
     def gather(ks):
         half = mm(chosen(places, ks, lanes), table[...])
         half = half.reshape(len(ks), rows, width)
-        if begun is not None:
-            ref, start = begun
-            half = half + ref[pl.ds(ks[0], len(ks)), pl.ds(start, rows), :].astype(F32)
-        return half + base[None]
+        if begun is None:
+            return half + base[None]
+        ref, start = begun
+        return half + ref[pl.ds(ks[0], len(ks)), pl.ds(start, rows), :].astype(F32)
 
     total = jnp.zeros((rows, width), F32)
     ahead = gather(groups[0])
@@ -253,7 +224,7 @@
         half = ahead
         if i + 1 < len(groups):
             ahead = gather(groups[i + 1])
-        y = mm(half_silu(half.reshape(len(ks) * rows, width)), w2)
+        y = mm(half_silu_edges(half.reshape(len(ks) * rows, width)), w2)
         scale = inverse_norm(y).reshape(len(ks), rows, 1)
         y = y.reshape(len(ks), rows, width)
         for j, k in enumerate(ks):
@@ -262,30 +233,32 @@
     return total * (1.0 + vectors[1:2, :])
 
 
-def begin(places, pieces, block, slots, latents=(), ew=None, ev=None, nw=None, nv=None):
+def begin(places, pieces, block, slots, base=None, latents=(), ew=None, ev=None, nw=None, nv=None):
     count, degree = places.shape
     pieces = ranged(pieces)
     width = pieces[0][0].shape[1]
     table_rows = sum(p[2] for p in pieces)
-    groups = [[p[0] for p in pieces], list(latents), [ew, ev, nw, nv] if latents else []]
-    outs = [SDS((degree, count, width), BF)] + [SDS((count, width), F32)] * (2 if latents else 0)
+    groups = [[p[0] for p in pieces], list(latents), [ew, ev, nw, nv] if latents else [base]]
+    outs = [SDS((degree, count, width), BF)] + [SDS((count, width), F32)] * (1 if latents else 0)
 
     def body(places, *refs):
         (pieces_in, latents, extra), refs = taken(groups, refs)
         out, table = refs[0], refs[-1]
         lay(pieces_in, table, pieces)
+        if latents:
+            ew, ev, nw, nv = extra
+            x = rows_of(latents, 0, count)
+            base = (mm(x, ew[1]) + ev[0:1, :]) * 0.5
+            refs[1][...] = mm(x, nw[0]) + nv[0:1, :]
+        else:
+            base = extra[0][...]
         lanes = lax.broadcasted_iota(I32, (block, table_rows), 1)
         for at in range(0, count, block):
             near = places[pl.ds(at, block), :]
             for k in range(0, degree, slots):
                 ks = range(k, min(k + slots, degree))
-                picked = mm(chosen(near, ks, lanes), table[...]).astype(BF)
-                out[pl.ds(k, len(ks)), pl.ds(at, block), :] = picked.reshape(len(ks), block, width)
-        if latents:
-            ew, ev, nw, nv = extra
-            x = rows_of(latents, 0, count)
-            refs[1][...] = (mm(x, ew[1]) + ev[0:1, :]) * 0.5
-            refs[2][...] = mm(x, nw[0]) + nv[0:1, :]
+                picked = mm(chosen(near, ks, lanes), table[...]).reshape(len(ks), block, width)
+                out[pl.ds(k, len(ks)), pl.ds(at, block), :] = (picked + base[at : at + block][None]).astype(BF)
 
     return launch(
         body, "begin", [places] + [x for g in groups for x in g], outs, [((table_rows, width), BF)], 0,
@@ -331,38 +304,38 @@
     return picked[0] if len(picked) == 1 else jnp.concatenate(picked, axis=0)
 
 
-def mesh_stage(x, own, places, count, pieces, base, ew2, ev, nw, nw2, nv, following, slots, name, lift, begun):
+def mesh_stage(x, own, places, count, pieces, ew2, ev, nw, nw2, nv, following, slots, name, lift, begun):
     width = x.shape[1]
     degree = places.shape[1]
     table_rows = sum(p.shape[0] for p in pieces)
     part = pl.ds(0, count)
 
-    def body(x, own, places, base, ew2, ev, nw, nw2, nv, follow, begun, *refs):
+    def body(x, own, places, ew2, ev, nw, nw2, nv, follow, begun, *refs):
         *pieces_in, new_o, proj, table = refs
         lay(pieces_in, table)
-        summed = edge_sum(places[part, :], degree, table, base[part, :], ew2[...], ev, slots, lift, (begun, 0))
+        summed = edge_sum(places[part, :], degree, table, None, ew2[...], ev, slots, lift, (begun, 0))
         new = node_update(x[part, :], own[part, :], summed, nw[1], nw2[...], nv)
         new_o[...] = new
         proj[...] = (mm(new, follow[0]) * 0.5).astype(BF)
 
     flops = count * degree * (2 * width * table_rows + 2 * width * width)
     outs = [SDS((count, width), BF), SDS((count, width), BF), SDS((table_rows, width), BF)]
-    ins = [x, own, places, base, ew2, ev, nw, nw2, nv, following, begun] + pieces
+    ins = [x, own, places, ew2, ev, nw, nw2, nv, following, begun] + pieces
     return launch(body, name, ins, outs, [], 0, flops, 6 << 20)
 
 
-def edge_stage(places, at, count, table, base, ew2, ev, slots, lift, begun):
+def edge_stage(places, at, count, table, ew2, ev, slots, lift, begun):
     width = table.shape[1]
     degree = places.shape[1]
     part = pl.ds(at, count)
 
-    def body(places, table, base, ew2, ev, begun, out):
-        summed = edge_sum(places[part, :], degree, table, base[part, :], ew2[...], ev, slots, lift, (begun, at))
+    def body(places, table, ew2, ev, begun, out):
+        summed = edge_sum(places[part, :], degree, table, None, ew2[...], ev, slots, lift, (begun, at))
         out[...] = summed.astype(BF)
 
     flops = count * degree * (2 * width * table.shape[0] + 2 * width * width)
     return launch(
-        body, "edges", [places, table, base, ew2, ev, begun], [SDS((count, width), BF)], [], 0, flops, 4 << 20
+        body, "edges", [places, table, ew2, ev, begun], [SDS((count, width), BF)], [], 0, flops, 4 << 20
     )[0]
 
 
@@ -465,33 +438,33 @@
     facts = ((size_x, size_y), (grid_rows, mesh_rows, grid_border, mesh_border))
     outs = [
         ((grid_rows, width), BF), ((mesh_rows, width), BF), ((grid_rows, width), BF), ((mesh_rows, width), F32),
-        ((mesh_rows, width), F32), ((mesh_rows, degrees[0]), I32), square_shape, square_shape, pair_shape, pair_shape,
-    ]
-    grid_latent, mesh_latent, own, base, self_part, encode_at, ee2, en2, en01, pe01 = launch(
+        ((mesh_rows, width), F32), ((mesh_rows, degrees[0]), I32), ((mesh_rows, degrees[1]), I32),
+    ] + [square_shape] * 6 + [pair_shape] * 5
+    (
+        grid_latent, mesh_latent, own, base, self_part, encode_at, mesh_at, ee2, en2, pe2, pn2, de2, dn2, en01, pe01,
+        pn01, de01, dn01,
+    ) = launch(
         functools.partial(prepare_kernel, *facts), "prepare",
         [
-            grid_latent, mesh_latent, encode_senders, encoder_edges, encoder_nodes, process_edges, encoder_edgebias,
-            encoder_nodebias,
+            grid_latent, mesh_latent, encode_senders, mesh_senders, encoder_edges, encoder_nodes, process_edges, process_nodes,
+            decoder_edges, decoder_nodes, encoder_edgebias, encoder_nodebias,
         ],
         [SDS(s, d) for s, d in outs],
-        [(encode_senders.shape, I32), square_shape, square_shape, vectors_shape, vectors_shape, pair_shape],
-        11, grid_rows * square, 6 << 20, far_ins=range(8), mib=12,
-    )
-    outs = [((mesh_rows, degrees[1]), I32), square_shape, square_shape, pair_shape, pair_shape]
-    mesh_at, pe2, pn2, pn01, de01 = launch(
-        functools.partial(prepare_mesh_kernel, *facts), "prepare_mesh",
-        [mesh_senders, process_edges, process_nodes, decoder_edges], [SDS(s, d) for s, d in outs],
-        [(mesh_senders.shape, I32), pair_shape], 5, 1 << 20, 4 << 20, far_ins=range(4), mib=8,
-    )
-    e, o, z, own, mesh_at = lax.optimization_barrier((e, o, z, own, mesh_at))
+        [
+            (encode_senders.shape, I32), (mesh_senders.shape, I32), square_shape, square_shape, vectors_shape, vectors_shape,
+            ((6, width, width), BF),
+        ],
+        19, grid_rows * square, 6 << 20, far_ins=range(12), mib=20,
+    )
+    e, o, z, own = lax.optimization_barrier((e, o, z, own))
     ec = send(e, pair_y)
     oc = send(o, pair_y)
     ez = send(z, pair_x)
     oz = send(o, next_y)
-    begun = begin(encode_at, [own, c, z, e, o], mesh_border, 8)[0]
+    begun = begin(encode_at, [own, c, z, e, o], mesh_border, 8, base)[0]
     lift = grid_rows + 4 * grid_border
     encoded, border, table = mesh_stage(
-        mesh_latent, self_part, encode_at, mesh_border, [ec, ez, oc, oz], base, ee2, encoder_edgebias, en01, en2,
+        mesh_latent, self_part, encode_at, mesh_border, [ec, ez, oc, oz], ee2, encoder_edgebias, en01, en2,
         encoder_nodebias, pe01, 8, "encode", lift, begun,
     )
     cuts = [mesh_rows * k // 8 for k in (2, 4, 5, 8)]
@@ -499,9 +472,9 @@
 
     def advance(arrived):
         at, end = cuts[len(sums)], cuts[len(sums) + 1]
-        arrived, ready = lax.optimization_barrier((arrived, base))
+        arrived, ready = lax.optimization_barrier((arrived, encode_at))
         sums.append(
-            edge_stage(encode_at, at, end - at, table, ready, ee2, encoder_edgebias, max(4, 256 // (end - at)), lift, begun)
+            edge_stage(ready, at, end - at, table, ee2, encoder_edgebias, max(4, 256 // (end - at)), lift, begun)
         )
         return arrived
 
@@ -521,42 +494,37 @@
     relayed, sums[1] = lax.optimization_barrier((relayed, sums[1]))
     column = [(border, 0, CM), (c, 0, CM)] + heads + [(relayed, 0, CM * len(heads))]
     others = [(flip, (other, 0, mesh_border)) for flip, rows, other in direct if rows == mesh_border]
-    stack = glue([(border, 0, mesh_border), (c, 0, mesh_border), others] + column, size_y)
     column = glue(column)
+    stack = glue([(border, 0, mesh_border), (c, 0, mesh_border), others, (column, 0, CM * size_y)], size_y)
+    far = [send(column, lambda i, j, d=d: (i - d, j)) for d in range(2, size_x - 1)]
     e = send(stack, pair_x)
     o = send(stack, next_x)
-    far = [send(column, lambda i, j, d=d: (i - d, j)) for d in range(2, size_x - 1)]
     while len(sums) < len(cuts) - 1:
         column = advance(column)
     rest, projected = node_stage([mesh_latent], self_part, mesh_border, sums, en01, en2, encoder_nodebias, pe01)
     near = [border, projected, (stack, mesh_border, 2 * mesh_border), column] + far
-    begun, base, self_part = begin(
-        mesh_at, near, mesh_border, 8, [encoded, rest], pe01, process_edgebias, pn01, process_nodebias
+    begun, self_part = begin(
+        mesh_at, near, mesh_border, 8, None, [encoded, rest], pe01, process_edgebias, pn01, process_nodebias
     )
     lift = mesh_rows + 2 * mesh_border + CM * size_y * (size_x - 2)
     first, border, table = mesh_stage(
-        encoded, self_part, mesh_at, mesh_border, [e, o], base, pe2, process_edgebias, pn01, pn2, process_nodebias,
+        encoded, self_part, mesh_at, mesh_border, [e, o], pe2, process_edgebias, pn01, pn2, process_nodebias,
         de01, 8, "process", lift, begun,
     )
     c = send(border, pair_y)
     z = send(border, next_y)
     half = (mesh_rows - mesh_border) // 2
     sums = [
-        edge_stage(mesh_at, at, half, table, base, pe2, process_edgebias, 4, lift, begun)
+        edge_stage(mesh_at, at, half, table, pe2, process_edgebias, 4, lift, begun)
         for at in (mesh_border, mesh_border + half)
     ]
     c, z, sums[0] = lax.optimization_barrier((c, z, sums[0]))
     z, senders = lax.optimization_barrier((z, decode_senders))
-    outs = [
-        ((grid_rows, width), F32), ((grid_rows, width), F32), ((grid_rows, degrees[2]), I32),
-        square_shape, square_shape, pair_shape,
-    ]
-    grid_base, grid_self, decode_at, de2, dn2, dn01 = launch(
+    outs = [((grid_rows, width), F32), ((grid_rows, width), F32), ((grid_rows, degrees[2]), I32)]
+    grid_base, grid_self, decode_at = launch(
         functools.partial(prepare_grid_kernel, *facts), "prepare_grid",
-        [senders, decoder_edges, decoder_nodes, decoder_edgebias, decoder_nodebias, grid_latent, de01],
-        [SDS(s, d) for s, d in outs],
-        [(decode_senders.shape, I32), vectors_shape, vectors_shape, pair_shape],
-        6, 2 * grid_rows * square, 4 << 20, far_ins=range(5), mib=10,
+        [senders, decoder_edgebias, decoder_nodebias, grid_latent, de01, dn01],
+        [SDS(s, d) for s, d in outs], [], 0, 2 * grid_rows * square, 4 << 20,
     )
     processed, projected = node_stage([rest], self_part, mesh_border, sums, pn01, pn2, process_nodebias, de01, [first])
     stack = glue([(border, 0, mesh_border), (c, 0, mesh_border), (z, 0, mesh_border)])

time: 61.3 us -> 59.8 us (0.976)
  Pallas kernels: 33.6 us -> 30.2 us
  waiting for transfers between devices: 3.5 us -> 4.76 us
    pallas_call x21 -> x20, Pallas kernels: 33.6 us -> 30.2 us  [launch(): pl.pallas_call(body, out_shape=outs, in_specs=[far if i in far_ins else n...]
    ppermute x20, waiting for transfers between devices: 3.5 us -> 4.76 us  [send(): return lax.ppermute(rows, AXES, pairs)]
  transfers between devices with their start and end apart: 20 -> 20, of which waited for: 4 -> 4; matrix products, arithmetic and copies ran while one was open for 0% -> 0% of each run, Pallas kernels for 39% -> 36%
where the time goes in v5:
time: 59.8 us; the launch traced here: 59.4 us
  Pallas kernels  30.2 us (51%)
  starting transfers between devices  23.3 us (39%)
  waiting for transfers between devices  4.76 us (8%)
  between operations  1.08 us (2%)
    pallas_call x20, Pallas kernels, launch(): pl.pallas_call(body, out_shape=outs, in_specs=[far if i in far_ins else n...  30.2 us
    ppermute x20, starting transfers between devices, send(): return lax.ppermute(rows, AXES, pairs)  23.3 us
    ppermute x20, waiting for transfers between devices, send(): return lax.ppermute(rows, AXES, pairs)  4.76 us
  transfers between devices with their start and end apart: 20, of which 4 were waited for; matrix products, arithmetic and copies ran while one was open for 0% of the time, Pallas kernels for 36%

profile of v5, /device:TPU:0, one launch (start us, length us, event | category | flops | bytes accessed | tf_op | source)
XLA Modules:
  0.0 59.4 jit_solution(15667424477306794976)
XLA Ops:
  0.6 1.4 %project_border.1 = bf16[128,512]{1,0:T(8,128)(2,1)S(1)} custom-call(bf16[512,512]{1,0:T(8,128)(2,1)} %x.1, bf16[3,512,512]{2,1,0:T(8,128)(2,1)} %w.1), custom_call_target="tpu_custom_call" | custom-call | flops 67108864 | bytes 1048576 | tf_op jit(solution)/shard_map/project_border/pallas_call | solution.py:59
  2.1 3.0 %collective-permute-start = (bf16[128,512]{1,0:T(8,128)(2,1)S(1)}, bf16[128,512]{1,0:T(8,128)(2,1)S(1)}, u32[]{:S(2)}, u32[]{:S(2)}) collective-permute-start(bf16[128,512]{1,0:T(8,128)(2,1)S(1)} %project_border.1), channel_id=1, source_target_pairs={{0,8},{1,9},{2,10},{3,11},{4,12},{5,13},{6,14},{7,15},{8,0},{9,1},... | collective-permute-start | bytes 393224 | tf_op jit(solution)/shard_map/ppermute | solution.py:397
  5.1 1.5 %collective-permute-start.1 = (bf16[128,512]{1,0:T(8,128)(2,1)S(1)}, bf16[128,512]{1,0:T(8,128)(2,1)S(1)}, u32[]{:S(2)}, u32[]{:S(2)}) collective-permute-start(bf16[128,512]{1,0:T(8,128)(2,1)S(1)} %project_border.1), channel_id=1, source_target_pairs={{0,24},{1,25},{2,26},{3,27},{4,28},{5,29},{6,30},{7,31},{8,16},{9,... | collective-permute-start | bytes 393224 | tf_op jit(solution)/shard_map/ppermute | solution.py:397
  6.6 2.5 %collective-permute-start.2 = (bf16[128,512]{1,0:T(8,128)(2,1)S(1)}, bf16[128,512]{1,0:T(8,128)(2,1)S(1)}, u32[]{:S(2)}, u32[]{:S(2)}) collective-permute-start(bf16[128,512]{1,0:T(8,128)(2,1)S(1)} %project_border.1), channel_id=1, source_target_pairs={{0,7},{1,2},{2,1},{3,4},{4,3},{5,6},{6,5},{7,0},{8,15},{9,10},{10,... | collective-permute-start | bytes 393224 | tf_op jit(solution)/shard_map/ppermute | solution.py:397
  9.1 4.1 %prepare.1 = (bf16[512,512]{1,0:T(8,128)(2,1)S(1)}, bf16[128,512]{1,0:T(8,128)(2,1)S(1)}, bf16[512,512]{1,0:T(8,128)(2,1)S(1)}, f32[128,512]{1,0:T(8,128)S(1)}, ...) custom-call(bf16[512,512]{1,0:T(8,128)(2,1)} %x.1, ...), custom_call_target="tpu_custom_call" | custom-call | flops 268435456 | bytes 6291456 | tf_op jit(solution)/shard_map/prepare/pallas_call | solution.py:59
  13.2 0.6 %collective-permute-done.2.refs_2_ = bf16[128,512]{1,0:T(8,128)(2,1)S(1)} collective-permute-done((bf16[128,512]{1,0:T(8,128)(2,1)S(1)}, bf16[128,512]{1,0:T(8,128)(2,1)S(1)}, u32[]{:S(2)}, u32[]{:S(2)}) %collective-permute-start.2) | collective-permute-done | bytes 131104 | tf_op jit(solution)/shard_map/ppermute | solution.py:397
  13.8 2.5 %collective-permute-start.7 = (bf16[128,512]{1,0:T(8,128)(2,1)S(1)}, bf16[128,512]{1,0:T(8,128)(2,1)S(1)}, u32[]{:S(2)}, u32[]{:S(2)}) collective-permute-start(bf16[128,512]{1,0:T(8,128)(2,1)S(1)} %collective-permute-done.1.refs_4_), channel_id=1, source_target_pairs={{0,7},{1,2},{2,1},{3,4},{4,3},{5,6},{6,5},{7,0},{8,15},{9,10},{10,... | collective-permute-start | bytes 393224 | tf_op jit(solution)/shard_map/ppermute | solution.py:397
  16.3 1.5 %collective-permute-start.5 = (bf16[128,512]{1,0:T(8,128)(2,1)S(1)}, bf16[128,512]{1,0:T(8,128)(2,1)S(1)}, u32[]{:S(2)}, u32[]{:S(2)}) collective-permute-start(bf16[128,512]{1,0:T(8,128)(2,1)S(1)} %collective-permute-done.2.refs_2_), channel_id=1, source_target_pairs={{0,8},{1,9},{2,10},{3,11},{4,12},{5,13},{6,14},{7,15},{8,0},{9,1},... | collective-permute-start | bytes 393224 | tf_op jit(solution)/shard_map/ppermute | solution.py:397
  17.8 4.5 %begin.2.begun = bf16[32,128,512]{2,1,0:T(8,128)(2,1)S(1)} custom-call(s32[128,32]{1,0:T(8,128)S(1)} %get-tuple-element.78.places, bf16[512,512]{1,0:T(8,128)(2,1)S(1)} %get-tuple-element.62.refs_0_, bf16[128,512]{1,0:T(8,128)(2,1)S(1)} %collective-permute-done.3.refs_1_, bf16[128,512]{1,0:T(8,128)(2,1)S(1)} %collective-permute-done.2.refs_2_, ...), custom_call_target="tpu_custom_call" | custom-call | flops 4294967296 | bytes 4194304 | tf_op jit(solution)/shard_map/begin/pallas_call | solution.py:59
  22.5 2.2 %encode.1 = (bf16[32,512]{1,0:T(8,128)(2,1)S(1)}, bf16[32,512]{1,0:T(8,128)(2,1)S(1)}, bf16[512,512]{1,0:T(8,128)(2,1)S(1)}) custom-call(bf16[128,512]{1,0:T(8,128)(2,1)S(1)} %get-tuple-element.54.x.refs_0_, f32[128,512]{1,0:T(8,128)S(1)} %get-tuple-element.55.own.refs_4_, s32[128,32]{1,0:T(8,128)S(1)} %get-tuple-element.78.places, ...), custom_call_target="tpu_custom_call" | custom-call | flops 1073741824 | bytes 6291456 | tf_op jit(solution)/shard_map/encode/pallas_call | solution.py:59
  24.9 1.3 %collective-permute-start.10 = (bf16[32,512]{1,0:T(8,128)(2,1)S(1)}, bf16[32,512]{1,0:T(8,128)(2,1)S(1)}, u32[]{:S(2)}, u32[]{:S(2)}) collective-permute-start(bf16[32,512]{1,0:T(8,128)(2,1)S(1)} %get-tuple-element.69.refs_0_), channel_id=1, source_target_pairs={{0,7},{1,6},{2,5},{3,4},{4,3},{5,2},{6,1},{7,0},{8,15},{9,14},{10,... | collective-permute-start | bytes 98312 | tf_op jit(solution)/shard_map/ppermute | solution.py:397
  26.2 2.7 %collective-permute-start.9 = (bf16[4,512]{1,0:T(4,128)(2,1)S(1)}, bf16[4,512]{1,0:T(4,128)(2,1)S(1)}, u32[]{:S(2)}, u32[]{:S(2)}) collective-permute-start(bf16[4,512]{1,0:T(4,128)(2,1)S(1)} %glue.5), channel_id=1, source_target_pairs={{0,5},{1,4},{2,7},{3,6},{4,1},{5,0},{6,3},{7,2},{8,13},{9,12},{10,... | collective-permute-start | bytes 12296 | tf_op jit(solution)/shard_map/ppermute | solution.py:397
  28.9 1.6 %edges.5.refs_1_ = bf16[32,512]{1,0:T(8,128)(2,1)S(1)} custom-call(s32[128,32]{1,0:T(8,128)S(1)} %get-tuple-element.78.places, bf16[512,512]{1,0:T(8,128)(2,1)S(1)} %get-tuple-element.71.table, bf16[512,512]{1,0:T(8,128)(2,1)S(1)} %get-tuple-element.57.ew2, f32[2,512]{1,0:T(2,128)S(1)} %copy-done, bf16[32,128,512]{2,1,0:T(8,128)(2,1)S(1)} %begin.2.begun), custom_call_target="tpu_custom_call" | custom-call | flops 1073741824 | bytes 4194304 | tf_op jit(solution)/shard_map/edges/pallas_call | solution.py:59
  30.8 1.0 %edges.6.refs_2_ = bf16[16,512]{1,0:T(8,128)(2,1)S(1)} custom-call(s32[128,32]{1,0:T(8,128)S(1)} %get-tuple-element.78.places, bf16[512,512]{1,0:T(8,128)(2,1)S(1)} %get-tuple-element.71.table, bf16[512,512]{1,0:T(8,128)(2,1)S(1)} %get-tuple-element.57.ew2, f32[2,512]{1,0:T(2,128)S(1)} %copy-done, bf16[32,128,512]{2,1,0:T(8,128)(2,1)S(1)} %begin.2.begun), custom_call_target="tpu_custom_call" | custom-call | flops 536870912 | bytes 4194304 | tf_op jit(solution)/shard_map/edges/pallas_call | solution.py:59
  31.9 0.6 collective-permute-start.13
  32.5 1.3 %collective-permute-start.14 = (bf16[128,512]{1,0:T(8,128)(2,1)S(1)}, bf16[128,512]{1,0:T(8,128)(2,1)S(1)}, u32[]{:S(2)}, u32[]{:S(2)}) collective-permute-start(bf16[128,512]{1,0:T(8,128)(2,1)S(1)} %glue.8.refs_2_), channel_id=1, source_target_pairs={{0,8},{1,9},{2,10},{3,11},{4,12},{5,13},{6,14},{7,15},{8,0},{9,1},... | collective-permute-start | bytes 393224 | tf_op jit(solution)/shard_map/ppermute | solution.py:397
  33.7 1.8 %collective-permute-start.15 = (bf16[128,512]{1,0:T(8,128)(2,1)S(1)}, bf16[128,512]{1,0:T(8,128)(2,1)S(1)}, u32[]{:S(2)}, u32[]{:S(2)}) collective-permute-start(bf16[128,512]{1,0:T(8,128)(2,1)S(1)} %glue.8.refs_2_), channel_id=1, source_target_pairs={{0,24},{1,25},{2,26},{3,27},{4,28},{5,29},{6,30},{7,31},{8,16},{9,... | collective-permute-start | bytes 393224 | tf_op jit(solution)/shard_map/ppermute | solution.py:397
  35.5 2.5 %edges.7.refs_3_ = bf16[48,512]{1,0:T(8,128)(2,1)S(1)} custom-call(s32[128,32]{1,0:T(8,128)S(1)} %get-tuple-element.78.places, bf16[512,512]{1,0:T(8,128)(2,1)S(1)} %get-tuple-element.71.table, bf16[512,512]{1,0:T(8,128)(2,1)S(1)} %get-tuple-element.57.ew2, f32[2,512]{1,0:T(2,128)S(1)} %copy-done, bf16[32,128,512]{2,1,0:T(8,128)(2,1)S(1)} %begin.2.begun), custom_call_target="tpu_custom_call" | custom-call | flops 1610612736 | bytes 4194304 | tf_op jit(solution)/shard_map/edges/pallas_call | solution.py:59
  38.0 0.7 %nodes.2 = (bf16[96,512]{1,0:T(8,128)(2,1)S(1)}, bf16[96,512]{1,0:T(8,128)(2,1)S(1)}) custom-call(bf16[128,512]{1,0:T(8,128)(2,1)S(1)} %get-tuple-element.54.x.refs_0_, bf16[32,512]{1,0:T(8,128)(2,1)S(1)} %edges.5.refs_1_, bf16[16,512]{1,0:T(8,128)(2,1)S(1)} %edges.6.refs_2_, bf16[48,512]{1,0:T(8,128)(2,1)S(1)} %edges.7.refs_3_, ...), custom_call_target="tpu_custom_call" | custom-call | flops 251658240 | bytes 4194304 | tf_op jit(solution)/shard_map/nodes/pallas_call | solution.py:59
  38.7 1.4 %begin.3 = (bf16[32,128,512]{2,1,0:T(8,128)(2,1)S(1)}, f32[128,512]{1,0:T(8,128)S(1)}) custom-call(s32[128,32]{1,0:T(8,128)S(1)} %get-tuple-element.68.places, bf16[32,512]{1,0:T(8,128)(2,1)S(1)} %get-tuple-element.69.refs_0_, bf16[96,512]{1,0:T(8,128)(2,1)S(1)} %get-tuple-element.79.refs_1_, bf16[128,512]{1,0:T(8,128)(2,1)S(1)} %glue.8.refs_2_, ...), custom_call_target="tpu_custom_call" | custom-call | flops 1073741824 | bytes 4194304 | tf_op jit(solution)/shard_map/begin/pallas_call | solution.py:59
  40.2 1.5 %collective-permute-done.15.refs_1_ = bf16[128,512]{1,0:T(8,128)(2,1)S(1)} collective-permute-done((bf16[128,512]{1,0:T(8,128)(2,1)S(1)}, bf16[128,512]{1,0:T(8,128)(2,1)S(1)}, u32[]{:S(2)}, u32[]{:S(2)}) %collective-permute-start.15) | collective-permute-done | bytes 131104 | tf_op jit(solution)/shard_map/ppermute | solution.py:397
  41.7 1.8 %process.1 = (bf16[32,512]{1,0:T(8,128)(2,1)S(1)}, bf16[32,512]{1,0:T(8,128)(2,1)S(1)}, bf16[256,512]{1,0:T(8,128)(2,1)S(1)}) custom-call(bf16[32,512]{1,0:T(8,128)(2,1)S(1)} %get-tuple-element.67.refs_5_.x, f32[128,512]{1,0:T(8,128)S(1)} %get-tuple-element.83.own.refs_3_, s32[128,32]{1,0:T(8,128)S(1)} %get-tuple-element.68.places, ...), custom_call_target="tpu_custom_call" | custom-call | flops 805306368 | bytes 6291456 | tf_op jit(solution)/shard_map/process/pallas_call | solution.py:59
  43.5 2.1 %collective-permute-start.17 = (bf16[32,512]{1,0:T(8,128)(2,1)S(1)}, bf16[32,512]{1,0:T(8,128)(2,1)S(1)}, u32[]{:S(2)}, u32[]{:S(2)}) collective-permute-start(bf16[32,512]{1,0:T(8,128)(2,1)S(1)} %get-tuple-element.88.refs_0_), channel_id=1, source_target_pairs={{0,7},{1,2},{2,1},{3,4},{4,3},{5,6},{6,5},{7,0},{8,15},{9,10},{10,... | collective-permute-start | bytes 98312 | tf_op jit(solution)/shard_map/ppermute | solution.py:397
  45.6 1.9 %edges.8.refs_1_ = bf16[48,512]{1,0:T(8,128)(2,1)S(1)} custom-call(s32[128,32]{1,0:T(8,128)S(1)} %get-tuple-element.68.places, bf16[256,512]{1,0:T(8,128)(2,1)S(1)} %get-tuple-element.89.table, bf16[512,512]{1,0:T(8,128)(2,1)S(1)} %get-tuple-element.84.ew2, f32[2,512]{1,0:T(2,128)S(1)} %copy-done.2, bf16[32,128,512]{2,1,0:T(8,128)(2,1)S(1)} %get-tuple-element.87.begun), custom_call_target="tpu_custom_call" | custom-call | flops 1207959552 | bytes 4194304 | tf_op jit(solution)/shard_map/edges/pallas_call | solution.py:59
  47.6 1.1 %collective-permute-done.17.refs_2_ = bf16[32,512]{1,0:T(8,128)(2,1)S(1)} collective-permute-done((bf16[32,512]{1,0:T(8,128)(2,1)S(1)}, bf16[32,512]{1,0:T(8,128)(2,1)S(1)}, u32[]{:S(2)}, u32[]{:S(2)}) %collective-permute-start.17) | collective-permute-done | bytes 32800 | tf_op jit(solution)/shard_map/ppermute | solution.py:397
  48.7 1.3 %collective-permute-start.18 = (bf16[96,512]{1,0:T(8,128)(2,1)S(1)}, bf16[96,512]{1,0:T(8,128)(2,1)S(1)}, u32[]{:S(2)}, u32[]{:S(2)}) collective-permute-start(bf16[96,512]{1,0:T(8,128)(2,1)S(1)} %glue.9.refs_2_), channel_id=1, source_target_pairs={{0,8},{1,9},{2,10},{3,11},{4,12},{5,13},{6,14},{7,15},{8,0},{9,1},... | collective-permute-start | bytes 294920 | tf_op jit(solution)/shard_map/ppermute | solution.py:397
  50.1 0.7 %collective-permute-start.19 = (bf16[96,512]{1,0:T(8,128)(2,1)S(1)}, bf16[96,512]{1,0:T(8,128)(2,1)S(1)}, u32[]{:S(2)}, u32[]{:S(2)}) collective-permute-start(bf16[96,512]{1,0:T(8,128)(2,1)S(1)} %glue.9.refs_2_), channel_id=1, source_target_pairs={{0,24},{1,25},{2,26},{3,27},{4,28},{5,29},{6,30},{7,31},{8,16},{9,... | collective-permute-start | bytes 294920 | tf_op jit(solution)/shard_map/ppermute | solution.py:397
  50.8 1.9 %edges.9.refs_2_ = bf16[48,512]{1,0:T(8,128)(2,1)S(1)} custom-call(s32[128,32]{1,0:T(8,128)S(1)} %get-tuple-element.68.places, bf16[256,512]{1,0:T(8,128)(2,1)S(1)} %get-tuple-element.89.table, bf16[512,512]{1,0:T(8,128)(2,1)S(1)} %get-tuple-element.84.ew2, f32[2,512]{1,0:T(2,128)S(1)} %copy-done.2, bf16[32,128,512]{2,1,0:T(8,128)(2,1)S(1)} %get-tuple-element.87.begun), custom_call_target="tpu_custom_call" | custom-call | flops 1207959552 | bytes 4194304 | tf_op jit(solution)/shard_map/edges/pallas_call | solution.py:59
  52.8 0.7 %nodes.3 = (bf16[128,512]{1,0:T(8,128)(2,1)S(1)}, bf16[96,512]{1,0:T(8,128)(2,1)S(1)}) custom-call(bf16[96,512]{1,0:T(8,128)(2,1)S(1)} %get-tuple-element.81.refs_6_.refs_0_, bf16[48,512]{1,0:T(8,128)(2,1)S(1)} %edges.8.refs_1_, bf16[48,512]{1,0:T(8,128)(2,1)S(1)} %edges.9.refs_2_, f32[128,512]{1,0:T(8,128)S(1)} %get-tuple-element.83.own.refs_3_, ...), custom_call_target="tpu_custom_call" | custom-call | flops 251658240 | bytes 4194304 | tf_op jit(solution)/shard_map/nodes/pallas_call | solution.py:59
  53.5 0.7 %prepare_grid.1 = (f32[512,512]{1,0:T(8,128)S(1)}, f32[512,512]{1,0:T(8,128)S(1)}, s32[512,8]{1,0:T(8,128)S(1)}) custom-call(s32[3,512]{1,0:T(4,128)S(1)} %copy-done.6, f32[2,512]{1,0:T(2,128)S(1)} %copy-done.4, f32[2,512]{1,0:T(2,128)S(1)} %copy-done.5, bf16[512,512]{1,0:T(8,128)(2,1)S(1)} %get-tuple-element.53.grid.x, ...), custom_call_target="tpu_custom_call" | custom-call | flops 536870912 | bytes 4194304 | tf_op jit(solution)/shard_map/prepare_grid/pallas_call | solution.py:59
  54.2 1.4 %collective-permute-done.19.refs_4_ = bf16[96,512]{1,0:T(8,128)(2,1)S(1)} collective-permute-done((bf16[96,512]{1,0:T(8,128)(2,1)S(1)}, bf16[96,512]{1,0:T(8,128)(2,1)S(1)}, u32[]{:S(2)}, u32[]{:S(2)}) %collective-permute-start.19) | collective-permute-done | bytes 98336 | tf_op jit(solution)/shard_map/ppermute | solution.py:397
  55.6 3.6 %decode.1 = (bf16[512,512]{1,0:T(8,128)(2,1)}, bf16[128,512]{1,0:T(8,128)(2,1)}) custom-call(bf16[512,512]{1,0:T(8,128)(2,1)S(1)} %get-tuple-element.53.grid.x, f32[512,512]{1,0:T(8,128)S(1)} %get-tuple-element.93.own, s32[512,8]{1,0:T(8,128)S(1)} %get-tuple-element.94.places, f32[512,512]{1,0:T(8,128)S(1)} %get-tuple-element.95.base, ...), custom_call_target="tpu_custom_call" | custom-call | flops 1409286144 | bytes 6291456 | tf_op jit(solution)/shard_map/decode/pallas_call | solution.py:59
  (42 shorter events, 0.7 us)
Async XLA Ops:
  2.1 11.1 %collective-permute-start = (bf16[128,512]{1,0:T(8,128)(2,1)S(1)}, bf16[128,512]{1,0:T(8,128)(2,1)S(1)}, u32[]{:S(2)}, u32[]{:S(2)}) collective-permute-start(bf16[128,512]{1,0:T(8,128)(2,1)S(1)} %project_border.1), channel_id=1, source_target_pairs={{0,8},{1,9},{2,10},{3,11},{4,12},{5,13},{6,14},{7,15},{8,0},{9,1},... | collective-permute-start | bytes 393224 | tf_op jit(solution)/shard_map/ppermute | solution.py:397
  5.1 8.1 %collective-permute-start.1 = (bf16[128,512]{1,0:T(8,128)(2,1)S(1)}, bf16[128,512]{1,0:T(8,128)(2,1)S(1)}, u32[]{:S(2)}, u32[]{:S(2)}) collective-permute-start(bf16[128,512]{1,0:T(8,128)(2,1)S(1)} %project_border.1), channel_id=1, source_target_pairs={{0,24},{1,25},{2,26},{3,27},{4,28},{5,29},{6,30},{7,31},{8,16},{9,... | collective-permute-start | bytes 393224 | tf_op jit(solution)/shard_map/ppermute | solution.py:397
  6.6 7.2 %collective-permute-start.2 = (bf16[128,512]{1,0:T(8,128)(2,1)S(1)}, bf16[128,512]{1,0:T(8,128)(2,1)S(1)}, u32[]{:S(2)}, u32[]{:S(2)}) collective-permute-start(bf16[128,512]{1,0:T(8,128)(2,1)S(1)} %project_border.1), channel_id=1, source_target_pairs={{0,7},{1,2},{2,1},{3,4},{4,3},{5,6},{6,5},{7,0},{8,15},{9,10},{10,... | collective-permute-start | bytes 393224 | tf_op jit(solution)/shard_map/ppermute | solution.py:397
  9.1 8.8 %collective-permute-start.3 = (bf16[128,512]{1,0:T(8,128)(2,1)S(1)}, bf16[128,512]{1,0:T(8,128)(2,1)S(1)}, u32[]{:S(2)}, u32[]{:S(2)}) collective-permute-start(bf16[128,512]{1,0:T(8,128)(2,1)S(1)} %project_border.1), channel_id=1, source_target_pairs={{0,1},{1,0},{2,3},{3,2},{4,5},{5,4},{6,7},{7,6},{8,9},{9,8},{10,11... | collective-permute-start | bytes 393224 | tf_op jit(solution)/shard_map/ppermute | solution.py:397
  13.8 8.6 %collective-permute-start.6 = (bf16[128,512]{1,0:T(8,128)(2,1)S(1)}, bf16[128,512]{1,0:T(8,128)(2,1)S(1)}, u32[]{:S(2)}, u32[]{:S(2)}) collective-permute-start(bf16[128,512]{1,0:T(8,128)(2,1)S(1)} %collective-permute-done.1.refs_4_), channel_id=1, source_target_pairs={{0,1},{1,0},{2,3},{3,2},{4,5},{5,4},{6,7},{7,6},{8,9},{9,8},{10,11... | collective-permute-start | bytes 393224 | tf_op jit(solution)/shard_map/ppermute | solution.py:397
  13.8 8.6 %collective-permute-start.7 = (bf16[128,512]{1,0:T(8,128)(2,1)S(1)}, bf16[128,512]{1,0:T(8,128)(2,1)S(1)}, u32[]{:S(2)}, u32[]{:S(2)}) collective-permute-start(bf16[128,512]{1,0:T(8,128)(2,1)S(1)} %collective-permute-done.1.refs_4_), channel_id=1, source_target_pairs={{0,7},{1,2},{2,1},{3,4},{4,3},{5,6},{6,5},{7,0},{8,15},{9,10},{10,... | collective-permute-start | bytes 393224 | tf_op jit(solution)/shard_map/ppermute | solution.py:397
  16.3 6.1 %collective-permute-start.4 = (bf16[128,512]{1,0:T(8,128)(2,1)S(1)}, bf16[128,512]{1,0:T(8,128)(2,1)S(1)}, u32[]{:S(2)}, u32[]{:S(2)}) collective-permute-start(bf16[128,512]{1,0:T(8,128)(2,1)S(1)} %collective-permute-done.refs_3_), channel_id=1, source_target_pairs={{0,1},{1,0},{2,3},{3,2},{4,5},{5,4},{6,7},{7,6},{8,9},{9,8},{10,11... | collective-permute-start | bytes 393224 | tf_op jit(solution)/shard_map/ppermute | solution.py:397
  16.3 6.1 %collective-permute-start.5 = (bf16[128,512]{1,0:T(8,128)(2,1)S(1)}, bf16[128,512]{1,0:T(8,128)(2,1)S(1)}, u32[]{:S(2)}, u32[]{:S(2)}) collective-permute-start(bf16[128,512]{1,0:T(8,128)(2,1)S(1)} %collective-permute-done.2.refs_2_), channel_id=1, source_target_pairs={{0,8},{1,9},{2,10},{3,11},{4,12},{5,13},{6,14},{7,15},{8,0},{9,1},... | collective-permute-start | bytes 393224 | tf_op jit(solution)/shard_map/ppermute | solution.py:397
  17.8 4.6 %copy-start = (f32[2,512]{1,0:T(2,128)S(1)}, f32[2,512]{1,0:T(2,128)}, u32[]{:S(2)}) copy-start(f32[2,512]{1,0:T(2,128)} %ev.11) | copy-start | bytes 12292
  17.8 4.6 %copy-start.1 = (f32[2,512]{1,0:T(2,128)S(1)}, f32[2,512]{1,0:T(2,128)}, u32[]{:S(2)}) copy-start(f32[2,512]{1,0:T(2,128)} %refs_7_.1) | copy-start | bytes 12292
  24.6 4.2 %collective-permute-start.11 = (bf16[32,512]{1,0:T(8,128)(2,1)S(1)}, bf16[32,512]{1,0:T(8,128)(2,1)S(1)}, u32[]{:S(2)}, u32[]{:S(2)}) collective-permute-start(bf16[32,512]{1,0:T(8,128)(2,1)S(1)} %get-tuple-element.69.refs_0_), channel_id=1, source_target_pairs={{0,1},{1,0},{2,3},{3,2},{4,5},{5,4},{6,7},{7,6},{8,9},{9,8},{10,11... | collective-permute-start | bytes 98312 | tf_op jit(solution)/shard_map/ppermute | solution.py:397
  24.9 5.6 %collective-permute-start.10 = (bf16[32,512]{1,0:T(8,128)(2,1)S(1)}, bf16[32,512]{1,0:T(8,128)(2,1)S(1)}, u32[]{:S(2)}, u32[]{:S(2)}) collective-permute-start(bf16[32,512]{1,0:T(8,128)(2,1)S(1)} %get-tuple-element.69.refs_0_), channel_id=1, source_target_pairs={{0,7},{1,6},{2,5},{3,4},{4,3},{5,2},{6,1},{7,0},{8,15},{9,14},{10,... | collective-permute-start | bytes 98312 | tf_op jit(solution)/shard_map/ppermute | solution.py:397
  26.2 4.3 %collective-permute-start.8 = (bf16[32,512]{1,0:T(8,128)(2,1)S(1)}, bf16[32,512]{1,0:T(8,128)(2,1)S(1)}, u32[]{:S(2)}, u32[]{:S(2)}) collective-permute-start(bf16[32,512]{1,0:T(8,128)(2,1)S(1)} %get-tuple-element.69.refs_0_), channel_id=1, source_target_pairs={{0,3},{1,2},{2,1},{3,0},{4,7},{5,6},{6,5},{7,4},{8,11},{9,10},{10,... | collective-permute-start | bytes 98312 | tf_op jit(solution)/shard_map/ppermute | solution.py:397
  26.2 4.3 %collective-permute-start.9 = (bf16[4,512]{1,0:T(4,128)(2,1)S(1)}, bf16[4,512]{1,0:T(4,128)(2,1)S(1)}, u32[]{:S(2)}, u32[]{:S(2)}) collective-permute-start(bf16[4,512]{1,0:T(4,128)(2,1)S(1)} %glue.5), channel_id=1, source_target_pairs={{0,5},{1,4},{2,7},{3,6},{4,1},{5,0},{6,3},{7,2},{8,13},{9,12},{10,... | collective-permute-start | bytes 12296 | tf_op jit(solution)/shard_map/ppermute | solution.py:397
  30.5 1.3 %collective-permute-start.12 = (bf16[12,512]{1,0:T(8,128)(2,1)S(1)}, bf16[12,512]{1,0:T(8,128)(2,1)S(1)}, u32[]{:S(2)}, u32[]{:S(2)}) collective-permute-start(bf16[12,512]{1,0:T(8,128)(2,1)S(1)} %glue.6), channel_id=1, source_target_pairs={{0,1},{1,0},{2,3},{3,2},{4,5},{5,4},{6,7},{7,6},{8,9},{9,8},{10,11... | collective-permute-start | bytes 36872 | tf_op jit(solution)/shard_map/ppermute | solution.py:397
  31.9 6.8 %collective-permute-start.13 = (bf16[32,512]{1,0:T(8,128)(2,1)S(1)}, bf16[32,512]{1,0:T(8,128)(2,1)S(1)}, u32[]{:S(2)}, u32[]{:S(2)}) collective-permute-start(bf16[32,512]{1,0:T(8,128)(2,1)S(1)} %glue.7.refs_4_.refs_3_), channel_id=1, source_target_pairs={{0,16},{1,17},{2,18},{3,19},{4,20},{5,21},{6,22},{7,23},{8,24},{9,... | collective-permute-start | bytes 98312 | tf_op jit(solution)/shard_map/ppermute | solution.py:397
  32.5 7.7 %collective-permute-start.14 = (bf16[128,512]{1,0:T(8,128)(2,1)S(1)}, bf16[128,512]{1,0:T(8,128)(2,1)S(1)}, u32[]{:S(2)}, u32[]{:S(2)}) collective-permute-start(bf16[128,512]{1,0:T(8,128)(2,1)S(1)} %glue.8.refs_2_), channel_id=1, source_target_pairs={{0,8},{1,9},{2,10},{3,11},{4,12},{5,13},{6,14},{7,15},{8,0},{9,1},... | collective-permute-start | bytes 393224 | tf_op jit(solution)/shard_map/ppermute | solution.py:397
  33.7 8.0 %collective-permute-start.15 = (bf16[128,512]{1,0:T(8,128)(2,1)S(1)}, bf16[128,512]{1,0:T(8,128)(2,1)S(1)}, u32[]{:S(2)}, u32[]{:S(2)}) collective-permute-start(bf16[128,512]{1,0:T(8,128)(2,1)S(1)} %glue.8.refs_2_), channel_id=1, source_target_pairs={{0,24},{1,25},{2,26},{3,27},{4,28},{5,29},{6,30},{7,31},{8,16},{9,... | collective-permute-start | bytes 393224 | tf_op jit(solution)/shard_map/ppermute | solution.py:397
  38.0 0.7 %copy-start.2 = (f32[2,512]{1,0:T(2,128)S(1)}, f32[2,512]{1,0:T(2,128)}, u32[]{:S(2)}) copy-start(f32[2,512]{1,0:T(2,128)} %ev.14) | copy-start | bytes 12292
  38.0 0.7 %copy-start.3 = (f32[2,512]{1,0:T(2,128)S(1)}, f32[2,512]{1,0:T(2,128)}, u32[]{:S(2)}) copy-start(f32[2,512]{1,0:T(2,128)} %refs_6_.1) | copy-start | bytes 12292
  43.5 4.1 %collective-permute-start.16 = (bf16[32,512]{1,0:T(8,128)(2,1)S(1)}, bf16[32,512]{1,0:T(8,128)(2,1)S(1)}, u32[]{:S(2)}, u32[]{:S(2)}) collective-permute-start(bf16[32,512]{1,0:T(8,128)(2,1)S(1)} %get-tuple-element.88.refs_0_), channel_id=1, source_target_pairs={{0,1},{1,0},{2,3},{3,2},{4,5},{5,4},{6,7},{7,6},{8,9},{9,8},{10,11... | collective-permute-start | bytes 98312 | tf_op jit(solution)/shard_map/ppermute | solution.py:397
  43.5 5.2 %collective-permute-start.17 = (bf16[32,512]{1,0:T(8,128)(2,1)S(1)}, bf16[32,512]{1,0:T(8,128)(2,1)S(1)}, u32[]{:S(2)}, u32[]{:S(2)}) collective-permute-start(bf16[32,512]{1,0:T(8,128)(2,1)S(1)} %get-tuple-element.88.refs_0_), channel_id=1, source_target_pairs={{0,7},{1,2},{2,1},{3,4},{4,3},{5,6},{6,5},{7,0},{8,15},{9,10},{10,... | collective-permute-start | bytes 98312 | tf_op jit(solution)/shard_map/ppermute | solution.py:397
  48.7 5.4 %collective-permute-start.18 = (bf16[96,512]{1,0:T(8,128)(2,1)S(1)}, bf16[96,512]{1,0:T(8,128)(2,1)S(1)}, u32[]{:S(2)}, u32[]{:S(2)}) collective-permute-start(bf16[96,512]{1,0:T(8,128)(2,1)S(1)} %glue.9.refs_2_), channel_id=1, source_target_pairs={{0,8},{1,9},{2,10},{3,11},{4,12},{5,13},{6,14},{7,15},{8,0},{9,1},... | collective-permute-start | bytes 294920 | tf_op jit(solution)/shard_map/ppermute | solution.py:397
  50.1 5.5 %collective-permute-start.19 = (bf16[96,512]{1,0:T(8,128)(2,1)S(1)}, bf16[96,512]{1,0:T(8,128)(2,1)S(1)}, u32[]{:S(2)}, u32[]{:S(2)}) collective-permute-start(bf16[96,512]{1,0:T(8,128)(2,1)S(1)} %glue.9.refs_2_), channel_id=1, source_target_pairs={{0,24},{1,25},{2,26},{3,27},{4,28},{5,29},{6,30},{7,31},{8,16},{9,... | collective-permute-start | bytes 294920 | tf_op jit(solution)/shard_map/ppermute | solution.py:397
  52.7 0.7 %copy-start.4 = (f32[2,512]{1,0:T(2,128)S(1)}, f32[2,512]{1,0:T(2,128)}, u32[]{:S(2)}) copy-start(f32[2,512]{1,0:T(2,128)} %ev.15) | copy-start | bytes 12292
  52.7 0.7 %copy-start.5 = (f32[2,512]{1,0:T(2,128)S(1)}, f32[2,512]{1,0:T(2,128)}, u32[]{:S(2)}) copy-start(f32[2,512]{1,0:T(2,128)} %nv.5) | copy-start | bytes 12292
  52.8 0.7 %copy-start.6 = (s32[3,512]{1,0:T(4,128)S(1)}, s32[3,512]{1,0:T(4,128)}, u32[]{:S(2)}) copy-start(s32[3,512]{1,0:T(4,128)} %dids) | copy-start | bytes 18436
